TPU v7x, 256 devices: a whole 4x4x8 slice. The times are simulated.
256 devices in a mesh: section: 4 (over y), seq: 64 (over z, x, core).
Axes of the slice: x: 4, y: 4, z: 8, core: 2. Of those that a mesh axis runs over, the one named last changes fastest.
Arguments:
- queries: bfloat16 [4, 8192, 2048], P('section', 'seq'), may hold values from -6 to 6
- key_rows: bfloat16 [4, 8192, 2048], P('section', 'seq'), may hold values from -6 to 6
- value_rows: bfloat16 [4, 8192, 2048], P('section', 'seq'), may hold values from -6 to 6
- grad_out: bfloat16 [4, 8192, 2048], P('section', 'seq'), may hold values from -24 to 24
- log_sums: bfloat16 [4, 16, 8192], P('section', None, 'seq'), may hold values from 4 to 6
- deltas: bfloat16 [4, 16, 8192], P('section', None, 'seq'), may hold values from -96 to 96
- offsets: int32 [64, 16], P('seq'), may hold values from 0 to 7
Outputs:
- grad_query: bfloat16 [4, 8192, 2048], P('section', 'seq')
- grad_key: bfloat16 [4, 8192, 2048], P('section', 'seq')
- grad_value: bfloat16 [4, 8192, 2048], P('section', 'seq')
All inputs are finite; a program needn't handle non-finite values.
Results may differ from a plain program's by a relative error of at most 0.012.
Values may be sent and summed in bfloat16 or wider, within the bound.
No kernel may reach another device: no remote copies, remote signals or barrier semaphores. Data moves between devices by JAX's collectives and lax.ppermute only.
A program may use at most 128 MiB of HBM per device.

v0:
```python
import jax
import jax.numpy as jnp
from jax import lax
from jax.experimental import pallas as pl
from jax.experimental.pallas import tpu as pltpu
from jax.sharding import PartitionSpec as P


HEADS = 16
HD = 128
PICK = 16
RATE = 8
TOK = 128
NZ, NX, NC = 8, 4, 2
QG_ROWS = 40
GROUP = NZ * NC
SCALE = HD ** (-0.5)
BF = jnp.bfloat16
F32 = jnp.float32

VM = pl.BlockSpec(memory_space=pltpu.VMEM)
SM = pl.BlockSpec(memory_space=pltpu.SMEM)


def dot(a, b):
    return lax.dot_general(a, b, (((1,), (0,)), ((), ())), preferred_element_type=F32)


def dot_t(a, b):
    return lax.dot_general(a, b, (((1,), (1,)), ((), ())), preferred_element_type=F32)


def dot_l(a, b):
    return lax.dot_general(a, b, (((0,), (0,)), ((), ())), preferred_element_type=F32)


def pick(x, off):
    t = x.astype(F32).reshape(PICK, RATE, HD)
    row = lax.broadcasted_iota(jnp.int32, (PICK, RATE, HD), 1)
    return jnp.sum(jnp.where(row == off, t, 0.0), axis=1).astype(BF)


def small(mib=12):
    return pltpu.CompilerParams(vmem_limit_bytes=mib << 20)


def pick_grad_kernel(off_ref, g_ref, o_ref):
    for h in range(HEADS):
        o_ref[h] = pick(g_ref[0, :, h * HD:(h + 1) * HD], off_ref[0, h])


def pick_kv_kernel(off_ref, k_ref, v_ref, o_ref):
    for h in range(HEADS):
        cols = slice(h * HD, (h + 1) * HD)
        o_ref[h, 0:16] = pick(k_ref[0, :, cols], off_ref[0, h])
        o_ref[h, 16:32] = pick(v_ref[0, :, cols], off_ref[0, h])


def pick_q_kernel(off_ref, pos_ref, q_ref, g_ref, l_ref, d_ref, o_ref):
    n = pos_ref[0]
    head = lax.broadcasted_iota(jnp.int32, (HEADS, TOK), 0)
    lane = lax.broadcasted_iota(jnp.int32, (HEADS, TOK), 1)
    off = jnp.zeros((HEADS, TOK), jnp.int32)
    for h in range(HEADS):
        off = jnp.where(head == h, off_ref[0, h], off)
    hit = (lane % RATE) == off
    src = lax.broadcasted_iota(jnp.int32, (TOK, TOK), 0)
    dst = lax.broadcasted_iota(jnp.int32, (TOK, TOK), 1)
    place = jnp.where(dst == (n % 8) * PICK + src // RATE, 1.0, 0.0).astype(BF)
    lses = dot(jnp.where(hit, l_ref[0].astype(F32), 0.0).astype(BF), place)
    dlts = dot(jnp.where(hit, d_ref[0].astype(F32), 0.0).astype(BF), place)
    row = lax.broadcasted_iota(jnp.int32, (8, HD), 0)
    for h in range(HEADS):
        o_ref[h, 0:16] = pick(q_ref[0, :, h * HD:(h + 1) * HD], off_ref[0, h])
        o_ref[h, 16:32] = g_ref[h]
        lse = jnp.broadcast_to(lses[h:h + 1], (8, HD))
        dlt = jnp.broadcast_to(dlts[h:h + 1], (8, HD))
        stats = jnp.where(row == n // 8, lse, jnp.where(row == 2 + n // 8, dlt, 0.0))
        o_ref[h, 32:40] = stats.astype(BF)


def pick_grad(offsets, grad):
    return pl.pallas_call(
        pick_grad_kernel,
        in_specs=[SM, VM],
        out_specs=VM,
        out_shape=jax.ShapeDtypeStruct((HEADS, PICK, HD), BF),
        compiler_params=small(),
        name="pick_grad",
    )(offsets, grad)


def pick_kv(offsets, key, value):
    return pl.pallas_call(
        pick_kv_kernel,
        in_specs=[SM, VM, VM],
        out_specs=VM,
        out_shape=jax.ShapeDtypeStruct((HEADS, 2 * PICK, HD), BF),
        compiler_params=small(),
        name="pick_kv",
    )(offsets, key, value)


def pick_q(offsets, pos, query, grad, lse, delta):
    return pl.pallas_call(
        pick_q_kernel,
        in_specs=[SM, SM, VM, VM, VM, VM],
        out_specs=VM,
        out_shape=jax.ShapeDtypeStruct((HEADS, QG_ROWS, HD), BF),
        compiler_params=small(),
        name="pick_q",
    )(offsets, pos, query, grad, lse, delta)


def local_kernel(q_ref, k_ref, v_ref, g_ref, l_ref, d_ref, dq_ref, dk_ref, dv_ref, st_ref):
    step = pl.program_id(0)

    @pl.when(step == 0)
    def _():
        st_ref[0] = l_ref[0].astype(F32)
        st_ref[1] = d_ref[0].astype(F32)

    base = pl.multiple_of(step * 4, 4)
    lses = st_ref[0, pl.ds(base, 4), :]
    dlts = st_ref[1, pl.ds(base, 4), :]
    for i in range(4):
        cols = slice(i * HD, (i + 1) * HD)
        q, k, v, g = q_ref[0, :, cols], k_ref[0, :, cols], v_ref[0, :, cols], g_ref[0, :, cols]
        p = jnp.exp(dot_t(k, q) * SCALE - lses[i:i + 1])
        ds = (p * (dot_t(v, g) - dlts[i:i + 1])).astype(BF)
        dv_ref[:, cols] = dot(p.astype(BF), g).astype(BF)
        dk_ref[:, cols] = (dot(ds, q) * SCALE).astype(BF)
        dq_ref[:, cols] = (dot_l(ds, k) * SCALE).astype(BF)


def local_grads(query, key, value, grad, lse, delta):
    wide = pl.BlockSpec((1, TOK, 4 * HD), lambda i: (0, 0, i))
    out = pl.BlockSpec((TOK, 4 * HD), lambda i: (0, i))
    stat = pl.BlockSpec((1, HEADS, TOK), lambda i: (0, 0, 0))
    shape = jax.ShapeDtypeStruct((TOK, HEADS * HD), BF)
    return pl.pallas_call(
        local_kernel,
        grid=(4,),
        in_specs=[wide, wide, wide, wide, stat, stat],
        out_specs=[out, out, out],
        out_shape=[shape, shape, shape],
        scratch_shapes=[pltpu.VMEM((2, HEADS, TOK), F32)],
        compiler_params=small(),
        cost_estimate=pl.CostEstimate(flops=16 * 5 * 2 * 128 ** 3 * 4, bytes_accessed=3670016, transcendentals=262144),
        name="local_grads",
    )(query, key, value, grad, lse, delta)


def rows_of(ref, part):
    count = ref.shape[0]
    return ref[:, part * PICK:(part + 1) * PICK, :].reshape(count * PICK, HD)


def both_halves(a, b, part):
    return jnp.concatenate([rows_of(a, part), rows_of(b, part)], axis=0)


def stats_of(ref):
    return jnp.sum(ref[:, 32:40, :].astype(F32), axis=0)


def key_side(k, v, q, g, stats):
    lse = jnp.concatenate([stats[0:1], stats[1:2]], axis=1)
    dlt = jnp.concatenate([stats[2:3], stats[3:4]], axis=1)
    p = jnp.exp(dot_t(k, q) * SCALE - lse)
    ds = (p * (dot_t(v, g) - dlt)).astype(BF)
    return dot(ds, q), dot(p.astype(BF), g)


def wide_kernel(qg_ref, kv_ref, lkv_ref, rkv_ref, akv_ref, bkv_ref, lqg_ref, rqg_ref, dq_ref, dk_ref, dv_ref):
    q, g, k, v = rows_of(qg_ref, 0), rows_of(qg_ref, 1), rows_of(kv_ref, 0), rows_of(kv_ref, 1)
    stats = stats_of(qg_ref)
    turned = jnp.transpose(jnp.concatenate([stats, jnp.zeros((HD - 8, HD), F32)], axis=0))
    lse = jnp.concatenate([turned[:, 0:1], turned[:, 1:2]], axis=0)
    dlt = jnp.concatenate([turned[:, 2:3], turned[:, 3:4]], axis=0)
    dq = None
    for kx, vx in (
        (k, v),
        (rows_of(lkv_ref, 0), rows_of(lkv_ref, 1)),
        (rows_of(rkv_ref, 0), rows_of(rkv_ref, 1)),
        (both_halves(akv_ref, bkv_ref, 0), both_halves(akv_ref, bkv_ref, 1)),
    ):
        p = jnp.exp(dot_t(q, kx) * SCALE - lse)
        ds = (p * (dot_t(g, vx) - dlt)).astype(BF)
        part = dot(ds, kx)
        dq = part if dq is None else dq + part
    dq_ref[...] = (dq * SCALE).astype(BF).reshape(GROUP, PICK, HD)
    dk, dv = key_side(k, v, q, g, stats)
    for ref in (lqg_ref, rqg_ref):
        more_k, more_v = key_side(k, v, rows_of(ref, 0), rows_of(ref, 1), stats_of(ref))
        dk, dv = dk + more_k, dv + more_v
    dk_ref[...] = dk
    dv_ref[...] = dv


def wide_grads(*args):
    part = jax.ShapeDtypeStruct((GROUP * PICK, HD), F32)
    return pl.pallas_call(
        wide_kernel,
        in_specs=[VM] * 8,
        out_specs=[VM] * 3,
        out_shape=[jax.ShapeDtypeStruct((GROUP, PICK, HD), BF), part, part],
        compiler_params=small(),
        cost_estimate=pl.CostEstimate(flops=14 * 2 * 256 * 256 * 128 * 2, bytes_accessed=1572864, transcendentals=524288),
        name="wide_grads",
    )(*args)


def last_kernel(kv_ref, aqg_ref, bqg_ref, dq_ref, dk_ref, dv_ref, o_ref):
    k, v = rows_of(kv_ref, 0), rows_of(kv_ref, 1)
    q, g = both_halves(aqg_ref, bqg_ref, 0), both_halves(aqg_ref, bqg_ref, 1)
    dk, dv = key_side(k, v, q, g, stats_of(aqg_ref) + stats_of(bqg_ref))
    o_ref[:, 0:16, :] = dq_ref[...]
    o_ref[:, 16:32, :] = ((dk_ref[...] + dk) * SCALE).astype(BF).reshape(GROUP, PICK, HD)
    o_ref[:, 32:48, :] = (dv_ref[...] + dv).astype(BF).reshape(GROUP, PICK, HD)


def last_grads(*args):
    return pl.pallas_call(
        last_kernel,
        in_specs=[VM] * 6,
        out_specs=VM,
        out_shape=jax.ShapeDtypeStruct((GROUP, 3 * PICK, HD), BF),
        compiler_params=small(),
        name="last_grads",
    )(*args)


def combine_kernel(off_ref, w_ref, *refs):
    row = lax.broadcasted_iota(jnp.int32, (PICK, RATE, HD), 1)
    for h in range(HEADS):
        hit = row == off_ref[0, h]
        for part in range(3):
            w = w_ref[h, part * PICK:(part + 1) * PICK, :].astype(F32)
            local = refs[part][:, h * HD:(h + 1) * HD].astype(F32).reshape(PICK, RATE, HD)
            total = local + jnp.where(hit, w[:, None, :], 0.0)
            refs[3 + part][0, :, h * HD:(h + 1) * HD] = total.reshape(TOK, HD).astype(BF)


def combine(offsets, wide, local):
    shape = jax.ShapeDtypeStruct((1, TOK, HEADS * HD), BF)
    return pl.pallas_call(
        combine_kernel,
        in_specs=[SM] + [VM] * 4,
        out_specs=[VM] * 3,
        out_shape=[shape, shape, shape],
        compiler_params=small(),
        name="combine",
    )(offsets, wide, *local)


def place_of(z, x, c):
    return (z * NX + x) * NC + c


GROUPS = [[place_of(z, x, c) for z in range(NZ) for c in range(NC)] for x in range(NX)]


def shift_x(value, steps):
    pairs = [
        (place_of(z, x, c), place_of(z, (x + steps) % NX, c))
        for z in range(NZ) for x in range(NX) for c in range(NC)
    ]
    return lax.ppermute(value, "seq", pairs)


def from_next(value):
    count = lax.axis_size("section")
    return lax.ppermute(value, "section", [((s + 1) % count, s) for s in range(count)])


def swap(value):
    return lax.all_to_all(value, "seq", 0, 0, axis_index_groups=GROUPS, tiled=True)


def body(queries, key_rows, value_rows, grad_out, log_sums, deltas, offsets):
    seat = lax.axis_index("seq")
    pos = ((seat // (NX * NC)) * NC + seat % NC).astype(jnp.int32).reshape(1)
    grad_rows = pick_grad(offsets, grad_out)
    picked_grad = from_next(grad_rows)
    kv_rows = pick_kv(offsets, key_rows, value_rows)
    kv = swap(kv_rows)
    grad_src, picked_grad = lax.optimization_barrier((grad_out, picked_grad))
    grad = from_next(grad_src)
    qg_rows = pick_q(offsets, pos, queries, picked_grad, log_sums, deltas)
    qg_rows, _ = lax.optimization_barrier((qg_rows, kv))
    qg = swap(qg_rows)
    half = GROUP // 2
    left_kv = shift_x(kv, 1)
    right_kv = shift_x(kv, -1)
    left_qg = shift_x(qg, 1)
    right_qg = shift_x(qg, -1)
    left_far_kv = shift_x(left_kv[:half], 1)
    right_far_kv = shift_x(right_kv[half:], -1)
    far_kv = (left_far_kv, right_far_kv)
    far_qg = (shift_x(left_qg[:half], 1), shift_x(right_qg[half:], -1))
    local = local_grads(queries, key_rows, value_rows, grad, log_sums, deltas)
    dq, dk, dv = wide_grads(qg, kv, left_kv, right_kv, *far_kv, left_qg, right_qg)
    back = swap(last_grads(kv, *far_qg, dq, dk, dv))
    return tuple(combine(offsets, back, local))


def solution(mesh):
    rows = P("section", "seq", None)
    stats = P("section", None, "seq")
    return jax.shard_map(
        body,
        mesh=mesh,
        in_specs=(rows, rows, rows, rows, stats, stats, P("seq", None)),
        out_specs=(rows, rows, rows),
        check_vma=False,
    )
```

profile of v0, /device:TPU:1, one launch (start us, length us, event | category | flops | bytes accessed | tf_op | source)
XLA Modules:
  0.0 79.2 jit_solution(18383347437913464248)
XLA Ops:
  0.7 1.1 %copy-done.2 = bf16[1,128,2048]{2,1,0:T(8,128)(2,1)S(1)} copy-done((bf16[1,128,2048]{2,1,0:T(8,128)(2,1)S(1)}, bf16[1,128,2048]{2,1,0:T(8,128)(2,1)}, u32[]{:S(2)}) %copy-start.2) | copy-done | bytes 524312
  3.4 1.9 %pick_kv.1 = bf16[16,32,128]{2,1,0:T(8,128)(2,1)} custom-call(s32[1,16]{1,0:T(1,128)S(1)} %copy-done.6, bf16[1,128,2048]{2,1,0:T(8,128)(2,1)S(1)} %copy-done.2, bf16[1,128,2048]{2,1,0:T(8,128)(2,1)S(1)} %copy-done.4), custom_call_target="tpu_custom_call" | custom-call | tf_op jit(solution)/shard_map/pick_kv/pallas_call | solution.py:94
  5.4 10.1 %all-to-all-start = ((bf16[16,32,128]{2,1,0:T(8,128)(2,1)}), bf16[16,32,128]{2,1,0:T(8,128)(2,1)S(1)}, u32[]{:S(2)}, u32[]{:S(2)}) async-start(bf16[16,32,128]{2,1,0:T(8,128)(2,1)} %pick_kv.1), calls=%async_computation | async-start | bytes 262144 | tf_op jit(solution)/shard_map/all_to_all | solution.py:278
  16.4 2.8 %collective-permute-start = (bf16[16,16,128]{2,1,0:T(8,128)(2,1)S(1)}, bf16[16,16,128]{2,1,0:T(8,128)(2,1)S(1)}, u32[]{:S(2)}, u32[]{:S(2)}) collective-permute-start(bf16[16,16,128]{2,1,0:T(8,128)(2,1)S(1)} %pick_grad.1), channel_id=1, source_target_pairs={{64,0},{128,64},{192,128},{0,192},{65,1},{129,65},{193,129},{1,193... | collective-permute-start | bytes 196616 | tf_op jit(solution)/shard_map/ppermute | solution.py:274
  19.3 1.3 %collective-permute-done.g_ref = bf16[16,16,128]{2,1,0:T(8,128)(2,1)S(1)} collective-permute-done((bf16[16,16,128]{2,1,0:T(8,128)(2,1)S(1)}, bf16[16,16,128]{2,1,0:T(8,128)(2,1)S(1)}, u32[]{:S(2)}, u32[]{:S(2)}) %collective-permute-start) | collective-permute-done | bytes 65568 | tf_op jit(solution)/shard_map/ppermute | solution.py:274
  20.6 1.7 %pick_q.1 = bf16[16,40,128]{2,1,0:T(8,128)(2,1)} custom-call(s32[1,16]{1,0:T(1,128)S(1)} %copy-done.7, s32[1]{0:T(128)} %bitcast.pos_ref, bf16[1,128,2048]{2,1,0:T(8,128)(2,1)S(1)} %copy-done, bf16[16,16,128]{2,1,0:T(8,128)(2,1)S(1)} %collective-permute-done.g_ref, bf16[1,16,128]{2,1,0:T(8,128)(2,1)S(1)} %copy-done.8, bf16[1,16,128]{2,1,0:T(8,128)(2,1)S(1)} %copy-done.9), custom_call_target="tpu_custom_call" | custom-call | tf_op jit(solution)/shard_map/pick_q/pallas_call | solution.py:105
  22.2 2.1 %all-to-all-done.kv_ref = bf16[16,32,128]{2,1,0:T(8,128)(2,1)S(1)} async-done(((bf16[16,32,128]{2,1,0:T(8,128)(2,1)}), bf16[16,32,128]{2,1,0:T(8,128)(2,1)S(1)}, u32[]{:S(2)}, u32[]{:S(2)}) %all-to-all-start) | async-done | bytes 131104 | tf_op jit(solution)/shard_map/all_to_all | solution.py:278
  24.4 6.0 %all-to-all-start.1 = ((bf16[16,40,128]{2,1,0:T(8,128)(2,1)}), bf16[16,40,128]{2,1,0:T(8,128)(2,1)S(1)}, u32[]{:S(2)}, u32[]{:S(2)}) async-start(bf16[16,40,128]{2,1,0:T(8,128)(2,1)} %pick_q.1), calls=%async_computation.1 | async-start | bytes 327680 | tf_op jit(solution)/shard_map/all_to_all | solution.py:278
  30.3 3.3 %collective-permute-start.9 = (bf16[1,128,2048]{2,1,0:T(8,128)(2,1)S(1)}, bf16[1,128,2048]{2,1,0:T(8,128)(2,1)S(1)}, u32[]{:S(2)}, u32[]{:S(2)}) collective-permute-start(bf16[1,128,2048]{2,1,0:T(8,128)(2,1)S(1)} %copy-done.1), channel_id=1, source_target_pairs={{64,0},{128,64},{192,128},{0,192},{65,1},{129,65},{193,129},{1,193... | collective-permute-start | bytes 1572872 | tf_op jit(solution)/shard_map/ppermute | solution.py:274
  33.6 6.2 %all-to-all-done.1.qg_ref = bf16[16,40,128]{2,1,0:T(8,128)(2,1)S(1)} async-done(((bf16[16,40,128]{2,1,0:T(8,128)(2,1)}), bf16[16,40,128]{2,1,0:T(8,128)(2,1)S(1)}, u32[]{:S(2)}, u32[]{:S(2)}) %all-to-all-start.1) | async-done | bytes 163872 | tf_op jit(solution)/shard_map/all_to_all | solution.py:278
  39.9 2.5 %collective-permute-start.3 = (bf16[16,40,128]{2,1,0:T(8,128)(2,1)S(1)}, bf16[16,40,128]{2,1,0:T(8,128)(2,1)S(1)}, u32[]{:S(2)}, u32[]{:S(2)}) collective-permute-start(bf16[16,40,128]{2,1,0:T(8,128)(2,1)S(1)} %all-to-all-done.1.qg_ref), channel_id=1, source_target_pairs={{0,6},{1,7},{2,0},{3,1},{4,2},{5,3},{6,4},{7,5},{8,14},{9,15},{10,... | collective-permute-start | bytes 491528 | tf_op jit(solution)/shard_map/ppermute | solution.py:269
  42.3 2.7 %collective-permute-start.6 = (bf16[16,32,128]{2,1,0:T(8,128)(2,1)S(1)}, bf16[16,32,128]{2,1,0:T(8,128)(2,1)S(1)}, u32[]{:S(2)}, u32[]{:S(2)}) collective-permute-start(bf16[16,32,128]{2,1,0:T(8,128)(2,1)S(1)} %all-to-all-done.kv_ref), channel_id=1, source_target_pairs={{0,6},{1,7},{2,0},{3,1},{4,2},{5,3},{6,4},{7,5},{8,14},{9,15},{10,... | collective-permute-start | bytes 393224 | tf_op jit(solution)/shard_map/ppermute | solution.py:269
  45.0 3.9 %collective-permute-done.6.rkv_ref = bf16[16,32,128]{2,1,0:T(8,128)(2,1)S(1)} collective-permute-done((bf16[16,32,128]{2,1,0:T(8,128)(2,1)S(1)}, bf16[16,32,128]{2,1,0:T(8,128)(2,1)S(1)}, u32[]{:S(2)}, u32[]{:S(2)}) %collective-permute-start.6) | collective-permute-done | bytes 131104 | tf_op jit(solution)/shard_map/ppermute | solution.py:269
  48.9 3.4 %collective-permute-start.8 = (bf16[8,32,128]{2,1,0:T(8,128)(2,1)S(1)}, bf16[8,32,128]{2,1,0:T(8,128)(2,1)S(1)}, u32[]{:S(2)}, u32[]{:S(2)}) collective-permute-start(bf16[8,32,128]{2,1,0:T(8,128)(2,1)S(1)} %slice.19), channel_id=1, source_target_pairs={{0,6},{1,7},{2,0},{3,1},{4,2},{5,3},{6,4},{7,5},{8,14},{9,15},{10,... | collective-permute-start | bytes 196616 | tf_op jit(solution)/shard_map/ppermute | solution.py:269
  52.5 2.7 %collective-permute-start.4 = (bf16[8,40,128]{2,1,0:T(8,128)(2,1)S(1)}, bf16[8,40,128]{2,1,0:T(8,128)(2,1)S(1)}, u32[]{:S(2)}, u32[]{:S(2)}) collective-permute-start(bf16[8,40,128]{2,1,0:T(8,128)(2,1)S(1)} %slice.17), channel_id=1, source_target_pairs={{0,6},{1,7},{2,0},{3,1},{4,2},{5,3},{6,4},{7,5},{8,14},{9,15},{10,... | collective-permute-start | bytes 245768 | tf_op jit(solution)/shard_map/ppermute | solution.py:269
  55.3 1.4 %collective-permute-done.7.akv_ref = bf16[8,32,128]{2,1,0:T(8,128)(2,1)S(1)} collective-permute-done((bf16[8,32,128]{2,1,0:T(8,128)(2,1)S(1)}, bf16[8,32,128]{2,1,0:T(8,128)(2,1)S(1)}, u32[]{:S(2)}, u32[]{:S(2)}) %collective-permute-start.7) | collective-permute-done | bytes 65568 | tf_op jit(solution)/shard_map/ppermute | solution.py:269
  56.8 1.4 %wide_grads.1 = (bf16[16,16,128]{2,1,0:T(8,128)(2,1)S(1)}, f32[256,128]{1,0:T(8,128)S(1)}, f32[256,128]{1,0:T(8,128)S(1)}) custom-call(bf16[16,40,128]{2,1,0:T(8,128)(2,1)S(1)} %all-to-all-done.1.qg_ref, bf16[16,32,128]{2,1,0:T(8,128)(2,1)S(1)} %all-to-all-done.kv_ref, bf16[16,32,128]{2,1,0:T(8,128)(2,1)S(1)} %collective-permute-done.5.lkv_ref, ...), custom_call_target="tpu_custom_call" | custom-call | flops 469762048 | bytes 1572864 | tf_op jit(solution)/shard_map/wide_grads/pallas_call | solution.py:203
  58.2 1.6 %collective-permute-done.2.aqg_ref = bf16[8,40,128]{2,1,0:T(8,128)(2,1)S(1)} collective-permute-done((bf16[8,40,128]{2,1,0:T(8,128)(2,1)S(1)}, bf16[8,40,128]{2,1,0:T(8,128)(2,1)S(1)}, u32[]{:S(2)}, u32[]{:S(2)}) %collective-permute-start.2) | collective-permute-done | bytes 81952 | tf_op jit(solution)/shard_map/ppermute | solution.py:269
  59.8 1.1 %last_grads.1 = bf16[16,48,128]{2,1,0:T(8,128)(2,1)} custom-call(bf16[16,32,128]{2,1,0:T(8,128)(2,1)S(1)} %all-to-all-done.kv_ref, bf16[8,40,128]{2,1,0:T(8,128)(2,1)S(1)} %collective-permute-done.2.aqg_ref, bf16[8,40,128]{2,1,0:T(8,128)(2,1)S(1)} %collective-permute-done.4.bqg_ref, bf16[16,16,128]{2,1,0:T(8,128)(2,1)S(1)} %get-tuple-element.14.dq_ref, ...), custom_call_target="tpu_custom_call" | custom-call | tf_op jit(solution)/shard_map/last_grads/pallas_call | solution.py:224
  60.9 5.9 %all-to-all-start.2 = ((bf16[16,48,128]{2,1,0:T(8,128)(2,1)}), bf16[16,48,128]{2,1,0:T(8,128)(2,1)S(1)}, u32[]{:S(2)}, u32[]{:S(2)}) async-start(bf16[16,48,128]{2,1,0:T(8,128)(2,1)} %last_grads.1), calls=%async_computation.2 | async-start | bytes 393216 | tf_op jit(solution)/shard_map/all_to_all | solution.py:278
  67.6 1.0 %copy-done.11 = bf16[1,128,2048]{2,1,0:T(8,128)(2,1)S(1)} copy-done((bf16[1,128,2048]{2,1,0:T(8,128)(2,1)S(1)}, bf16[1,128,2048]{2,1,0:T(8,128)(2,1)}, u32[]{:S(2)}) %copy-start.11) | copy-done | bytes 524312
  68.6 4.4 %local_grads.1 = (bf16[128,2048]{1,0:T(8,128)(2,1)S(1)}, bf16[128,2048]{1,0:T(8,128)(2,1)S(1)}, bf16[128,2048]{1,0:T(8,128)(2,1)S(1)}) custom-call(bf16[1,128,2048]{2,1,0:T(8,128)(2,1)S(1)} %copy-done, bf16[1,128,2048]{2,1,0:T(8,128)(2,1)S(1)} %copy-done.3, bf16[1,128,2048]{2,1,0:T(8,128)(2,1)S(1)} %copy-done.5, bf16[1,128,2048]{2,1,0:T(8,128)(2,1)S(1)} %copy-done.11, ...), custom_call_target="tpu_custom_call" | custom-call | flops 1342177280 | bytes 3670016 | tf_op jit(solution)/shard_map/local_grads/pallas_call | solution.py:141
  73.0 4.0 %all-to-all-done.2.w_ref = bf16[16,48,128]{2,1,0:T(8,128)(2,1)S(1)} async-done(((bf16[16,48,128]{2,1,0:T(8,128)(2,1)}), bf16[16,48,128]{2,1,0:T(8,128)(2,1)S(1)}, u32[]{:S(2)}, u32[]{:S(2)}) %all-to-all-start.2) | async-done | bytes 196640 | tf_op jit(solution)/shard_map/all_to_all | solution.py:278
  77.1 2.2 %combine.1 = (bf16[1,128,2048]{2,1,0:T(8,128)(2,1)}, bf16[1,128,2048]{2,1,0:T(8,128)(2,1)}, bf16[1,128,2048]{2,1,0:T(8,128)(2,1)}) custom-call(s32[1,16]{1,0:T(1,128)S(1)} %copy-done.7, bf16[16,48,128]{2,1,0:T(8,128)(2,1)S(1)} %all-to-all-done.2.w_ref, bf16[128,2048]{1,0:T(8,128)(2,1)S(1)} %get-tuple-element.18.refs_0_, ...), custom_call_target="tpu_custom_call" | custom-call | tf_op jit(solution)/shard_map/combine/pallas_call | solution.py:247
  (37 shorter events, 3.7 us)
Async XLA Ops:
  0.6 14.9 %copy-start.1 = (bf16[1,128,2048]{2,1,0:T(8,128)(2,1)S(1)}, bf16[1,128,2048]{2,1,0:T(8,128)(2,1)}, u32[]{:S(2)}) copy-start(bf16[1,128,2048]{2,1,0:T(8,128)(2,1)} %g_ref.1) | copy-start | bytes 1572868
  0.6 1.1 %copy-start.2 = (bf16[1,128,2048]{2,1,0:T(8,128)(2,1)S(1)}, bf16[1,128,2048]{2,1,0:T(8,128)(2,1)}, u32[]{:S(2)}) copy-start(bf16[1,128,2048]{2,1,0:T(8,128)(2,1)} %k_ref.3) | copy-start | bytes 1572868
  1.7 1.0 %copy-start.4 = (bf16[1,128,2048]{2,1,0:T(8,128)(2,1)S(1)}, bf16[1,128,2048]{2,1,0:T(8,128)(2,1)}, u32[]{:S(2)}) copy-start(bf16[1,128,2048]{2,1,0:T(8,128)(2,1)} %v_ref.3) | copy-start | bytes 1572868
  3.4 12.1 %copy-start.7 = (s32[1,16]{1,0:T(1,128)S(1)}, s32[1,16]{1,0:T(1,128)}, u32[]{:S(2)}) copy-start(s32[1,16]{1,0:T(1,128)} %off_ref.7) | copy-start | bytes 196
  5.4 15.2 %copy-start = (bf16[1,128,2048]{2,1,0:T(8,128)(2,1)S(1)}, bf16[1,128,2048]{2,1,0:T(8,128)(2,1)}, u32[]{:S(2)}) copy-start(bf16[1,128,2048]{2,1,0:T(8,128)(2,1)} %q_ref.3) | copy-start | bytes 1572868
  5.4 19.0 %all-to-all-start = ((bf16[16,32,128]{2,1,0:T(8,128)(2,1)}), bf16[16,32,128]{2,1,0:T(8,128)(2,1)S(1)}, u32[]{:S(2)}, u32[]{:S(2)}) async-start(bf16[16,32,128]{2,1,0:T(8,128)(2,1)} %pick_kv.1), calls=%async_computation | async-start | bytes 262144 | tf_op jit(solution)/shard_map/all_to_all | solution.py:278
  16.4 4.1 %collective-permute-start = (bf16[16,16,128]{2,1,0:T(8,128)(2,1)S(1)}, bf16[16,16,128]{2,1,0:T(8,128)(2,1)S(1)}, u32[]{:S(2)}, u32[]{:S(2)}) collective-permute-start(bf16[16,16,128]{2,1,0:T(8,128)(2,1)S(1)} %pick_grad.1), channel_id=1, source_target_pairs={{64,0},{128,64},{192,128},{0,192},{65,1},{129,65},{193,129},{1,193... | collective-permute-start | bytes 196616 | tf_op jit(solution)/shard_map/ppermute | solution.py:274
  19.3 1.3 %copy-start.9 = (bf16[1,16,128]{2,1,0:T(8,128)(2,1)S(1)}, bf16[1,16,128]{2,1,0:T(8,128)(2,1)}, u32[]{:S(2)}) copy-start(bf16[1,16,128]{2,1,0:T(8,128)(2,1)} %d_ref.3) | copy-start | bytes 12292
  19.3 1.3 %copy-start.8 = (bf16[1,16,128]{2,1,0:T(8,128)(2,1)S(1)}, bf16[1,16,128]{2,1,0:T(8,128)(2,1)}, u32[]{:S(2)}) copy-start(bf16[1,16,128]{2,1,0:T(8,128)(2,1)} %l_ref.3) | copy-start | bytes 12292
  24.4 15.5 %all-to-all-start.1 = ((bf16[16,40,128]{2,1,0:T(8,128)(2,1)}), bf16[16,40,128]{2,1,0:T(8,128)(2,1)S(1)}, u32[]{:S(2)}, u32[]{:S(2)}) async-start(bf16[16,40,128]{2,1,0:T(8,128)(2,1)} %pick_q.1), calls=%async_computation.1 | async-start | bytes 327680 | tf_op jit(solution)/shard_map/all_to_all | solution.py:278
  30.3 36.5 %collective-permute-start.9 = (bf16[1,128,2048]{2,1,0:T(8,128)(2,1)S(1)}, bf16[1,128,2048]{2,1,0:T(8,128)(2,1)S(1)}, u32[]{:S(2)}, u32[]{:S(2)}) collective-permute-start(bf16[1,128,2048]{2,1,0:T(8,128)(2,1)S(1)} %copy-done.1), channel_id=1, source_target_pairs={{64,0},{128,64},{192,128},{0,192},{65,1},{129,65},{193,129},{1,193... | collective-permute-start | bytes 1572872 | tf_op jit(solution)/shard_map/ppermute | solution.py:274
  39.9 12.6 %collective-permute-start.3 = (bf16[16,40,128]{2,1,0:T(8,128)(2,1)S(1)}, bf16[16,40,128]{2,1,0:T(8,128)(2,1)S(1)}, u32[]{:S(2)}, u32[]{:S(2)}) collective-permute-start(bf16[16,40,128]{2,1,0:T(8,128)(2,1)S(1)} %all-to-all-done.1.qg_ref), channel_id=1, source_target_pairs={{0,6},{1,7},{2,0},{3,1},{4,2},{5,3},{6,4},{7,5},{8,14},{9,15},{10,... | collective-permute-start | bytes 491528 | tf_op jit(solution)/shard_map/ppermute | solution.py:269
  42.3 12.9 %collective-permute-start.1 = (bf16[16,40,128]{2,1,0:T(8,128)(2,1)S(1)}, bf16[16,40,128]{2,1,0:T(8,128)(2,1)S(1)}, u32[]{:S(2)}, u32[]{:S(2)}) collective-permute-start(bf16[16,40,128]{2,1,0:T(8,128)(2,1)S(1)} %all-to-all-done.1.qg_ref), channel_id=1, source_target_pairs={{0,2},{1,3},{2,4},{3,5},{4,6},{5,7},{6,0},{7,1},{8,10},{9,11},{10,... | collective-permute-start | bytes 491528 | tf_op jit(solution)/shard_map/ppermute | solution.py:269
  42.3 6.6 %collective-permute-start.6 = (bf16[16,32,128]{2,1,0:T(8,128)(2,1)S(1)}, bf16[16,32,128]{2,1,0:T(8,128)(2,1)S(1)}, u32[]{:S(2)}, u32[]{:S(2)}) collective-permute-start(bf16[16,32,128]{2,1,0:T(8,128)(2,1)S(1)} %all-to-all-done.kv_ref), channel_id=1, source_target_pairs={{0,6},{1,7},{2,0},{3,1},{4,2},{5,3},{6,4},{7,5},{8,14},{9,15},{10,... | collective-permute-start | bytes 393224 | tf_op jit(solution)/shard_map/ppermute | solution.py:269
  45.0 7.3 %collective-permute-start.5 = (bf16[16,32,128]{2,1,0:T(8,128)(2,1)S(1)}, bf16[16,32,128]{2,1,0:T(8,128)(2,1)S(1)}, u32[]{:S(2)}, u32[]{:S(2)}) collective-permute-start(bf16[16,32,128]{2,1,0:T(8,128)(2,1)S(1)} %all-to-all-done.kv_ref), channel_id=1, source_target_pairs={{0,2},{1,3},{2,4},{3,5},{4,6},{5,7},{6,0},{7,1},{8,10},{9,11},{10,... | collective-permute-start | bytes 393224 | tf_op jit(solution)/shard_map/ppermute | solution.py:269
  48.9 6.4 %collective-permute-start.8 = (bf16[8,32,128]{2,1,0:T(8,128)(2,1)S(1)}, bf16[8,32,128]{2,1,0:T(8,128)(2,1)S(1)}, u32[]{:S(2)}, u32[]{:S(2)}) collective-permute-start(bf16[8,32,128]{2,1,0:T(8,128)(2,1)S(1)} %slice.19), channel_id=1, source_target_pairs={{0,6},{1,7},{2,0},{3,1},{4,2},{5,3},{6,4},{7,5},{8,14},{9,15},{10,... | collective-permute-start | bytes 196616 | tf_op jit(solution)/shard_map/ppermute | solution.py:269
  52.4 4.4 %collective-permute-start.7 = (bf16[8,32,128]{2,1,0:T(8,128)(2,1)S(1)}, bf16[8,32,128]{2,1,0:T(8,128)(2,1)S(1)}, u32[]{:S(2)}, u32[]{:S(2)}) collective-permute-start(bf16[8,32,128]{2,1,0:T(8,128)(2,1)S(1)} %slice.18), channel_id=1, source_target_pairs={{0,2},{1,3},{2,4},{3,5},{4,6},{5,7},{6,0},{7,1},{8,10},{9,11},{10,... | collective-permute-start | bytes 196616 | tf_op jit(solution)/shard_map/ppermute | solution.py:269
  52.5 5.7 %collective-permute-start.4 = (bf16[8,40,128]{2,1,0:T(8,128)(2,1)S(1)}, bf16[8,40,128]{2,1,0:T(8,128)(2,1)S(1)}, u32[]{:S(2)}, u32[]{:S(2)}) collective-permute-start(bf16[8,40,128]{2,1,0:T(8,128)(2,1)S(1)} %slice.17), channel_id=1, source_target_pairs={{0,6},{1,7},{2,0},{3,1},{4,2},{5,3},{6,4},{7,5},{8,14},{9,15},{10,... | collective-permute-start | bytes 245768 | tf_op jit(solution)/shard_map/ppermute | solution.py:269
  55.2 4.6 %collective-permute-start.2 = (bf16[8,40,128]{2,1,0:T(8,128)(2,1)S(1)}, bf16[8,40,128]{2,1,0:T(8,128)(2,1)S(1)}, u32[]{:S(2)}, u32[]{:S(2)}) collective-permute-start(bf16[8,40,128]{2,1,0:T(8,128)(2,1)S(1)} %slice.16), channel_id=1, source_target_pairs={{0,2},{1,3},{2,4},{3,5},{4,6},{5,7},{6,0},{7,1},{8,10},{9,11},{10,... | collective-permute-start | bytes 245768 | tf_op jit(solution)/shard_map/ppermute | solution.py:269
  59.8 7.8 %copy-start.3 = (bf16[1,128,2048]{2,1,0:T(8,128)(2,1)S(1)}, bf16[1,128,2048]{2,1,0:T(8,128)(2,1)}, u32[]{:S(2)}) copy-start(bf16[1,128,2048]{2,1,0:T(8,128)(2,1)} %k_ref.3) | copy-start | bytes 1572868
  59.8 7.8 %copy-start.5 = (bf16[1,128,2048]{2,1,0:T(8,128)(2,1)S(1)}, bf16[1,128,2048]{2,1,0:T(8,128)(2,1)}, u32[]{:S(2)}) copy-start(bf16[1,128,2048]{2,1,0:T(8,128)(2,1)} %v_ref.3) | copy-start | bytes 1572868
  60.9 16.2 %all-to-all-start.2 = ((bf16[16,48,128]{2,1,0:T(8,128)(2,1)}), bf16[16,48,128]{2,1,0:T(8,128)(2,1)S(1)}, u32[]{:S(2)}, u32[]{:S(2)}) async-start(bf16[16,48,128]{2,1,0:T(8,128)(2,1)} %last_grads.1), calls=%async_computation.2 | async-start | bytes 393216 | tf_op jit(solution)/shard_map/all_to_all | solution.py:278
  66.8 0.8 %copy-start.10 = (bf16[1,128,2048]{2,1,0:T(8,128)(2,1)}, bf16[1,128,2048]{2,1,0:T(8,128)(2,1)S(1)}, u32[]{:S(2)}) copy-start(bf16[1,128,2048]{2,1,0:T(8,128)(2,1)S(1)} %collective-permute-done.9.g_ref) | copy-start | bytes 1572868
  67.6 1.0 %copy-start.11 = (bf16[1,128,2048]{2,1,0:T(8,128)(2,1)S(1)}, bf16[1,128,2048]{2,1,0:T(8,128)(2,1)}, u32[]{:S(2)}) copy-start(bf16[1,128,2048]{2,1,0:T(8,128)(2,1)} %copy-done.10) | copy-start | bytes 1572868
  (1 other events, 0.7 us)
where the time goes:
time: 79.7 us; the launch traced here: 79.2 us
  starting transfers between devices  39.5 us (50%)
  waiting for transfers between devices  20.7 us (26%)
  Pallas kernels  13.6 us (17%)
  local copies, waits for them, and re-layouts  4.67 us (6%)
    all_to_all x3, starting transfers between devices, swap(): lax.all_to_all(value, 'seq', 0, 0, axis_index_groups=GROUPS, tiled=True)  22 us
    all_to_all x3, waiting for transfers between devices, swap(): lax.all_to_all(value, 'seq', 0, 0, axis_index_groups=GROUPS, tiled=True)  12.4 us
    ppermute x8, starting transfers between devices, shift_x(): return lax.ppermute(value, 'seq', pairs)  11.5 us
    ppermute x8, waiting for transfers between devices, shift_x(): return lax.ppermute(value, 'seq', pairs)  6.95 us
    ppermute x2, starting transfers between devices, from_next(): lax.ppermute(value, 'section', [((s + 1) % count, s) for s in range(count)])  6.1 us
    unnamed x24, local copies, waits for them, and re-layouts  4.65 us
    pallas_call x1, Pallas kernels, local_grads(): pl.pallas_call(local_kernel, grid=(4,), in_specs=[wide, wide, wide, wide,...  4.38 us
    pallas_call x1, Pallas kernels, combine(): pl.pallas_call(combine_kernel, in_specs=[SM] + [VM] * 4, out_specs=[VM] *...  2.19 us
  transfers between devices with their start and end apart: 13, of which 7 were waited for; matrix products, arithmetic and copies ran while one was open for 0% of the time, Pallas kernels for 12%

commit v1 on v0

--- a/solution.py
+++ b/solution.py
@@ -12,7 +12,7 @@
 RATE = 8
 TOK = 128
 NZ, NX, NC = 8, 4, 2
-QG_ROWS = 40
+ROWS = 72
 GROUP = NZ * NC
 SCALE = HD ** (-0.5)
 BF = jnp.bfloat16
@@ -49,14 +49,7 @@
         o_ref[h] = pick(g_ref[0, :, h * HD:(h + 1) * HD], off_ref[0, h])
 
 
-def pick_kv_kernel(off_ref, k_ref, v_ref, o_ref):
-    for h in range(HEADS):
-        cols = slice(h * HD, (h + 1) * HD)
-        o_ref[h, 0:16] = pick(k_ref[0, :, cols], off_ref[0, h])
-        o_ref[h, 16:32] = pick(v_ref[0, :, cols], off_ref[0, h])
-
-
-def pick_q_kernel(off_ref, pos_ref, q_ref, g_ref, l_ref, d_ref, o_ref):
+def pick_kernel(off_ref, pos_ref, q_ref, k_ref, v_ref, l_ref, d_ref, o_ref):
     n = pos_ref[0]
     head = lax.broadcasted_iota(jnp.int32, (HEADS, TOK), 0)
     lane = lax.broadcasted_iota(jnp.int32, (HEADS, TOK), 1)
@@ -71,12 +64,18 @@
     dlts = dot(jnp.where(hit, d_ref[0].astype(F32), 0.0).astype(BF), place)
     row = lax.broadcasted_iota(jnp.int32, (8, HD), 0)
     for h in range(HEADS):
-        o_ref[h, 0:16] = pick(q_ref[0, :, h * HD:(h + 1) * HD], off_ref[0, h])
-        o_ref[h, 16:32] = g_ref[h]
+        cols = slice(h * HD, (h + 1) * HD)
+        o_ref[h, 0:16] = pick(q_ref[0, :, cols], off_ref[0, h])
+        o_ref[h, 16:32] = pick(k_ref[0, :, cols], off_ref[0, h])
+        o_ref[h, 32:48] = pick(v_ref[0, :, cols], off_ref[0, h])
         lse = jnp.broadcast_to(lses[h:h + 1], (8, HD))
         dlt = jnp.broadcast_to(dlts[h:h + 1], (8, HD))
         stats = jnp.where(row == n // 8, lse, jnp.where(row == 2 + n // 8, dlt, 0.0))
-        o_ref[h, 32:40] = stats.astype(BF)
+        o_ref[h, 64:72] = stats.astype(BF)
+
+
+def join_kernel(rows_ref, g_ref, o_ref):
+    o_ref[:, 48:64, :] = g_ref[...]
 
 
 def pick_grad(offsets, grad):
@@ -90,26 +89,27 @@
     )(offsets, grad)
 
 
-def pick_kv(offsets, key, value):
-    return pl.pallas_call(
-        pick_kv_kernel,
-        in_specs=[SM, VM, VM],
+def pick_rest(offsets, pos, query, key, value, lse, delta):
+    return pl.pallas_call(
+        pick_kernel,
+        in_specs=[SM, SM] + [VM] * 5,
         out_specs=VM,
-        out_shape=jax.ShapeDtypeStruct((HEADS, 2 * PICK, HD), BF),
-        compiler_params=small(),
-        name="pick_kv",
-    )(offsets, key, value)
-
-
-def pick_q(offsets, pos, query, grad, lse, delta):
-    return pl.pallas_call(
-        pick_q_kernel,
-        in_specs=[SM, SM, VM, VM, VM, VM],
+        out_shape=jax.ShapeDtypeStruct((HEADS, ROWS, HD), BF),
+        compiler_params=small(),
+        name="pick_rest",
+    )(offsets, pos, query, key, value, lse, delta)
+
+
+def join(rows, grad):
+    return pl.pallas_call(
+        join_kernel,
+        in_specs=[VM, VM],
         out_specs=VM,
-        out_shape=jax.ShapeDtypeStruct((HEADS, QG_ROWS, HD), BF),
-        compiler_params=small(),
-        name="pick_q",
-    )(offsets, pos, query, grad, lse, delta)
+        out_shape=jax.ShapeDtypeStruct((HEADS, ROWS, HD), BF),
+        input_output_aliases={0: 0},
+        compiler_params=small(),
+        name="join",
+    )(rows, grad)
 
 
 def local_kernel(q_ref, k_ref, v_ref, g_ref, l_ref, d_ref, dq_ref, dk_ref, dv_ref, st_ref):
@@ -161,7 +161,13 @@
 
 
 def stats_of(ref):
-    return jnp.sum(ref[:, 32:40, :].astype(F32), axis=0)
+    return jnp.sum(ref[:, 64:72, :].astype(F32), axis=0)
+
+
+def query_side(q, g, k, v, lse, dlt):
+    p = jnp.exp(dot_t(q, k) * SCALE - lse)
+    ds = (p * (dot_t(g, v) - dlt)).astype(BF)
+    return dot(ds, k)
 
 
 def key_side(k, v, q, g, stats):
@@ -172,62 +178,61 @@
     return dot(ds, q), dot(p.astype(BF), g)
 
 
-def wide_kernel(qg_ref, kv_ref, lkv_ref, rkv_ref, akv_ref, bkv_ref, lqg_ref, rqg_ref, dq_ref, dk_ref, dv_ref):
-    q, g, k, v = rows_of(qg_ref, 0), rows_of(qg_ref, 1), rows_of(kv_ref, 0), rows_of(kv_ref, 1)
-    stats = stats_of(qg_ref)
+def columns(stats):
     turned = jnp.transpose(jnp.concatenate([stats, jnp.zeros((HD - 8, HD), F32)], axis=0))
     lse = jnp.concatenate([turned[:, 0:1], turned[:, 1:2]], axis=0)
     dlt = jnp.concatenate([turned[:, 2:3], turned[:, 3:4]], axis=0)
-    dq = None
-    for kx, vx in (
-        (k, v),
-        (rows_of(lkv_ref, 0), rows_of(lkv_ref, 1)),
-        (rows_of(rkv_ref, 0), rows_of(rkv_ref, 1)),
-        (both_halves(akv_ref, bkv_ref, 0), both_halves(akv_ref, bkv_ref, 1)),
-    ):
-        p = jnp.exp(dot_t(q, kx) * SCALE - lse)
-        ds = (p * (dot_t(g, vx) - dlt)).astype(BF)
-        part = dot(ds, kx)
-        dq = part if dq is None else dq + part
-    dq_ref[...] = (dq * SCALE).astype(BF).reshape(GROUP, PICK, HD)
+    return lse, dlt
+
+
+def near_kernel(own_ref, left_ref, right_ref, dq_ref, dk_ref, dv_ref):
+    q, k, v, g = (rows_of(own_ref, part) for part in range(4))
+    stats = stats_of(own_ref)
+    lse, dlt = columns(stats)
+    dq = query_side(q, g, k, v, lse, dlt)
     dk, dv = key_side(k, v, q, g, stats)
-    for ref in (lqg_ref, rqg_ref):
-        more_k, more_v = key_side(k, v, rows_of(ref, 0), rows_of(ref, 1), stats_of(ref))
+    for ref in (left_ref, right_ref):
+        qx, kx, vx, gx = (rows_of(ref, part) for part in range(4))
+        dq = dq + query_side(q, g, kx, vx, lse, dlt)
+        more_k, more_v = key_side(k, v, qx, gx, stats_of(ref))
         dk, dv = dk + more_k, dv + more_v
+    dq_ref[...] = dq
     dk_ref[...] = dk
     dv_ref[...] = dv
 
 
-def wide_grads(*args):
+def near_grads(*args):
     part = jax.ShapeDtypeStruct((GROUP * PICK, HD), F32)
     return pl.pallas_call(
-        wide_kernel,
-        in_specs=[VM] * 8,
+        near_kernel,
+        in_specs=[VM] * 3,
         out_specs=[VM] * 3,
-        out_shape=[jax.ShapeDtypeStruct((GROUP, PICK, HD), BF), part, part],
-        compiler_params=small(),
-        cost_estimate=pl.CostEstimate(flops=14 * 2 * 256 * 256 * 128 * 2, bytes_accessed=1572864, transcendentals=524288),
-        name="wide_grads",
+        out_shape=[part] * 3,
+        compiler_params=small(),
+        cost_estimate=pl.CostEstimate(flops=21 * 2 * 256 * 256 * 128 * 2, bytes_accessed=1572864, transcendentals=524288),
+        name="near_grads",
     )(*args)
 
 
-def last_kernel(kv_ref, aqg_ref, bqg_ref, dq_ref, dk_ref, dv_ref, o_ref):
-    k, v = rows_of(kv_ref, 0), rows_of(kv_ref, 1)
-    q, g = both_halves(aqg_ref, bqg_ref, 0), both_halves(aqg_ref, bqg_ref, 1)
-    dk, dv = key_side(k, v, q, g, stats_of(aqg_ref) + stats_of(bqg_ref))
-    o_ref[:, 0:16, :] = dq_ref[...]
+def far_kernel(own_ref, a_ref, b_ref, dq_ref, dk_ref, dv_ref, o_ref):
+    q, k, v, g = (rows_of(own_ref, part) for part in range(4))
+    lse, dlt = columns(stats_of(own_ref))
+    qx, kx, vx, gx = (both_halves(a_ref, b_ref, part) for part in range(4))
+    dq = query_side(q, g, kx, vx, lse, dlt)
+    dk, dv = key_side(k, v, qx, gx, stats_of(a_ref) + stats_of(b_ref))
+    o_ref[:, 0:16, :] = ((dq_ref[...] + dq) * SCALE).astype(BF).reshape(GROUP, PICK, HD)
     o_ref[:, 16:32, :] = ((dk_ref[...] + dk) * SCALE).astype(BF).reshape(GROUP, PICK, HD)
     o_ref[:, 32:48, :] = (dv_ref[...] + dv).astype(BF).reshape(GROUP, PICK, HD)
 
 
-def last_grads(*args):
-    return pl.pallas_call(
-        last_kernel,
+def far_grads(*args):
+    return pl.pallas_call(
+        far_kernel,
         in_specs=[VM] * 6,
         out_specs=VM,
         out_shape=jax.ShapeDtypeStruct((GROUP, 3 * PICK, HD), BF),
         compiler_params=small(),
-        name="last_grads",
+        name="far_grads",
     )(*args)
 
 
@@ -283,25 +288,15 @@
     pos = ((seat // (NX * NC)) * NC + seat % NC).astype(jnp.int32).reshape(1)
     grad_rows = pick_grad(offsets, grad_out)
     picked_grad = from_next(grad_rows)
-    kv_rows = pick_kv(offsets, key_rows, value_rows)
-    kv = swap(kv_rows)
-    grad_src, picked_grad = lax.optimization_barrier((grad_out, picked_grad))
-    grad = from_next(grad_src)
-    qg_rows = pick_q(offsets, pos, queries, picked_grad, log_sums, deltas)
-    qg_rows, _ = lax.optimization_barrier((qg_rows, kv))
-    qg = swap(qg_rows)
+    grad = from_next(grad_out)
+    rows = pick_rest(offsets, pos, queries, key_rows, value_rows, log_sums, deltas)
+    own = swap(join(rows, picked_grad))
     half = GROUP // 2
-    left_kv = shift_x(kv, 1)
-    right_kv = shift_x(kv, -1)
-    left_qg = shift_x(qg, 1)
-    right_qg = shift_x(qg, -1)
-    left_far_kv = shift_x(left_kv[:half], 1)
-    right_far_kv = shift_x(right_kv[half:], -1)
-    far_kv = (left_far_kv, right_far_kv)
-    far_qg = (shift_x(left_qg[:half], 1), shift_x(right_qg[half:], -1))
+    left, right = shift_x(own, 1), shift_x(own, -1)
+    far = (shift_x(left[:half], 1), shift_x(right[half:], -1))
     local = local_grads(queries, key_rows, value_rows, grad, log_sums, deltas)
-    dq, dk, dv = wide_grads(qg, kv, left_kv, right_kv, *far_kv, left_qg, right_qg)
-    back = swap(last_grads(kv, *far_qg, dq, dk, dv))
+    dq, dk, dv = near_grads(own, left, right)
+    back = swap(far_grads(own, *far, dq, dk, dv))
     return tuple(combine(offsets, back, local))
 
 

time: 79.7 us -> 71 us (0.89)
  starting transfers between devices: 39.5 us -> 15.1 us
  blocking collectives: 0 us -> 21.6 us
  waiting for transfers between devices: 20.7 us -> 14.9 us
  Pallas kernels: 13.6 us -> 11.9 us
  local copies, waits for them, and re-layouts: 4.67 us -> 6.34 us
    all_to_all x0 -> x1, blocking collectives: none -> 21.6 us  [swap(): lax.all_to_all(value, 'seq', 0, 0, axis_index_groups=GROUPS, tiled=True)]
    all_to_all x3 -> x1, starting transfers between devices: 22 us -> 4.88 us  [swap(): lax.all_to_all(value, 'seq', 0, 0, axis_index_groups=GROUPS, tiled=True)]
    all_to_all x3 -> x1, waiting for transfers between devices: 12.4 us -> 4.03 us  [swap(): lax.all_to_all(value, 'seq', 0, 0, axis_index_groups=GROUPS, tiled=True)]
    ppermute x8 -> x4, starting transfers between devices: 11.5 us -> 6.05 us  [shift_x(): return lax.ppermute(value, 'seq', pairs)]
    ppermute x8 -> x4, waiting for transfers between devices: 6.95 us -> 10.9 us  [shift_x(): return lax.ppermute(value, 'seq', pairs)]
    ppermute x2, starting transfers between devices: 6.1 us -> 4.13 us  [from_next(): lax.ppermute(value, 'section', [((s + 1) % count, s) for s in range(count)])]
    pallas_call x4, Pallas kernels: 6.1 us -> 4.37 us  [the longest x1 1.73 us: pick_rest(): pl.pallas_call(pick_kernel, in_specs=[SM, SM] + [VM] * 5, out_specs=VM, o...]
    unnamed x24 -> x26, local copies, waits for them, and re-layouts: 4.65 us -> 6.32 us
  transfers between devices with their start and end apart: 13 -> 7, of which waited for: 7 -> 4; matrix products, arithmetic and copies ran while one was open for 0% -> 0% of each run, Pallas kernels for 12% -> 12%
where the time goes in v1:
time: 71 us; the launch traced here: 70.6 us
  blocking collectives  21.6 us (30%)
  starting transfers between devices  15.1 us (21%)
  waiting for transfers between devices  14.9 us (21%)
  Pallas kernels  11.9 us (17%)
  local copies, waits for them, and re-layouts  6.34 us (9%)
  between operations  0.73 us (1%)
    all_to_all x1, blocking collectives, swap(): lax.all_to_all(value, 'seq', 0, 0, axis_index_groups=GROUPS, tiled=True)  21.6 us
    ppermute x4, waiting for transfers between devices, shift_x(): return lax.ppermute(value, 'seq', pairs)  10.9 us
    unnamed x26, local copies, waits for them, and re-layouts  6.32 us
    ppermute x4, starting transfers between devices, shift_x(): return lax.ppermute(value, 'seq', pairs)  6.05 us
    all_to_all x1, starting transfers between devices, swap(): lax.all_to_all(value, 'seq', 0, 0, axis_index_groups=GROUPS, tiled=True)  4.88 us
    pallas_call x1, Pallas kernels, local_grads(): pl.pallas_call(local_kernel, grid=(4,), in_specs=[wide, wide, wide, wide,...  4.38 us
    ppermute x2, starting transfers between devices, from_next(): lax.ppermute(value, 'section', [((s + 1) % count, s) for s in range(count)])  4.13 us
    all_to_all x1, waiting for transfers between devices, swap(): lax.all_to_all(value, 'seq', 0, 0, axis_index_groups=GROUPS, tiled=True)  4.03 us
  transfers between devices with their start and end apart: 7, of which 4 were waited for; matrix products, arithmetic and copies ran while one was open for 0% of the time, Pallas kernels for 12%

profile of v1, /device:TPU:1, one launch (start us, length us, event | category | flops | bytes accessed | tf_op | source)
XLA Modules:
  0.0 70.6 jit_solution(12788716794288608387)
XLA Ops:
  0.6 1.0 %copy-done.5 = bf16[1,128,2048]{2,1,0:T(8,128)(2,1)S(1)} copy-done((bf16[1,128,2048]{2,1,0:T(8,128)(2,1)S(1)}, bf16[1,128,2048]{2,1,0:T(8,128)(2,1)}, u32[]{:S(2)}) %copy-start.5) | copy-done | bytes 524312
  1.7 0.7 copy-done.7
  2.3 0.9 %pick_grad.1 = bf16[16,16,128]{2,1,0:T(8,128)(2,1)S(1)} custom-call(s32[1,16]{1,0:T(1,128)S(1)} %copy-done.7, bf16[1,128,2048]{2,1,0:T(8,128)(2,1)S(1)} %copy-done.5), custom_call_target="tpu_custom_call" | custom-call | tf_op jit(solution)/shard_map/pick_grad/pallas_call | solution.py:82
  3.3 3.6 %collective-permute-start = (bf16[16,16,128]{2,1,0:T(8,128)(2,1)S(1)}, bf16[16,16,128]{2,1,0:T(8,128)(2,1)S(1)}, u32[]{:S(2)}, u32[]{:S(2)}) collective-permute-start(bf16[16,16,128]{2,1,0:T(8,128)(2,1)S(1)} %pick_grad.1), channel_id=1, source_target_pairs={{64,0},{128,64},{192,128},{0,192},{65,1},{129,65},{193,129},{1,193... | collective-permute-start | bytes 196616 | tf_op jit(solution)/shard_map/ppermute | solution.py:279
  6.9 0.7 copy-done.10
  7.6 1.0 %copy-done.1 = bf16[1,128,2048]{2,1,0:T(8,128)(2,1)S(1)} copy-done((bf16[1,128,2048]{2,1,0:T(8,128)(2,1)S(1)}, bf16[1,128,2048]{2,1,0:T(8,128)(2,1)}, u32[]{:S(2)}) %copy-start.1) | copy-done | bytes 524312
  8.6 1.0 %copy-done.3 = bf16[1,128,2048]{2,1,0:T(8,128)(2,1)S(1)} copy-done((bf16[1,128,2048]{2,1,0:T(8,128)(2,1)S(1)}, bf16[1,128,2048]{2,1,0:T(8,128)(2,1)}, u32[]{:S(2)}) %copy-start.3) | copy-done | bytes 524312
  9.7 1.7 %pick_rest.1.rows_ref = bf16[16,72,128]{2,1,0:T(8,128)(2,1)S(1)} custom-call(s32[1,16]{1,0:T(1,128)S(1)} %copy-done.8, s32[1]{0:T(128)} %bitcast.pos_ref, bf16[1,128,2048]{2,1,0:T(8,128)(2,1)S(1)} %copy-done, bf16[1,128,2048]{2,1,0:T(8,128)(2,1)S(1)} %copy-done.1, bf16[1,128,2048]{2,1,0:T(8,128)(2,1)S(1)} %copy-done.3, bf16[1,16,128]{2,1,0:T(8,128)(2,1)S(1)} %copy-done.9, ...), custom_call_target="tpu_custom_call" | custom-call | tf_op jit(solution)/shard_map/pick_rest/pallas_call | solution.py:93
  11.5 21.6 %all_to_all.10.own_ref = bf16[16,72,128]{2,1,0:T(8,128)(2,1)S(1)} all-to-all(bf16[16,72,128]{2,1,0:T(8,128)(2,1)S(1)} %join.1), channel_id=1, replica_groups={{0,1,8,9,16,17,24,25,32,33,40,41,48,49,56,57},{2,3,10,11,18,19,26,27,34..., dimensions={0} | all-to-all | bytes 589824 | tf_op jit(solution)/shard_map/all_to_all | solution.py:283
  33.1 2.5 %collective-permute-start.3 = (bf16[16,72,128]{2,1,0:T(8,128)(2,1)S(1)}, bf16[16,72,128]{2,1,0:T(8,128)(2,1)S(1)}, u32[]{:S(2)}, u32[]{:S(2)}) collective-permute-start(bf16[16,72,128]{2,1,0:T(8,128)(2,1)S(1)} %all_to_all.10.own_ref), channel_id=1, source_target_pairs={{0,6},{1,7},{2,0},{3,1},{4,2},{5,3},{6,4},{7,5},{8,14},{9,15},{10,... | collective-permute-start | bytes 884744 | tf_op jit(solution)/shard_map/ppermute | solution.py:274
  35.6 0.5 collective-permute-start.5
  36.1 6.3 %collective-permute-done.3.right_ref = bf16[16,72,128]{2,1,0:T(8,128)(2,1)S(1)} collective-permute-done((bf16[16,72,128]{2,1,0:T(8,128)(2,1)S(1)}, bf16[16,72,128]{2,1,0:T(8,128)(2,1)S(1)}, u32[]{:S(2)}, u32[]{:S(2)}) %collective-permute-start.3) | collective-permute-done | bytes 294944 | tf_op jit(solution)/shard_map/ppermute | solution.py:274
  42.4 3.5 %collective-permute-start.4 = (bf16[8,72,128]{2,1,0:T(8,128)(2,1)S(1)}, bf16[8,72,128]{2,1,0:T(8,128)(2,1)S(1)}, u32[]{:S(2)}, u32[]{:S(2)}) collective-permute-start(bf16[8,72,128]{2,1,0:T(8,128)(2,1)S(1)} %slice.9), channel_id=1, source_target_pairs={{0,6},{1,7},{2,0},{3,1},{4,2},{5,3},{6,4},{7,5},{8,14},{9,15},{10,... | collective-permute-start | bytes 442376 | tf_op jit(solution)/shard_map/ppermute | solution.py:274
  45.9 0.1 collective-permute-start.2
  46.0 1.3 %near_grads.1 = (f32[256,128]{1,0:T(8,128)S(1)}, f32[256,128]{1,0:T(8,128)S(1)}, f32[256,128]{1,0:T(8,128)S(1)}) custom-call(bf16[16,72,128]{2,1,0:T(8,128)(2,1)S(1)} %all_to_all.10.own_ref, bf16[16,72,128]{2,1,0:T(8,128)(2,1)S(1)} %collective-permute-done.1.left_ref, bf16[16,72,128]{2,1,0:T(8,128)(2,1)S(1)} %collective-permute-done.3.right_ref), custom_call_target="tpu_custom_call" | custom-call | flops 704643072 | bytes 1572864 | tf_op jit(solution)/shard_map/near_grads/pallas_call | solution.py:206
  47.2 1.4 %collective-permute-done.4.b_ref = bf16[8,72,128]{2,1,0:T(8,128)(2,1)S(1)} collective-permute-done((bf16[8,72,128]{2,1,0:T(8,128)(2,1)S(1)}, bf16[8,72,128]{2,1,0:T(8,128)(2,1)S(1)}, u32[]{:S(2)}, u32[]{:S(2)}) %collective-permute-start.4) | collective-permute-done | bytes 147488 | tf_op jit(solution)/shard_map/ppermute | solution.py:274
  48.6 3.2 %collective-permute-done.2.a_ref = bf16[8,72,128]{2,1,0:T(8,128)(2,1)S(1)} collective-permute-done((bf16[8,72,128]{2,1,0:T(8,128)(2,1)S(1)}, bf16[8,72,128]{2,1,0:T(8,128)(2,1)S(1)}, u32[]{:S(2)}, u32[]{:S(2)}) %collective-permute-start.2) | collective-permute-done | bytes 147488 | tf_op jit(solution)/shard_map/ppermute | solution.py:274
  51.9 1.4 %far_grads.1 = bf16[16,48,128]{2,1,0:T(8,128)(2,1)} custom-call(bf16[16,72,128]{2,1,0:T(8,128)(2,1)S(1)} %all_to_all.10.own_ref, bf16[8,72,128]{2,1,0:T(8,128)(2,1)S(1)} %collective-permute-done.2.a_ref, bf16[8,72,128]{2,1,0:T(8,128)(2,1)S(1)} %collective-permute-done.4.b_ref, f32[256,128]{1,0:T(8,128)S(1)} %get-tuple-element.9.dq_ref, ...), custom_call_target="tpu_custom_call" | custom-call | tf_op jit(solution)/shard_map/far_grads/pallas_call | solution.py:229
  53.2 4.9 %all-to-all-start.1 = ((bf16[16,48,128]{2,1,0:T(8,128)(2,1)}), bf16[16,48,128]{2,1,0:T(8,128)(2,1)S(1)}, u32[]{:S(2)}, u32[]{:S(2)}) async-start(bf16[16,48,128]{2,1,0:T(8,128)(2,1)} %far_grads.1), calls=%async_computation.1 | async-start | bytes 393216 | tf_op jit(solution)/shard_map/all_to_all | solution.py:283
  58.1 0.8 %copy-done.11 = bf16[1,128,2048]{2,1,0:T(8,128)(2,1)} copy-done((bf16[1,128,2048]{2,1,0:T(8,128)(2,1)}, bf16[1,128,2048]{2,1,0:T(8,128)(2,1)S(1)}, u32[]{:S(2)}) %copy-start.11) | copy-done | bytes 524312
  58.9 1.0 %copy-done.12 = bf16[1,128,2048]{2,1,0:T(8,128)(2,1)S(1)} copy-done((bf16[1,128,2048]{2,1,0:T(8,128)(2,1)S(1)}, bf16[1,128,2048]{2,1,0:T(8,128)(2,1)}, u32[]{:S(2)}) %copy-start.12) | copy-done | bytes 524312
  60.0 4.4 %local_grads.1 = (bf16[128,2048]{1,0:T(8,128)(2,1)S(1)}, bf16[128,2048]{1,0:T(8,128)(2,1)S(1)}, bf16[128,2048]{1,0:T(8,128)(2,1)S(1)}) custom-call(bf16[1,128,2048]{2,1,0:T(8,128)(2,1)S(1)} %copy-done, bf16[1,128,2048]{2,1,0:T(8,128)(2,1)S(1)} %copy-done.2, bf16[1,128,2048]{2,1,0:T(8,128)(2,1)S(1)} %copy-done.4, bf16[1,128,2048]{2,1,0:T(8,128)(2,1)S(1)} %copy-done.12, ...), custom_call_target="tpu_custom_call" | custom-call | flops 1342177280 | bytes 3670016 | tf_op jit(solution)/shard_map/local_grads/pallas_call | solution.py:141
  64.4 4.0 %all-to-all-done.1.w_ref = bf16[16,48,128]{2,1,0:T(8,128)(2,1)S(1)} async-done(((bf16[16,48,128]{2,1,0:T(8,128)(2,1)}), bf16[16,48,128]{2,1,0:T(8,128)(2,1)S(1)}, u32[]{:S(2)}, u32[]{:S(2)}) %all-to-all-start.1) | async-done | bytes 196640 | tf_op jit(solution)/shard_map/all_to_all | solution.py:283
  68.4 2.2 %combine.1 = (bf16[1,128,2048]{2,1,0:T(8,128)(2,1)}, bf16[1,128,2048]{2,1,0:T(8,128)(2,1)}, bf16[1,128,2048]{2,1,0:T(8,128)(2,1)}) custom-call(s32[1,16]{1,0:T(1,128)S(1)} %copy-done.8, bf16[16,48,128]{2,1,0:T(8,128)(2,1)S(1)} %all-to-all-done.1.w_ref, bf16[128,2048]{1,0:T(8,128)(2,1)S(1)} %get-tuple-element.12.refs_0_, ...), custom_call_target="tpu_custom_call" | custom-call | tf_op jit(solution)/shard_map/combine/pallas_call | solution.py:252
  (26 shorter events, 0.1 us)
Async XLA Ops:
  0.6 1.0 %copy-start.5 = (bf16[1,128,2048]{2,1,0:T(8,128)(2,1)S(1)}, bf16[1,128,2048]{2,1,0:T(8,128)(2,1)}, u32[]{:S(2)}) copy-start(bf16[1,128,2048]{2,1,0:T(8,128)(2,1)} %g_ref.1) | copy-start | bytes 1572868
  1.7 0.7 copy-start.7
  2.3 4.6 %copy-start = (bf16[1,128,2048]{2,1,0:T(8,128)(2,1)S(1)}, bf16[1,128,2048]{2,1,0:T(8,128)(2,1)}, u32[]{:S(2)}) copy-start(bf16[1,128,2048]{2,1,0:T(8,128)(2,1)} %q_ref.3) | copy-start | bytes 1572868
  3.3 8.2 %collective-permute-start = (bf16[16,16,128]{2,1,0:T(8,128)(2,1)S(1)}, bf16[16,16,128]{2,1,0:T(8,128)(2,1)S(1)}, u32[]{:S(2)}, u32[]{:S(2)}) collective-permute-start(bf16[16,16,128]{2,1,0:T(8,128)(2,1)S(1)} %pick_grad.1), channel_id=1, source_target_pairs={{64,0},{128,64},{192,128},{0,192},{65,1},{129,65},{193,129},{1,193... | collective-permute-start | bytes 196616 | tf_op jit(solution)/shard_map/ppermute | solution.py:279
  6.9 0.7 copy-start.10
  6.9 0.7 copy-start.9
  6.9 0.7 copy-start.8
  7.6 1.0 %copy-start.1 = (bf16[1,128,2048]{2,1,0:T(8,128)(2,1)S(1)}, bf16[1,128,2048]{2,1,0:T(8,128)(2,1)}, u32[]{:S(2)}) copy-start(bf16[1,128,2048]{2,1,0:T(8,128)(2,1)} %k_ref.3) | copy-start | bytes 1572868
  8.6 1.0 %copy-start.3 = (bf16[1,128,2048]{2,1,0:T(8,128)(2,1)S(1)}, bf16[1,128,2048]{2,1,0:T(8,128)(2,1)}, u32[]{:S(2)}) copy-start(bf16[1,128,2048]{2,1,0:T(8,128)(2,1)} %v_ref.3) | copy-start | bytes 1572868
  11.4 24.2 %copy-start.6 = (bf16[1,128,2048]{2,1,0:T(8,128)(2,1)S(1)}, bf16[1,128,2048]{2,1,0:T(8,128)(2,1)}, u32[]{:S(2)}) copy-start(bf16[1,128,2048]{2,1,0:T(8,128)(2,1)} %g_ref.1) | copy-start | bytes 1572868
  33.1 9.3 %collective-permute-start.3 = (bf16[16,72,128]{2,1,0:T(8,128)(2,1)S(1)}, bf16[16,72,128]{2,1,0:T(8,128)(2,1)S(1)}, u32[]{:S(2)}, u32[]{:S(2)}) collective-permute-start(bf16[16,72,128]{2,1,0:T(8,128)(2,1)S(1)} %all_to_all.10.own_ref), channel_id=1, source_target_pairs={{0,6},{1,7},{2,0},{3,1},{4,2},{5,3},{6,4},{7,5},{8,14},{9,15},{10,... | collective-permute-start | bytes 884744 | tf_op jit(solution)/shard_map/ppermute | solution.py:274
  35.6 10.3 %collective-permute-start.1 = (bf16[16,72,128]{2,1,0:T(8,128)(2,1)S(1)}, bf16[16,72,128]{2,1,0:T(8,128)(2,1)S(1)}, u32[]{:S(2)}, u32[]{:S(2)}) collective-permute-start(bf16[16,72,128]{2,1,0:T(8,128)(2,1)S(1)} %all_to_all.10.own_ref), channel_id=1, source_target_pairs={{0,2},{1,3},{2,4},{3,5},{4,6},{5,7},{6,0},{7,1},{8,10},{9,11},{10,... | collective-permute-start | bytes 884744 | tf_op jit(solution)/shard_map/ppermute | solution.py:274
  35.6 22.5 %collective-permute-start.5 = (bf16[1,128,2048]{2,1,0:T(8,128)(2,1)S(1)}, bf16[1,128,2048]{2,1,0:T(8,128)(2,1)S(1)}, u32[]{:S(2)}, u32[]{:S(2)}) collective-permute-start(bf16[1,128,2048]{2,1,0:T(8,128)(2,1)S(1)} %copy-done.6), channel_id=1, source_target_pairs={{64,0},{128,64},{192,128},{0,192},{65,1},{129,65},{193,129},{1,193... | collective-permute-start | bytes 1572872 | tf_op jit(solution)/shard_map/ppermute | solution.py:279
  42.4 6.3 %collective-permute-start.4 = (bf16[8,72,128]{2,1,0:T(8,128)(2,1)S(1)}, bf16[8,72,128]{2,1,0:T(8,128)(2,1)S(1)}, u32[]{:S(2)}, u32[]{:S(2)}) collective-permute-start(bf16[8,72,128]{2,1,0:T(8,128)(2,1)S(1)} %slice.9), channel_id=1, source_target_pairs={{0,6},{1,7},{2,0},{3,1},{4,2},{5,3},{6,4},{7,5},{8,14},{9,15},{10,... | collective-permute-start | bytes 442376 | tf_op jit(solution)/shard_map/ppermute | solution.py:274
  45.9 6.0 %collective-permute-start.2 = (bf16[8,72,128]{2,1,0:T(8,128)(2,1)S(1)}, bf16[8,72,128]{2,1,0:T(8,128)(2,1)S(1)}, u32[]{:S(2)}, u32[]{:S(2)}) collective-permute-start(bf16[8,72,128]{2,1,0:T(8,128)(2,1)S(1)} %slice.8), channel_id=1, source_target_pairs={{0,2},{1,3},{2,4},{3,5},{4,6},{5,7},{6,0},{7,1},{8,10},{9,11},{10,... | collective-permute-start | bytes 442376 | tf_op jit(solution)/shard_map/ppermute | solution.py:274
  51.9 7.1 %copy-start.2 = (bf16[1,128,2048]{2,1,0:T(8,128)(2,1)S(1)}, bf16[1,128,2048]{2,1,0:T(8,128)(2,1)}, u32[]{:S(2)}) copy-start(bf16[1,128,2048]{2,1,0:T(8,128)(2,1)} %k_ref.3) | copy-start | bytes 1572868
  51.9 7.1 %copy-start.4 = (bf16[1,128,2048]{2,1,0:T(8,128)(2,1)S(1)}, bf16[1,128,2048]{2,1,0:T(8,128)(2,1)}, u32[]{:S(2)}) copy-start(bf16[1,128,2048]{2,1,0:T(8,128)(2,1)} %v_ref.3) | copy-start | bytes 1572868
  53.2 15.2 %all-to-all-start.1 = ((bf16[16,48,128]{2,1,0:T(8,128)(2,1)}), bf16[16,48,128]{2,1,0:T(8,128)(2,1)S(1)}, u32[]{:S(2)}, u32[]{:S(2)}) async-start(bf16[16,48,128]{2,1,0:T(8,128)(2,1)} %far_grads.1), calls=%async_computation.1 | async-start | bytes 393216 | tf_op jit(solution)/shard_map/all_to_all | solution.py:283
  58.1 0.8 %copy-start.11 = (bf16[1,128,2048]{2,1,0:T(8,128)(2,1)}, bf16[1,128,2048]{2,1,0:T(8,128)(2,1)S(1)}, u32[]{:S(2)}) copy-start(bf16[1,128,2048]{2,1,0:T(8,128)(2,1)S(1)} %collective-permute-done.5.g_ref) | copy-start | bytes 1572868
  58.9 1.0 %copy-start.12 = (bf16[1,128,2048]{2,1,0:T(8,128)(2,1)S(1)}, bf16[1,128,2048]{2,1,0:T(8,128)(2,1)}, u32[]{:S(2)}) copy-start(bf16[1,128,2048]{2,1,0:T(8,128)(2,1)} %copy-done.11) | copy-start | bytes 1572868

commit v2 on v1

--- a/solution.py
+++ b/solution.py
@@ -13,6 +13,7 @@
 TOK = 128
 NZ, NX, NC = 8, 4, 2
 ROWS = 72
+MAIN = 56
 GROUP = NZ * NC
 SCALE = HD ** (-0.5)
 BF = jnp.bfloat16
@@ -44,72 +45,66 @@
     return pltpu.CompilerParams(vmem_limit_bytes=mib << 20)
 
 
-def pick_grad_kernel(off_ref, g_ref, o_ref):
-    for h in range(HEADS):
-        o_ref[h] = pick(g_ref[0, :, h * HD:(h + 1) * HD], off_ref[0, h])
-
-
-def pick_kernel(off_ref, pos_ref, q_ref, k_ref, v_ref, l_ref, d_ref, o_ref):
+def pick_kernel(pos_ref, off_hbm, l_hbm, d_hbm, q_hbm, k_hbm, v_hbm, g_hbm, o_ref, off_ref, l_ref, d_ref, x_ref, sems):
+    loads = [
+        pltpu.make_async_copy(src, dst, sems.at[i])
+        for i, (src, dst) in enumerate(
+            (
+                (off_hbm, off_ref),
+                (q_hbm.at[0], x_ref.at[0]),
+                (k_hbm.at[0], x_ref.at[1]),
+                (v_hbm.at[0], x_ref.at[2]),
+                (g_hbm.at[0], x_ref.at[3]),
+                (l_hbm.at[0], l_ref),
+                (d_hbm.at[0], d_ref),
+            )
+        )
+    ]
+    for load in loads:
+        load.start()
     n = pos_ref[0]
+    src = lax.broadcasted_iota(jnp.int32, (TOK, TOK), 0)
+    dst = lax.broadcasted_iota(jnp.int32, (TOK, TOK), 1)
+    place = jnp.where(dst == (n % 8) * PICK + src // RATE, 1.0, 0.0).astype(BF)
+    loads[0].wait()
+    for part, first in ((0, 0), (1, 16), (2, 32), (3, MAIN)):
+        loads[1 + part].wait()
+        for h in range(HEADS):
+            o_ref[h, first:first + 16] = pick(x_ref[part, :, h * HD:(h + 1) * HD], off_ref[0, h])
+    loads[5].wait()
+    loads[6].wait()
     head = lax.broadcasted_iota(jnp.int32, (HEADS, TOK), 0)
     lane = lax.broadcasted_iota(jnp.int32, (HEADS, TOK), 1)
     off = jnp.zeros((HEADS, TOK), jnp.int32)
     for h in range(HEADS):
         off = jnp.where(head == h, off_ref[0, h], off)
     hit = (lane % RATE) == off
-    src = lax.broadcasted_iota(jnp.int32, (TOK, TOK), 0)
-    dst = lax.broadcasted_iota(jnp.int32, (TOK, TOK), 1)
-    place = jnp.where(dst == (n % 8) * PICK + src // RATE, 1.0, 0.0).astype(BF)
-    lses = dot(jnp.where(hit, l_ref[0].astype(F32), 0.0).astype(BF), place)
-    dlts = dot(jnp.where(hit, d_ref[0].astype(F32), 0.0).astype(BF), place)
+    lses = dot(jnp.where(hit, l_ref[...].astype(F32), 0.0).astype(BF), place)
+    dlts = dot(jnp.where(hit, d_ref[...].astype(F32), 0.0).astype(BF), place)
     row = lax.broadcasted_iota(jnp.int32, (8, HD), 0)
     for h in range(HEADS):
-        cols = slice(h * HD, (h + 1) * HD)
-        o_ref[h, 0:16] = pick(q_ref[0, :, cols], off_ref[0, h])
-        o_ref[h, 16:32] = pick(k_ref[0, :, cols], off_ref[0, h])
-        o_ref[h, 32:48] = pick(v_ref[0, :, cols], off_ref[0, h])
         lse = jnp.broadcast_to(lses[h:h + 1], (8, HD))
         dlt = jnp.broadcast_to(dlts[h:h + 1], (8, HD))
         stats = jnp.where(row == n // 8, lse, jnp.where(row == 2 + n // 8, dlt, 0.0))
-        o_ref[h, 64:72] = stats.astype(BF)
-
-
-def join_kernel(rows_ref, g_ref, o_ref):
-    o_ref[:, 48:64, :] = g_ref[...]
-
-
-def pick_grad(offsets, grad):
-    return pl.pallas_call(
-        pick_grad_kernel,
-        in_specs=[SM, VM],
-        out_specs=VM,
-        out_shape=jax.ShapeDtypeStruct((HEADS, PICK, HD), BF),
-        compiler_params=small(),
-        name="pick_grad",
-    )(offsets, grad)
-
-
-def pick_rest(offsets, pos, query, key, value, lse, delta):
+        o_ref[h, 48:MAIN] = stats.astype(BF)
+
+
+def pick_all(pos, offsets, lse, delta, query, key, value, grad):
+    raw = pl.BlockSpec(memory_space=pltpu.HBM)
     return pl.pallas_call(
         pick_kernel,
-        in_specs=[SM, SM] + [VM] * 5,
+        in_specs=[SM] + [raw] * 7,
         out_specs=VM,
         out_shape=jax.ShapeDtypeStruct((HEADS, ROWS, HD), BF),
-        compiler_params=small(),
-        name="pick_rest",
-    )(offsets, pos, query, key, value, lse, delta)
-
-
-def join(rows, grad):
-    return pl.pallas_call(
-        join_kernel,
-        in_specs=[VM, VM],
-        out_specs=VM,
-        out_shape=jax.ShapeDtypeStruct((HEADS, ROWS, HD), BF),
-        input_output_aliases={0: 0},
-        compiler_params=small(),
-        name="join",
-    )(rows, grad)
+        scratch_shapes=[
+            pltpu.SMEM((1, HEADS), jnp.int32),
+            pltpu.VMEM((HEADS, TOK), BF),
+            pltpu.VMEM((HEADS, TOK), BF),
+            pltpu.VMEM((4, TOK, HEADS * HD), BF),
+            pltpu.SemaphoreType.DMA((7,)),
+        ],
+        name="pick_all",
+    )(pos, offsets, lse, delta, query, key, value, grad)
 
 
 def local_kernel(q_ref, k_ref, v_ref, g_ref, l_ref, d_ref, dq_ref, dk_ref, dv_ref, st_ref):
@@ -156,12 +151,8 @@
     return ref[:, part * PICK:(part + 1) * PICK, :].reshape(count * PICK, HD)
 
 
-def both_halves(a, b, part):
-    return jnp.concatenate([rows_of(a, part), rows_of(b, part)], axis=0)
-
-
 def stats_of(ref):
-    return jnp.sum(ref[:, 64:72, :].astype(F32), axis=0)
+    return jnp.sum(ref[:, 48:MAIN, :].astype(F32), axis=0)
 
 
 def query_side(q, g, k, v, lse, dlt):
@@ -185,14 +176,18 @@
     return lse, dlt
 
 
-def near_kernel(own_ref, left_ref, right_ref, dq_ref, dk_ref, dv_ref):
-    q, k, v, g = (rows_of(own_ref, part) for part in range(4))
+def block_of(ref, g_ref):
+    return rows_of(ref, 0), rows_of(ref, 1), rows_of(ref, 2), g_ref[...].reshape(GROUP * PICK, HD)
+
+
+def near_kernel(own_ref, og_ref, left_ref, lg_ref, right_ref, rg_ref, dq_ref, dk_ref, dv_ref):
+    q, k, v, g = block_of(own_ref, og_ref)
     stats = stats_of(own_ref)
     lse, dlt = columns(stats)
     dq = query_side(q, g, k, v, lse, dlt)
     dk, dv = key_side(k, v, q, g, stats)
-    for ref in (left_ref, right_ref):
-        qx, kx, vx, gx = (rows_of(ref, part) for part in range(4))
+    for ref, g_ref in ((left_ref, lg_ref), (right_ref, rg_ref)):
+        qx, kx, vx, gx = block_of(ref, g_ref)
         dq = dq + query_side(q, g, kx, vx, lse, dlt)
         more_k, more_v = key_side(k, v, qx, gx, stats_of(ref))
         dk, dv = dk + more_k, dv + more_v
@@ -205,7 +200,7 @@
     part = jax.ShapeDtypeStruct((GROUP * PICK, HD), F32)
     return pl.pallas_call(
         near_kernel,
-        in_specs=[VM] * 3,
+        in_specs=[VM] * 6,
         out_specs=[VM] * 3,
         out_shape=[part] * 3,
         compiler_params=small(),
@@ -214,12 +209,12 @@
     )(*args)
 
 
-def far_kernel(own_ref, a_ref, b_ref, dq_ref, dk_ref, dv_ref, o_ref):
-    q, k, v, g = (rows_of(own_ref, part) for part in range(4))
+def far_kernel(own_ref, og_ref, far_ref, fg_ref, dq_ref, dk_ref, dv_ref, o_ref):
+    q, k, v, g = block_of(own_ref, og_ref)
     lse, dlt = columns(stats_of(own_ref))
-    qx, kx, vx, gx = (both_halves(a_ref, b_ref, part) for part in range(4))
+    qx, kx, vx, gx = block_of(far_ref, fg_ref)
     dq = query_side(q, g, kx, vx, lse, dlt)
-    dk, dv = key_side(k, v, qx, gx, stats_of(a_ref) + stats_of(b_ref))
+    dk, dv = key_side(k, v, qx, gx, stats_of(far_ref))
     o_ref[:, 0:16, :] = ((dq_ref[...] + dq) * SCALE).astype(BF).reshape(GROUP, PICK, HD)
     o_ref[:, 16:32, :] = ((dk_ref[...] + dk) * SCALE).astype(BF).reshape(GROUP, PICK, HD)
     o_ref[:, 32:48, :] = (dv_ref[...] + dv).astype(BF).reshape(GROUP, PICK, HD)
@@ -228,7 +223,7 @@
 def far_grads(*args):
     return pl.pallas_call(
         far_kernel,
-        in_specs=[VM] * 6,
+        in_specs=[VM] * 7,
         out_specs=VM,
         out_shape=jax.ShapeDtypeStruct((GROUP, 3 * PICK, HD), BF),
         compiler_params=small(),
@@ -279,6 +274,15 @@
     return lax.ppermute(value, "section", [((s + 1) % count, s) for s in range(count)])
 
 
+def from_next_x(value, steps):
+    count, seats = lax.axis_size("section"), lax.axis_size("seq")
+    pairs = [
+        (((s + 1) % count) * seats + place_of(z, x, c), s * seats + place_of(z, (x + steps) % NX, c))
+        for s in range(count) for z in range(NZ) for x in range(NX) for c in range(NC)
+    ]
+    return lax.ppermute(value, ("section", "seq"), pairs)
+
+
 def swap(value):
     return lax.all_to_all(value, "seq", 0, 0, axis_index_groups=GROUPS, tiled=True)
 
@@ -286,17 +290,20 @@
 def body(queries, key_rows, value_rows, grad_out, log_sums, deltas, offsets):
     seat = lax.axis_index("seq")
     pos = ((seat // (NX * NC)) * NC + seat % NC).astype(jnp.int32).reshape(1)
-    grad_rows = pick_grad(offsets, grad_out)
-    picked_grad = from_next(grad_rows)
+    picked = pick_all(pos, offsets, log_sums, deltas, queries, key_rows, value_rows, grad_out)
+    mine = swap(picked)
+    own, grad_row = mine[:, :MAIN], mine[:, MAIN:]
+    far = shift_x(own, 2)
+    left = shift_x(own, 1)
+    right = shift_x(own, -1)
+    far_g = from_next_x(grad_row, 2)
+    left_g = from_next_x(grad_row, 1)
+    right_g = from_next_x(grad_row, -1)
+    own_g = from_next_x(grad_row, 0)
     grad = from_next(grad_out)
-    rows = pick_rest(offsets, pos, queries, key_rows, value_rows, log_sums, deltas)
-    own = swap(join(rows, picked_grad))
-    half = GROUP // 2
-    left, right = shift_x(own, 1), shift_x(own, -1)
-    far = (shift_x(left[:half], 1), shift_x(right[half:], -1))
     local = local_grads(queries, key_rows, value_rows, grad, log_sums, deltas)
-    dq, dk, dv = near_grads(own, left, right)
-    back = swap(far_grads(own, *far, dq, dk, dv))
+    part = near_grads(own, own_g, left, left_g, right, right_g)
+    back = swap(far_grads(own, own_g, far, far_g, *part))
     return tuple(combine(offsets, back, local))
 
 

time: 71 us -> 79.6 us (1.12); the launches traced: 70.6 us -> 78.3 us
  starting transfers between devices: 15.1 us -> 20.4 us
  waiting for transfers between devices: 14.9 us -> 19.5 us
  local copies, waits for them, and re-layouts: 6.34 us -> 2.53 us
  Pallas kernels: 11.9 us -> 12.7 us
  blocking collectives: 21.6 us -> 22.4 us
    ppermute x0 -> x4, waiting for transfers between devices: none -> 15.5 us  [from_next_x(): return lax.ppermute(value, ('section', 'seq'), pairs)]
    ppermute x4 -> x3, waiting for transfers between devices: 10.9 us -> 0.01 us  [shift_x(): return lax.ppermute(value, 'seq', pairs)]
    ppermute x0 -> x4, starting transfers between devices: none -> 8.03 us  [from_next_x(): return lax.ppermute(value, ('section', 'seq'), pairs)]
    unnamed x26 -> x18, local copies, waits for them, and re-layouts: 6.32 us -> 2.51 us
    ppermute x4 -> x3, starting transfers between devices: 6.05 us -> 2.56 us  [shift_x(): return lax.ppermute(value, 'seq', pairs)]
    all_to_all x1, starting transfers between devices: 4.88 us -> 7.08 us  [swap(): lax.all_to_all(value, 'seq', 0, 0, axis_index_groups=GROUPS, tiled=True)]
    ppermute x2 -> x1, starting transfers between devices: 4.13 us -> 2.73 us  [from_next(): lax.ppermute(value, 'section', [((s + 1) % count, s) for s in range(count)])]
    pallas_call x5 -> x3, Pallas kernels: 5.29 us -> 6.13 us  [the longest x1 3.5 us: pick_all(): pl.pallas_call(pick_kernel, in_specs=[SM] + [raw] * 7, out_specs=VM, out_...]
  transfers between devices with their start and end apart: 7 -> 9, of which waited for: 4 -> 5; matrix products, arithmetic and copies ran while one was open for 0% -> 0% of each run, Pallas kernels for 12% -> 9%
where the time goes in v2:
time: 79.6 us; the launch traced here: 78.3 us
  blocking collectives  22.4 us (28%)
  starting transfers between devices  20.4 us (26%)
  waiting for transfers between devices  19.5 us (24%)
  Pallas kernels  12.7 us (16%)
  local copies, waits for them, and re-layouts  2.53 us (3%)
    all_to_all x1, blocking collectives, swap(): lax.all_to_all(value, 'seq', 0, 0, axis_index_groups=GROUPS, tiled=True)  22.4 us
    ppermute x4, waiting for transfers between devices, from_next_x(): return lax.ppermute(value, ('section', 'seq'), pairs)  15.5 us
    ppermute x4, starting transfers between devices, from_next_x(): return lax.ppermute(value, ('section', 'seq'), pairs)  8.03 us
    all_to_all x1, starting transfers between devices, swap(): lax.all_to_all(value, 'seq', 0, 0, axis_index_groups=GROUPS, tiled=True)  7.08 us
    pallas_call x1, Pallas kernels, local_grads(): pl.pallas_call(local_kernel, grid=(4,), in_specs=[wide, wide, wide, wide,...  4.38 us
    all_to_all x1, waiting for transfers between devices, swap(): lax.all_to_all(value, 'seq', 0, 0, axis_index_groups=GROUPS, tiled=True)  4.01 us
    pallas_call x1, Pallas kernels, pick_all(): pl.pallas_call(pick_kernel, in_specs=[SM] + [raw] * 7, out_specs=VM, out_...  3.5 us
    ppermute x1, starting transfers between devices, from_next(): lax.ppermute(value, 'section', [((s + 1) % count, s) for s in range(count)])  2.73 us
  transfers between devices with their start and end apart: 9, of which 5 were waited for; matrix products, arithmetic and copies ran while one was open for 0% of the time, Pallas kernels for 9%

profile of v2, /device:TPU:1, one launch (start us, length us, event | category | flops | bytes accessed | tf_op | source)
XLA Modules:
  0.0 78.3 jit_solution(15791725574252342326)
XLA Ops:
  0.7 3.5 %pick_all.1 = bf16[16,72,128]{2,1,0:T(8,128)(2,1)} custom-call(s32[1]{0:T(128)} %bitcast.pos_ref, s32[1,16]{1,0:T(1,128)} %off_ref.1, bf16[1,16,128]{2,1,0:T(8,128)(2,1)} %l_ref.1, bf16[1,16,128]{2,1,0:T(8,128)(2,1)} %d_ref.1, bf16[1,128,2048]{2,1,0:T(8,128)(2,1)} %q_ref.1, bf16[1,128,2048]{2,1,0:T(8,128)(2,1)} %k_ref.1, bf16[1,128,2048]{2,1,0:T(8,128)(2,1)} %v_ref.1, ...), custom_call_target="tpu_custom_call" | custom-call | tf_op jit(solution)/shard_map/pick_all/pallas_call | solution.py:94
  4.2 0.0 copy-start.8
  4.2 22.4 %all_to_all.10 = bf16[16,72,128]{2,1,0:T(8,128)(2,1)S(1)} all-to-all(bf16[16,72,128]{2,1,0:T(8,128)(2,1)} %pick_all.1), channel_id=1, replica_groups={{0,1,8,9,16,17,24,25,32,33,40,41,48,49,56,57},{2,3,10,11,18,19,26,27,34..., dimensions={0} | all-to-all | bytes 589824 | tf_op jit(solution)/shard_map/all_to_all | solution.py:287
  26.6 2.6 %collective-permute-start.5 = (bf16[16,56,128]{2,1,0:T(8,128)(2,1)S(1)}, bf16[16,56,128]{2,1,0:T(8,128)(2,1)S(1)}, u32[]{:S(2)}, u32[]{:S(2)}) collective-permute-start(bf16[16,56,128]{2,1,0:T(8,128)(2,1)S(1)} %slice.8.own_ref), channel_id=1, source_target_pairs={{0,6},{1,7},{2,0},{3,1},{4,2},{5,3},{6,4},{7,5},{8,14},{9,15},{10,... | collective-permute-start | bytes 688136 | tf_op jit(solution)/shard_map/ppermute | solution.py:269
  29.1 2.7 %collective-permute-start.7 = (bf16[1,128,2048]{2,1,0:T(8,128)(2,1)S(1)}, bf16[1,128,2048]{2,1,0:T(8,128)(2,1)S(1)}, u32[]{:S(2)}, u32[]{:S(2)}) collective-permute-start(bf16[1,128,2048]{2,1,0:T(8,128)(2,1)S(1)} %copy-done.8), channel_id=1, source_target_pairs={{64,0},{128,64},{192,128},{0,192},{65,1},{129,65},{193,129},{1,193... | collective-permute-start | bytes 1572872 | tf_op jit(solution)/shard_map/ppermute | solution.py:274
  31.9 2.9 %collective-permute-start.6 = (bf16[16,16,128]{2,1,0:T(8,128)(2,1)S(1)}, bf16[16,16,128]{2,1,0:T(8,128)(2,1)S(1)}, u32[]{:S(2)}, u32[]{:S(2)}) collective-permute-start(bf16[16,16,128]{2,1,0:T(8,128)(2,1)S(1)} %slice.9), channel_id=1, source_target_pairs={{64,6},{65,7},{66,0},{67,1},{68,2},{69,3},{70,4},{71,5},{72,14},{7... | collective-permute-start | bytes 196616 | tf_op jit(solution)/shard_map/ppermute | solution.py:283
  34.7 6.4 %collective-permute-done.6.rg_ref = bf16[16,16,128]{2,1,0:T(8,128)(2,1)S(1)} collective-permute-done((bf16[16,16,128]{2,1,0:T(8,128)(2,1)S(1)}, bf16[16,16,128]{2,1,0:T(8,128)(2,1)S(1)}, u32[]{:S(2)}, u32[]{:S(2)}) %collective-permute-start.6) | collective-permute-done | bytes 65568 | tf_op jit(solution)/shard_map/ppermute | solution.py:283
  41.1 6.8 %collective-permute-done.4.lg_ref = bf16[16,16,128]{2,1,0:T(8,128)(2,1)S(1)} collective-permute-done((bf16[16,16,128]{2,1,0:T(8,128)(2,1)S(1)}, bf16[16,16,128]{2,1,0:T(8,128)(2,1)S(1)}, u32[]{:S(2)}, u32[]{:S(2)}) %collective-permute-start.4) | collective-permute-done | bytes 65568 | tf_op jit(solution)/shard_map/ppermute | solution.py:283
  47.9 1.9 %collective-permute-start = (bf16[16,16,128]{2,1,0:T(8,128)(2,1)S(1)}, bf16[16,16,128]{2,1,0:T(8,128)(2,1)S(1)}, u32[]{:S(2)}, u32[]{:S(2)}) collective-permute-start(bf16[16,16,128]{2,1,0:T(8,128)(2,1)S(1)} %slice.9), channel_id=1, source_target_pairs={{64,0},{65,1},{66,2},{67,3},{68,4},{69,5},{70,6},{71,7},{72,8},{73... | collective-permute-start | bytes 196616 | tf_op jit(solution)/shard_map/ppermute | solution.py:283
  49.9 1.3 %collective-permute-done.og_ref = bf16[16,16,128]{2,1,0:T(8,128)(2,1)S(1)} collective-permute-done((bf16[16,16,128]{2,1,0:T(8,128)(2,1)S(1)}, bf16[16,16,128]{2,1,0:T(8,128)(2,1)S(1)}, u32[]{:S(2)}, u32[]{:S(2)}) %collective-permute-start) | collective-permute-done | bytes 65568 | tf_op jit(solution)/shard_map/ppermute | solution.py:283
  51.2 3.2 %collective-permute-start.2 = (bf16[16,16,128]{2,1,0:T(8,128)(2,1)S(1)}, bf16[16,16,128]{2,1,0:T(8,128)(2,1)S(1)}, u32[]{:S(2)}, u32[]{:S(2)}) collective-permute-start(bf16[16,16,128]{2,1,0:T(8,128)(2,1)S(1)} %slice.9), channel_id=1, source_target_pairs={{64,4},{65,5},{66,6},{67,7},{68,0},{69,1},{70,2},{71,3},{72,12},{7... | collective-permute-start | bytes 196616 | tf_op jit(solution)/shard_map/ppermute | solution.py:283
  54.5 0.0 copy-start.4
  54.5 1.3 %near_grads.1 = (f32[256,128]{1,0:T(8,128)S(1)}, f32[256,128]{1,0:T(8,128)S(1)}, f32[256,128]{1,0:T(8,128)S(1)}) custom-call(bf16[16,56,128]{2,1,0:T(8,128)(2,1)S(1)} %slice.8.own_ref, bf16[16,16,128]{2,1,0:T(8,128)(2,1)S(1)} %collective-permute-done.og_ref, bf16[16,56,128]{2,1,0:T(8,128)(2,1)S(1)} %collective-permute-done.3.left_ref, ...), custom_call_target="tpu_custom_call" | custom-call | flops 704643072 | bytes 1572864 | tf_op jit(solution)/shard_map/near_grads/pallas_call | solution.py:201
  55.7 1.0 %collective-permute-done.2.fg_ref = bf16[16,16,128]{2,1,0:T(8,128)(2,1)S(1)} collective-permute-done((bf16[16,16,128]{2,1,0:T(8,128)(2,1)S(1)}, bf16[16,16,128]{2,1,0:T(8,128)(2,1)S(1)}, u32[]{:S(2)}, u32[]{:S(2)}) %collective-permute-start.2) | collective-permute-done | bytes 65568 | tf_op jit(solution)/shard_map/ppermute | solution.py:283
  56.7 1.4 %far_grads.1 = bf16[16,48,128]{2,1,0:T(8,128)(2,1)} custom-call(bf16[16,56,128]{2,1,0:T(8,128)(2,1)S(1)} %slice.8.own_ref, bf16[16,16,128]{2,1,0:T(8,128)(2,1)S(1)} %collective-permute-done.og_ref, bf16[16,56,128]{2,1,0:T(8,128)(2,1)S(1)} %collective-permute-done.1.far_ref, bf16[16,16,128]{2,1,0:T(8,128)(2,1)S(1)} %collective-permute-done.2.fg_ref, ...), custom_call_target="tpu_custom_call" | custom-call | tf_op jit(solution)/shard_map/far_grads/pallas_call | solution.py:224
  58.1 7.1 %all-to-all-start.1 = ((bf16[16,48,128]{2,1,0:T(8,128)(2,1)}), bf16[16,48,128]{2,1,0:T(8,128)(2,1)S(1)}, u32[]{:S(2)}, u32[]{:S(2)}) async-start(bf16[16,48,128]{2,1,0:T(8,128)(2,1)} %far_grads.1), calls=%async_computation.1 | async-start | bytes 393216 | tf_op jit(solution)/shard_map/all_to_all | solution.py:287
  65.2 0.0 copy-start.6
  65.2 0.8 %copy-done.6 = bf16[1,128,2048]{2,1,0:T(8,128)(2,1)} copy-done((bf16[1,128,2048]{2,1,0:T(8,128)(2,1)}, bf16[1,128,2048]{2,1,0:T(8,128)(2,1)S(1)}, u32[]{:S(2)}) %copy-start.6) | copy-done | bytes 524312
  66.0 0.0 copy-start.7
  66.0 1.0 %copy-done.7 = bf16[1,128,2048]{2,1,0:T(8,128)(2,1)S(1)} copy-done((bf16[1,128,2048]{2,1,0:T(8,128)(2,1)S(1)}, bf16[1,128,2048]{2,1,0:T(8,128)(2,1)}, u32[]{:S(2)}) %copy-start.7) | copy-done | bytes 524312
  67.1 4.4 %local_grads.1 = (bf16[128,2048]{1,0:T(8,128)(2,1)S(1)}, bf16[128,2048]{1,0:T(8,128)(2,1)S(1)}, bf16[128,2048]{1,0:T(8,128)(2,1)S(1)}) custom-call(bf16[1,128,2048]{2,1,0:T(8,128)(2,1)S(1)} %copy-done, bf16[1,128,2048]{2,1,0:T(8,128)(2,1)S(1)} %copy-done.1, bf16[1,128,2048]{2,1,0:T(8,128)(2,1)S(1)} %copy-done.2, bf16[1,128,2048]{2,1,0:T(8,128)(2,1)S(1)} %copy-done.7, ...), custom_call_target="tpu_custom_call" | custom-call | flops 1342177280 | bytes 3670016 | tf_op jit(solution)/shard_map/local_grads/pallas_call | solution.py:136
  71.4 4.0 %all-to-all-done.1.w_ref = bf16[16,48,128]{2,1,0:T(8,128)(2,1)S(1)} async-done(((bf16[16,48,128]{2,1,0:T(8,128)(2,1)}), bf16[16,48,128]{2,1,0:T(8,128)(2,1)S(1)}, u32[]{:S(2)}, u32[]{:S(2)}) %all-to-all-start.1) | async-done | bytes 196640 | tf_op jit(solution)/shard_map/all_to_all | solution.py:287
  75.5 0.7 copy-done.5
  76.1 2.2 %combine.1 = (bf16[1,128,2048]{2,1,0:T(8,128)(2,1)}, bf16[1,128,2048]{2,1,0:T(8,128)(2,1)}, bf16[1,128,2048]{2,1,0:T(8,128)(2,1)}) custom-call(s32[1,16]{1,0:T(1,128)S(1)} %copy-done.5, bf16[16,48,128]{2,1,0:T(8,128)(2,1)S(1)} %all-to-all-done.1.w_ref, bf16[128,2048]{1,0:T(8,128)(2,1)S(1)} %get-tuple-element.12.refs_0_, ...), custom_call_target="tpu_custom_call" | custom-call | tf_op jit(solution)/shard_map/combine/pallas_call | solution.py:247
  (20 shorter events, 0.1 us)
Async XLA Ops:
  4.2 25.0 %copy-start.8 = (bf16[1,128,2048]{2,1,0:T(8,128)(2,1)S(1)}, bf16[1,128,2048]{2,1,0:T(8,128)(2,1)}, u32[]{:S(2)}) copy-start(bf16[1,128,2048]{2,1,0:T(8,128)(2,1)} %g_hbm.1) | copy-start | bytes 1572868
  26.6 27.9 %collective-permute-start.5 = (bf16[16,56,128]{2,1,0:T(8,128)(2,1)S(1)}, bf16[16,56,128]{2,1,0:T(8,128)(2,1)S(1)}, u32[]{:S(2)}, u32[]{:S(2)}) collective-permute-start(bf16[16,56,128]{2,1,0:T(8,128)(2,1)S(1)} %slice.8.own_ref), channel_id=1, source_target_pairs={{0,6},{1,7},{2,0},{3,1},{4,2},{5,3},{6,4},{7,5},{8,14},{9,15},{10,... | collective-permute-start | bytes 688136 | tf_op jit(solution)/shard_map/ppermute | solution.py:269
  29.1 25.3 %collective-permute-start.3 = (bf16[16,56,128]{2,1,0:T(8,128)(2,1)S(1)}, bf16[16,56,128]{2,1,0:T(8,128)(2,1)S(1)}, u32[]{:S(2)}, u32[]{:S(2)}) collective-permute-start(bf16[16,56,128]{2,1,0:T(8,128)(2,1)S(1)} %slice.8.own_ref), channel_id=1, source_target_pairs={{0,2},{1,3},{2,4},{3,5},{4,6},{5,7},{6,0},{7,1},{8,10},{9,11},{10,... | collective-permute-start | bytes 688136 | tf_op jit(solution)/shard_map/ppermute | solution.py:269
  29.1 36.0 %collective-permute-start.7 = (bf16[1,128,2048]{2,1,0:T(8,128)(2,1)S(1)}, bf16[1,128,2048]{2,1,0:T(8,128)(2,1)S(1)}, u32[]{:S(2)}, u32[]{:S(2)}) collective-permute-start(bf16[1,128,2048]{2,1,0:T(8,128)(2,1)S(1)} %copy-done.8), channel_id=1, source_target_pairs={{64,0},{128,64},{192,128},{0,192},{65,1},{129,65},{193,129},{1,193... | collective-permute-start | bytes 1572872 | tf_op jit(solution)/shard_map/ppermute | solution.py:274
  31.9 9.2 %collective-permute-start.6 = (bf16[16,16,128]{2,1,0:T(8,128)(2,1)S(1)}, bf16[16,16,128]{2,1,0:T(8,128)(2,1)S(1)}, u32[]{:S(2)}, u32[]{:S(2)}) collective-permute-start(bf16[16,16,128]{2,1,0:T(8,128)(2,1)S(1)} %slice.9), channel_id=1, source_target_pairs={{64,6},{65,7},{66,0},{67,1},{68,2},{69,3},{70,4},{71,5},{72,14},{7... | collective-permute-start | bytes 196616 | tf_op jit(solution)/shard_map/ppermute | solution.py:283
  34.7 22.0 %collective-permute-start.1 = (bf16[16,56,128]{2,1,0:T(8,128)(2,1)S(1)}, bf16[16,56,128]{2,1,0:T(8,128)(2,1)S(1)}, u32[]{:S(2)}, u32[]{:S(2)}) collective-permute-start(bf16[16,56,128]{2,1,0:T(8,128)(2,1)S(1)} %slice.8.own_ref), channel_id=1, source_target_pairs={{0,4},{1,5},{2,6},{3,7},{4,0},{5,1},{6,2},{7,3},{8,12},{9,13},{10,... | collective-permute-start | bytes 688136 | tf_op jit(solution)/shard_map/ppermute | solution.py:269
  41.1 6.8 %collective-permute-start.4 = (bf16[16,16,128]{2,1,0:T(8,128)(2,1)S(1)}, bf16[16,16,128]{2,1,0:T(8,128)(2,1)S(1)}, u32[]{:S(2)}, u32[]{:S(2)}) collective-permute-start(bf16[16,16,128]{2,1,0:T(8,128)(2,1)S(1)} %slice.9), channel_id=1, source_target_pairs={{64,2},{65,3},{66,4},{67,5},{68,6},{69,7},{70,0},{71,1},{72,10},{7... | collective-permute-start | bytes 196616 | tf_op jit(solution)/shard_map/ppermute | solution.py:283
  47.9 3.3 %collective-permute-start = (bf16[16,16,128]{2,1,0:T(8,128)(2,1)S(1)}, bf16[16,16,128]{2,1,0:T(8,128)(2,1)S(1)}, u32[]{:S(2)}, u32[]{:S(2)}) collective-permute-start(bf16[16,16,128]{2,1,0:T(8,128)(2,1)S(1)} %slice.9), channel_id=1, source_target_pairs={{64,0},{65,1},{66,2},{67,3},{68,4},{69,5},{70,6},{71,7},{72,8},{73... | collective-permute-start | bytes 196616 | tf_op jit(solution)/shard_map/ppermute | solution.py:283
  51.2 5.5 %collective-permute-start.2 = (bf16[16,16,128]{2,1,0:T(8,128)(2,1)S(1)}, bf16[16,16,128]{2,1,0:T(8,128)(2,1)S(1)}, u32[]{:S(2)}, u32[]{:S(2)}) collective-permute-start(bf16[16,16,128]{2,1,0:T(8,128)(2,1)S(1)} %slice.9), channel_id=1, source_target_pairs={{64,4},{65,5},{66,6},{67,7},{68,0},{69,1},{70,2},{71,3},{72,12},{7... | collective-permute-start | bytes 196616 | tf_op jit(solution)/shard_map/ppermute | solution.py:283
  54.5 11.5 %copy-start.3 = (bf16[1,16,128]{2,1,0:T(8,128)(2,1)S(1)}, bf16[1,16,128]{2,1,0:T(8,128)(2,1)}, u32[]{:S(2)}) copy-start(bf16[1,16,128]{2,1,0:T(8,128)(2,1)} %l_ref.1) | copy-start | bytes 12292
  54.5 11.5 %copy-start.4 = (bf16[1,16,128]{2,1,0:T(8,128)(2,1)S(1)}, bf16[1,16,128]{2,1,0:T(8,128)(2,1)}, u32[]{:S(2)}) copy-start(bf16[1,16,128]{2,1,0:T(8,128)(2,1)} %d_ref.1) | copy-start | bytes 12292
  56.7 9.3 %copy-start = (bf16[1,128,2048]{2,1,0:T(8,128)(2,1)S(1)}, bf16[1,128,2048]{2,1,0:T(8,128)(2,1)}, u32[]{:S(2)}) copy-start(bf16[1,128,2048]{2,1,0:T(8,128)(2,1)} %q_ref.1) | copy-start | bytes 1572868
  56.7 9.3 %copy-start.1 = (bf16[1,128,2048]{2,1,0:T(8,128)(2,1)S(1)}, bf16[1,128,2048]{2,1,0:T(8,128)(2,1)}, u32[]{:S(2)}) copy-start(bf16[1,128,2048]{2,1,0:T(8,128)(2,1)} %k_ref.1) | copy-start | bytes 1572868
  56.7 9.3 %copy-start.2 = (bf16[1,128,2048]{2,1,0:T(8,128)(2,1)S(1)}, bf16[1,128,2048]{2,1,0:T(8,128)(2,1)}, u32[]{:S(2)}) copy-start(bf16[1,128,2048]{2,1,0:T(8,128)(2,1)} %v_ref.1) | copy-start | bytes 1572868
  58.1 17.3 %all-to-all-start.1 = ((bf16[16,48,128]{2,1,0:T(8,128)(2,1)}), bf16[16,48,128]{2,1,0:T(8,128)(2,1)S(1)}, u32[]{:S(2)}, u32[]{:S(2)}) async-start(bf16[16,48,128]{2,1,0:T(8,128)(2,1)} %far_grads.1), calls=%async_computation.1 | async-start | bytes 393216 | tf_op jit(solution)/shard_map/all_to_all | solution.py:287
  65.2 0.8 %copy-start.6 = (bf16[1,128,2048]{2,1,0:T(8,128)(2,1)}, bf16[1,128,2048]{2,1,0:T(8,128)(2,1)S(1)}, u32[]{:S(2)}) copy-start(bf16[1,128,2048]{2,1,0:T(8,128)(2,1)S(1)} %collective-permute-done.7.g_ref) | copy-start | bytes 1572868
  66.0 1.0 %copy-start.7 = (bf16[1,128,2048]{2,1,0:T(8,128)(2,1)S(1)}, bf16[1,128,2048]{2,1,0:T(8,128)(2,1)}, u32[]{:S(2)}) copy-start(bf16[1,128,2048]{2,1,0:T(8,128)(2,1)} %copy-done.6) | copy-start | bytes 1572868
  75.5 0.7 copy-start.5

commit v3 on v2

v3 whole, which is shorter than its diff:
```python
import jax
import jax.numpy as jnp
from jax import lax
from jax.experimental import pallas as pl
from jax.experimental.pallas import tpu as pltpu
from jax.sharding import PartitionSpec as P


HEADS = 16
HD = 128
PICK = 16
RATE = 8
TOK = 128
NZ, NX, NC = 8, 4, 2
ROWS = 40
MAIN = 24
GROUP = 32
HALF = GROUP * PICK // 2
SCALE = HD ** (-0.5)
BF = jnp.bfloat16
F32 = jnp.float32

VM = pl.BlockSpec(memory_space=pltpu.VMEM)
SM = pl.BlockSpec(memory_space=pltpu.SMEM)


def dot(a, b):
    return lax.dot_general(a, b, (((1,), (0,)), ((), ())), preferred_element_type=F32)


def dot_t(a, b):
    return lax.dot_general(a, b, (((1,), (1,)), ((), ())), preferred_element_type=F32)


def dot_l(a, b):
    return lax.dot_general(a, b, (((0,), (0,)), ((), ())), preferred_element_type=F32)


def pick(x, off):
    t = x.astype(F32).reshape(PICK, RATE, HD)
    row = lax.broadcasted_iota(jnp.int32, (PICK, RATE, HD), 1)
    return jnp.sum(jnp.where(row == off, t, 0.0), axis=1).astype(BF)


def small(mib=12):
    return pltpu.CompilerParams(vmem_limit_bytes=mib << 20)


def pick_kernel(pos_ref, off_hbm, l_hbm, d_hbm, q_hbm, k_hbm, v_hbm, g_hbm, o_ref, off_ref, l_ref, d_ref, x_ref, sems):
    loads = [
        pltpu.make_async_copy(src, dst, sems.at[i])
        for i, (src, dst) in enumerate(
            (
                (off_hbm, off_ref),
                (q_hbm.at[0], x_ref.at[0]),
                (k_hbm.at[0], x_ref.at[1]),
                (v_hbm.at[0], x_ref.at[2]),
                (g_hbm.at[0], x_ref.at[3]),
                (l_hbm.at[0], l_ref),
                (d_hbm.at[0], d_ref),
            )
        )
    ]
    for load in loads:
        load.start()
    n = pos_ref[0]
    src = lax.broadcasted_iota(jnp.int32, (TOK, TOK), 0)
    dst = lax.broadcasted_iota(jnp.int32, (TOK, TOK), 1)
    place = jnp.where(dst == (n % 8) * PICK + src // RATE, 1.0, 0.0).astype(BF)
    loads[0].wait()
    for part, core, first in ((0, 0, 0), (1, 0, MAIN), (2, 1, 0), (3, 1, MAIN)):
        loads[1 + part].wait()
        for h in range(HEADS):
            rows = pick(x_ref[part, :, h * HD:(h + 1) * HD], off_ref[0, h])
            o_ref[2 * h + core, first:first + 16] = rows
    loads[5].wait()
    loads[6].wait()
    head = lax.broadcasted_iota(jnp.int32, (HEADS, TOK), 0)
    lane = lax.broadcasted_iota(jnp.int32, (HEADS, TOK), 1)
    off = jnp.zeros((HEADS, TOK), jnp.int32)
    for h in range(HEADS):
        off = jnp.where(head == h, off_ref[0, h], off)
    hit = (lane % RATE) == off
    lses = dot(jnp.where(hit, l_ref[...].astype(F32), 0.0).astype(BF), place)
    dlts = dot(jnp.where(hit, d_ref[...].astype(F32), 0.0).astype(BF), place)
    row = lax.broadcasted_iota(jnp.int32, (8, HD), 0)
    for h in range(HEADS):
        lse = jnp.broadcast_to(lses[h:h + 1], (8, HD))
        dlt = jnp.broadcast_to(dlts[h:h + 1], (8, HD))
        stats = jnp.where(row == n // 8, lse, jnp.where(row == 4 + n // 8, dlt, 0.0))
        o_ref[2 * h, 16:MAIN] = stats.astype(BF)
        o_ref[2 * h + 1, 16:MAIN] = jnp.zeros((8, HD), BF)


def pick_all(pos, offsets, lse, delta, query, key, value, grad):
    raw = pl.BlockSpec(memory_space=pltpu.HBM)
    return pl.pallas_call(
        pick_kernel,
        in_specs=[SM] + [raw] * 7,
        out_specs=VM,
        out_shape=jax.ShapeDtypeStruct((GROUP, ROWS, HD), BF),
        scratch_shapes=[
            pltpu.SMEM((1, HEADS), jnp.int32),
            pltpu.VMEM((HEADS, TOK), BF),
            pltpu.VMEM((HEADS, TOK), BF),
            pltpu.VMEM((4, TOK, HEADS * HD), BF),
            pltpu.SemaphoreType.DMA((7,)),
        ],
        name="pick_all",
    )(pos, offsets, lse, delta, query, key, value, grad)


def local_kernel(off_ref, q_ref, k_ref, v_ref, g_ref, l_ref, d_ref, dq_ref, dk_ref, dv_ref, offs_ref, st_ref):
    step = pl.program_id(0)

    @pl.when(step == 0)
    def _():
        st_ref[0] = l_ref[0].astype(F32)
        st_ref[1] = d_ref[0].astype(F32)
        for h in range(HEADS):
            offs_ref[h:h + 1, :] = jnp.full((1, TOK), off_ref[0, h], jnp.int32)

    base = pl.multiple_of(step * 4, 4)
    lses = st_ref[0, pl.ds(base, 4), :]
    dlts = st_ref[1, pl.ds(base, 4), :]
    for i in range(4):
        cols = slice(i * HD, (i + 1) * HD)
        q, k, v, g = q_ref[0, :, cols], k_ref[0, :, cols], v_ref[0, :, cols], g_ref[0, :, cols]
        p = jnp.exp(dot_t(k, q) * SCALE - lses[i:i + 1])
        ds = (p * (dot_t(v, g) - dlts[i:i + 1])).astype(BF)
        dv_ref[:, cols] = dot(p.astype(BF), g).astype(BF)
        dk_ref[:, cols] = (dot(ds, q) * SCALE).astype(BF)
        dq_ref[:, cols] = (dot_l(ds, k) * SCALE).astype(BF)


def local_grads(offsets, query, key, value, grad, lse, delta):
    wide = pl.BlockSpec((1, TOK, 4 * HD), lambda i: (0, 0, i))
    out = pl.BlockSpec((TOK, 4 * HD), lambda i: (0, i))
    stat = pl.BlockSpec((1, HEADS, TOK), lambda i: (0, 0, 0))
    shape = jax.ShapeDtypeStruct((TOK, HEADS * HD), BF)
    return pl.pallas_call(
        local_kernel,
        grid=(4,),
        in_specs=[SM, wide, wide, wide, wide, stat, stat],
        out_specs=[out, out, out, pl.BlockSpec((HEADS, TOK), lambda i: (0, 0))],
        out_shape=[shape, shape, shape, jax.ShapeDtypeStruct((HEADS, TOK), jnp.int32)],
        scratch_shapes=[pltpu.VMEM((2, HEADS, TOK), F32)],
        compiler_params=small(),
        cost_estimate=pl.CostEstimate(flops=16 * 5 * 2 * 128 ** 3 * 4, bytes_accessed=3670016, transcendentals=262144),
        name="local_grads",
    )(offsets, query, key, value, grad, lse, delta)


def query_side(q, g, k, v, lse, dlt):
    p = jnp.exp(dot_t(q, k) * SCALE - lse)
    ds = (p * (dot_t(g, v) - dlt)).astype(BF)
    return dot(ds, k)


def key_side(k, v, q, g, stats):
    lse = jnp.concatenate([stats[i:i + 1] for i in range(4)], axis=1)
    dlt = jnp.concatenate([stats[i:i + 1] for i in range(4, 8)], axis=1)
    p = jnp.exp(dot_t(k, q) * SCALE - lse)
    ds = (p * (dot_t(v, g) - dlt)).astype(BF)
    return dot(ds, q), dot(p.astype(BF), g)


def flat(rows):
    return rows.reshape(GROUP * PICK, HD)


def whole(core, mine_a, mine_b, other_a, other_b):
    zero = core == 0
    q = jnp.where(zero, mine_a[:, 0:16], other_a[:, 0:16])
    v = jnp.where(zero, other_a[:, 0:16], mine_a[:, 0:16])
    st = jnp.sum(jnp.where(zero, mine_a[:, 16:MAIN], other_a[:, 16:MAIN]).astype(F32), axis=0)
    k = jnp.where(zero, mine_b[...], other_b[...])
    g = jnp.where(zero, other_b[...], mine_b[...])
    return flat(q), flat(k), flat(v), flat(g), st


def share(core, rows):
    width = rows.shape[-1]
    t = rows.astype(F32).reshape(GROUP, 2, 8, width)
    return jnp.where(core == 0, t[:, 0], t[:, 1]).reshape(HALF, width)


def near_kernel(core_ref, a_ref, b_ref, oa_ref, hop_ref, cross_ref, sub_ref, col_ref, dq_ref, dk_ref, dv_ref):
    core = core_ref[0]
    mine_b = jnp.where(core == 0, b_ref[...], hop_ref[...])
    q, k, v, g, stats = whole(core, a_ref, mine_b, oa_ref, cross_ref)
    turned = jnp.transpose(jnp.concatenate([stats, jnp.zeros((HD - 8, HD), F32)], axis=0))
    lse = share(core, jnp.concatenate([turned[:, i:i + 1] for i in range(4)], axis=0))
    dlt = share(core, jnp.concatenate([turned[:, i:i + 1] for i in range(4, 8)], axis=0))
    sq, sk, sv, sg = (share(core, rows).astype(BF) for rows in (q, k, v, g))
    for i, rows in enumerate((sq, sk, sv, sg)):
        sub_ref[i] = rows
    lane = lax.broadcasted_iota(jnp.int32, (HALF, HD), 1)
    col_ref[...] = jnp.where(lane == 0, lse, dlt)
    dq_ref[...] = query_side(sq, sg, k, v, lse, dlt)
    dk_ref[...], dv_ref[...] = key_side(sk, sv, q, g, stats)


def near_grads(*args):
    part = jax.ShapeDtypeStruct((HALF, HD), F32)
    return pl.pallas_call(
        near_kernel,
        in_specs=[SM] + [VM] * 5,
        out_specs=[VM] * 5,
        out_shape=[jax.ShapeDtypeStruct((4, HALF, HD), BF)] + [part] * 4,
        compiler_params=small(),
        cost_estimate=pl.CostEstimate(flops=14 * 2 * 256 * 256 * 128 * 2, bytes_accessed=1572864, transcendentals=262144),
        name="near_grads",
    )(*args)


def far_kernel(core_ref, a_ref, b_ref, oa_ref, ob_ref, sub_ref, col_ref, dq_ref, dk_ref, dv_ref, o_ref):
    core = core_ref[0]
    q, k, v, g, stats = whole(core, a_ref, b_ref, oa_ref, ob_ref)
    lse, dlt = col_ref[:, 0:1], col_ref[:, 1:2]
    dq = dq_ref[...] + query_side(sub_ref[0], sub_ref[3], k, v, lse, dlt)
    dk, dv = key_side(sub_ref[1], sub_ref[2], q, g, stats)
    o_ref[:, 0:8, :] = (dq * SCALE).reshape(GROUP, 8, HD).astype(BF)
    o_ref[:, 8:16, :] = ((dk_ref[...] + dk) * SCALE).reshape(GROUP, 8, HD).astype(BF)
    o_ref[:, 16:24, :] = (dv_ref[...] + dv).reshape(GROUP, 8, HD).astype(BF)


def far_grads(*args):
    return pl.pallas_call(
        far_kernel,
        in_specs=[SM] + [VM] * 9,
        out_specs=VM,
        out_shape=jax.ShapeDtypeStruct((GROUP, 24, HD), BF),
        compiler_params=small(),
        name="far_grads",
    )(*args)


def combine_kernel(w_ref, dq_ref, dk_ref, dv_ref, off_ref, oq_ref, ok_ref, ov_ref):
    row = lax.broadcasted_iota(jnp.int32, (PICK, RATE, HD), 1)
    for h in range(HEADS):
        hit = row == off_ref[h:h + 1, :].reshape(1, 1, TOK)
        for part, (src, out) in enumerate(((dq_ref, oq_ref), (dk_ref, ok_ref), (dv_ref, ov_ref))):
            rows = slice(part * 8, (part + 1) * 8)
            w = jnp.concatenate([w_ref[2 * h, rows, :].astype(F32), w_ref[2 * h + 1, rows, :].astype(F32)], axis=0)
            local = src[:, h * HD:(h + 1) * HD].astype(F32).reshape(PICK, RATE, HD)
            total = local + jnp.where(hit, w[:, None, :], 0.0)
            out[0, :, h * HD:(h + 1) * HD] = total.reshape(TOK, HD).astype(BF)


def combine(wide, local):
    shape = jax.ShapeDtypeStruct((1, TOK, HEADS * HD), BF)
    return pl.pallas_call(
        combine_kernel,
        in_specs=[VM] * 5,
        out_specs=[VM] * 3,
        out_shape=[shape, shape, shape],
        compiler_params=small(),
        name="combine",
    )(wide, *local)


def place_of(z, x, c):
    return (z * NX + x) * NC + c


def column(half, place):
    return place if half == 0 else NX - 1 - place


GROUPS = [
    [place_of(z, column(half, p), c) for z in range(NZ) for p in range(2) for c in range(NC)]
    for half in range(2)
]


def move(value, route):
    count, seats = lax.axis_size("section"), lax.axis_size("seq")
    pairs = []
    for s in range(count):
        for z in range(NZ):
            for x in range(NX):
                for c in range(NC):
                    target = route(s, x, c)
                    if target is not None:
                        ts, tx, tc = target
                        pairs.append((s * seats + place_of(z, x, c), (ts % count) * seats + place_of(z, tx, tc)))
    return lax.ppermute(value, ("section", "seq"), pairs)


def swap(value):
    return lax.all_to_all(value, "seq", 0, 0, axis_index_groups=GROUPS, tiled=True)


def body(queries, key_rows, value_rows, grad_out, log_sums, deltas, offsets):
    seat = lax.axis_index("seq").astype(jnp.int32)
    x = seat // NC % NX
    core = (seat % NC).reshape(1)
    pos = (seat // (NX * NC) * 4 + jnp.where(x < 2, x, NX - 1 - x) * 2 + seat % NC).reshape(1)
    grad = move(grad_out, lambda s, x, c: (s - 1, x, c))
    picked = pick_all(pos, offsets, log_sums, deltas, queries, key_rows, value_rows, grad_out)
    mine = swap(picked)
    a, b = mine[:, :MAIN], mine[:, MAIN:]
    far_a = move(a, lambda s, x, c: (s, 3 - x, c))
    far_b = move(b, lambda s, x, c: (s - c, 3 - x, c))
    hop = move(b, lambda s, x, c: (s - 1, x, 1) if c == 1 else None)
    cross = move(b, lambda s, x, c: (s - c, x, 1 - c))
    other_a = move(a, lambda s, x, c: (s, x, 1 - c))
    other_far_a = move(far_a, lambda s, x, c: (s, x, 1 - c))
    other_far_b = move(far_b, lambda s, x, c: (s, x, 1 - c))
    local = local_grads(offsets, queries, key_rows, value_rows, grad, log_sums, deltas)
    part = near_grads(core, a, b, other_a, hop, cross)
    back = swap(far_grads(core, far_a, far_b, other_far_a, other_far_b, *part))
    return tuple(combine(back, local))


def solution(mesh):
    rows = P("section", "seq", None)
    stats = P("section", None, "seq")
    return jax.shard_map(
        body,
        mesh=mesh,
        in_specs=(rows, rows, rows, rows, stats, stats, P("seq", None)),
        out_specs=(rows, rows, rows),
        check_vma=False,
    )
```

time: 79.6 us -> 68.1 us (0.86); the launches traced: 78.3 us -> 67.8 us
  waiting for transfers between devices: 19.5 us -> 11.3 us
  starting transfers between devices: 20.4 us -> 17.2 us
  blocking collectives: 22.4 us -> 23.8 us
    ppermute x8, waiting for transfers between devices: 15.5 us -> 8.77 us  [move(): return lax.ppermute(value, ('section', 'seq'), pairs)]
    all_to_all x1, starting transfers between devices: 7.08 us -> 3.78 us  [swap(): lax.all_to_all(value, 'seq', 0, 0, axis_index_groups=GROUPS, tiled=True)]
    all_to_all x1, blocking collectives: 22.4 us -> 23.8 us  [swap(): lax.all_to_all(value, 'seq', 0, 0, axis_index_groups=GROUPS, tiled=True)]
    all_to_all x1, waiting for transfers between devices: 4.01 us -> 2.56 us  [swap(): lax.all_to_all(value, 'seq', 0, 0, axis_index_groups=GROUPS, tiled=True)]
  transfers between devices with their start and end apart: 9 -> 9, of which waited for: 5 -> 3; matrix products, arithmetic and copies ran while one was open for 0% -> 0% of each run, Pallas kernels for 9% -> 11%
where the time goes in v3:
time: 68.1 us; the launch traced here: 67.8 us
  blocking collectives  23.8 us (35%)
  starting transfers between devices  17.2 us (25%)
  Pallas kernels  12.7 us (19%)
  waiting for transfers between devices  11.3 us (17%)
  local copies, waits for them, and re-layouts  1.89 us (3%)
  between operations  0.83 us (1%)
    all_to_all x1, blocking collectives, swap(): lax.all_to_all(value, 'seq', 0, 0, axis_index_groups=GROUPS, tiled=True)  23.8 us
    ppermute x8, starting transfers between devices, move(): return lax.ppermute(value, ('section', 'seq'), pairs)  13.4 us
    ppermute x8, waiting for transfers between devices, move(): return lax.ppermute(value, ('section', 'seq'), pairs)  8.77 us
    pallas_call x1, Pallas kernels, local_grads(): pl.pallas_call(local_kernel, grid=(4,), in_specs=[SM, wide, wide, wide, w...  4.99 us
    all_to_all x1, starting transfers between devices, swap(): lax.all_to_all(value, 'seq', 0, 0, axis_index_groups=GROUPS, tiled=True)  3.78 us
    pallas_call x1, Pallas kernels, pick_all(): pl.pallas_call(pick_kernel, in_specs=[SM] + [raw] * 7, out_specs=VM, out_...  3.51 us
    all_to_all x1, waiting for transfers between devices, swap(): lax.all_to_all(value, 'seq', 0, 0, axis_index_groups=GROUPS, tiled=True)  2.56 us
    unnamed x18, local copies, waits for them, and re-layouts  1.86 us
  transfers between devices with their start and end apart: 9, of which 3 were waited for; matrix products, arithmetic and copies ran while one was open for 0% of the time, Pallas kernels for 11%

profile of v3, /device:TPU:1, one launch (start us, length us, event | category | flops | bytes accessed | tf_op | source)
XLA Modules:
  0.0 67.8 jit_solution(6718020088476670678)
XLA Ops:
  0.7 3.5 %pick_all.1 = bf16[32,40,128]{2,1,0:T(8,128)(2,1)} custom-call(s32[1]{0:T(128)} %bitcast.1.pos_ref, s32[1,16]{1,0:T(1,128)} %off_ref.1, bf16[1,16,128]{2,1,0:T(8,128)(2,1)} %l_ref.1, bf16[1,16,128]{2,1,0:T(8,128)(2,1)} %d_ref.1, bf16[1,128,2048]{2,1,0:T(8,128)(2,1)} %q_ref.1, bf16[1,128,2048]{2,1,0:T(8,128)(2,1)} %k_ref.1, bf16[1,128,2048]{2,1,0:T(8,128)(2,1)} %v_ref.1, ...), custom_call_target="tpu_custom_call" | custom-call | tf_op jit(solution)/shard_map/pick_all/pallas_call | solution.py:97
  4.2 0.0 copy-start.8
  4.2 23.8 %all_to_all.10 = bf16[32,40,128]{2,1,0:T(8,128)(2,1)S(1)} all-to-all(bf16[32,40,128]{2,1,0:T(8,128)(2,1)} %pick_all.1), channel_id=1, replica_groups={{0,1,2,3,8,9,10,11,16,17,18,19,24,25,26,27,32,33,34,35,40,41,42,43,48,4..., dimensions={0} | all-to-all | bytes 655360 | tf_op jit(solution)/shard_map/all_to_all | solution.py:292
  28.1 1.9 %collective-permute-start = (bf16[32,24,128]{2,1,0:T(8,128)(2,1)S(1)}, bf16[32,24,128]{2,1,0:T(8,128)(2,1)S(1)}, u32[]{:S(2)}, u32[]{:S(2)}) collective-permute-start(bf16[32,24,128]{2,1,0:T(8,128)(2,1)S(1)} %slice.8.a_ref), channel_id=1, source_target_pairs={{0,6},{1,7},{2,4},{3,5},{4,2},{5,3},{6,0},{7,1},{8,14},{9,15},{10,... | collective-permute-start | bytes 589832 | tf_op jit(solution)/shard_map/ppermute | solution.py:288
  30.0 4.3 %collective-permute-start.6 = (bf16[32,16,128]{2,1,0:T(8,128)(2,1)S(1)}, bf16[32,16,128]{2,1,0:T(8,128)(2,1)S(1)}, u32[]{:S(2)}, u32[]{:S(2)}) collective-permute-start(bf16[32,16,128]{2,1,0:T(8,128)(2,1)S(1)} %slice.9.b_ref), channel_id=1, source_target_pairs={{0,1},{1,192},{2,3},{3,194},{4,5},{5,196},{6,7},{7,198},{8,9},{9,2... | collective-permute-start | bytes 393224 | tf_op jit(solution)/shard_map/ppermute | solution.py:288
  34.3 0.5 collective-permute-start.7
  34.8 0.7 %collective-permute-start.1 = (bf16[32,16,128]{2,1,0:T(8,128)(2,1)S(1)}, bf16[32,16,128]{2,1,0:T(8,128)(2,1)S(1)}, u32[]{:S(2)}, u32[]{:S(2)}) collective-permute-start(bf16[32,16,128]{2,1,0:T(8,128)(2,1)S(1)} %slice.9.b_ref), channel_id=1, source_target_pairs={{0,6},{1,199},{2,4},{3,197},{4,2},{5,195},{6,0},{7,193},{8,14},{9,... | collective-permute-start | bytes 393224 | tf_op jit(solution)/shard_map/ppermute | solution.py:288
  35.5 0.4 collective-permute-start.4
  36.0 0.7 %collective-permute-start.2 = (bf16[32,24,128]{2,1,0:T(8,128)(2,1)S(1)}, bf16[32,24,128]{2,1,0:T(8,128)(2,1)S(1)}, u32[]{:S(2)}, u32[]{:S(2)}) collective-permute-start(bf16[32,24,128]{2,1,0:T(8,128)(2,1)S(1)} %collective-permute-done.a_ref), channel_id=1, source_target_pairs={{0,1},{1,0},{2,3},{3,2},{4,5},{5,4},{6,7},{7,6},{8,9},{9,8},{10,11... | collective-permute-start | bytes 589832 | tf_op jit(solution)/shard_map/ppermute | solution.py:288
  36.7 0.3 collective-permute-done.6.cross_ref
  37.0 4.6 %collective-permute-start.5 = (bf16[32,16,128]{2,1,0:T(8,128)(2,1)S(1)}, bf16[32,16,128]{2,1,0:T(8,128)(2,1)S(1)}, u32[]{:S(2)}, u32[]{:S(2)}) collective-permute-start(bf16[32,16,128]{2,1,0:T(8,128)(2,1)S(1)} %slice.9.b_ref), channel_id=1, source_target_pairs={{1,193},{3,195},{5,197},{7,199},{9,201},{11,203},{13,205},{15,207}... | collective-permute-start | bytes 393224 | tf_op jit(solution)/shard_map/ppermute | solution.py:288
  41.6 0.2 collective-permute-start.3
  41.8 8.5 %collective-permute-done.5.hop_ref = bf16[32,16,128]{2,1,0:T(8,128)(2,1)S(1)} collective-permute-done((bf16[32,16,128]{2,1,0:T(8,128)(2,1)S(1)}, bf16[32,16,128]{2,1,0:T(8,128)(2,1)S(1)}, u32[]{:S(2)}, u32[]{:S(2)}) %collective-permute-start.5) | collective-permute-done | bytes 131104 | tf_op jit(solution)/shard_map/ppermute | solution.py:288
  50.3 1.0 %near_grads.1 = (bf16[4,256,128]{2,1,0:T(8,128)(2,1)S(1)}, f32[256,128]{1,0:T(8,128)S(1)}, f32[256,128]{1,0:T(8,128)S(1)}, f32[256,128]{1,0:T(8,128)S(1)}, f32[256,128]{1,0:T(8,128)S(1)}) custom-call(s32[1]{0:T(128)} %bitcast.core_ref, bf16[32,24,128]{2,1,0:T(8,128)(2,1)S(1)} %slice.8.a_ref, bf16[32,16,128]{2,1,0:T(8,128)(2,1)S(1)} %slice.9.b_ref, ...), custom_call_target="tpu_custom_call" | custom-call | flops 469762048 | bytes 1572864 | tf_op jit(solution)/shard_map/near_grads/pallas_call | solution.py:206
  51.3 0.0 copy-start
  51.3 0.0 copy-start.1
  51.4 0.0 copy-start.2
  51.4 1.5 %far_grads.1 = bf16[32,24,128]{2,1,0:T(8,128)(2,1)} custom-call(s32[1]{0:T(128)} %bitcast.core_ref, bf16[32,24,128]{2,1,0:T(8,128)(2,1)S(1)} %collective-permute-done.a_ref, bf16[32,16,128]{2,1,0:T(8,128)(2,1)S(1)} %collective-permute-done.1.b_ref, bf16[32,24,128]{2,1,0:T(8,128)(2,1)S(1)} %collective-permute-done.2.oa_ref, ...), custom_call_target="tpu_custom_call" | custom-call | tf_op jit(solution)/shard_map/far_grads/pallas_call | solution.py:229
  52.9 3.8 %all-to-all-start.1 = ((bf16[32,24,128]{2,1,0:T(8,128)(2,1)}), bf16[32,24,128]{2,1,0:T(8,128)(2,1)S(1)}, u32[]{:S(2)}, u32[]{:S(2)}) async-start(bf16[32,24,128]{2,1,0:T(8,128)(2,1)} %far_grads.1), calls=%async_computation.1 | async-start | bytes 393216 | tf_op jit(solution)/shard_map/all_to_all | solution.py:292
  56.7 0.8 %copy-done.6 = bf16[1,128,2048]{2,1,0:T(8,128)(2,1)} copy-done((bf16[1,128,2048]{2,1,0:T(8,128)(2,1)}, bf16[1,128,2048]{2,1,0:T(8,128)(2,1)S(1)}, u32[]{:S(2)}) %copy-start.6) | copy-done | bytes 524312
  57.5 1.0 %copy-done.7 = bf16[1,128,2048]{2,1,0:T(8,128)(2,1)S(1)} copy-done((bf16[1,128,2048]{2,1,0:T(8,128)(2,1)S(1)}, bf16[1,128,2048]{2,1,0:T(8,128)(2,1)}, u32[]{:S(2)}) %copy-start.7) | copy-done | bytes 524312
  58.6 5.0 %local_grads.1 = (bf16[128,2048]{1,0:T(8,128)(2,1)S(1)}, bf16[128,2048]{1,0:T(8,128)(2,1)S(1)}, bf16[128,2048]{1,0:T(8,128)(2,1)S(1)}, s32[16,128]{1,0:T(8,128)S(1)}) custom-call(s32[1,16]{1,0:T(1,128)S(1)} %copy-done.5, bf16[1,128,2048]{2,1,0:T(8,128)(2,1)S(1)} %copy-done, bf16[1,128,2048]{2,1,0:T(8,128)(2,1)S(1)} %copy-done.1, ...), custom_call_target="tpu_custom_call" | custom-call | flops 1342177280 | bytes 3670016 | tf_op jit(solution)/shard_map/local_grads/pallas_call | solution.py:141
  63.5 2.6 %all-to-all-done.1.w_ref = bf16[32,24,128]{2,1,0:T(8,128)(2,1)S(1)} async-done(((bf16[32,24,128]{2,1,0:T(8,128)(2,1)}), bf16[32,24,128]{2,1,0:T(8,128)(2,1)S(1)}, u32[]{:S(2)}, u32[]{:S(2)}) %all-to-all-start.1) | async-done | bytes 196640 | tf_op jit(solution)/shard_map/all_to_all | solution.py:292
  66.1 1.6 %combine.1 = (bf16[1,128,2048]{2,1,0:T(8,128)(2,1)}, bf16[1,128,2048]{2,1,0:T(8,128)(2,1)}, bf16[1,128,2048]{2,1,0:T(8,128)(2,1)}) custom-call(bf16[32,24,128]{2,1,0:T(8,128)(2,1)S(1)} %all-to-all-done.1.w_ref, bf16[128,2048]{1,0:T(8,128)(2,1)S(1)} %get-tuple-element.17.dq_ref, bf16[128,2048]{1,0:T(8,128)(2,1)S(1)} %get-tuple-element.18.dk_ref, ...), custom_call_target="tpu_custom_call" | custom-call | tf_op jit(solution)/shard_map/combine/pallas_call | solution.py:253
  (20 shorter events, 0.1 us)
Async XLA Ops:
  4.2 30.1 %copy-start.8 = (bf16[1,128,2048]{2,1,0:T(8,128)(2,1)S(1)}, bf16[1,128,2048]{2,1,0:T(8,128)(2,1)}, u32[]{:S(2)}) copy-start(bf16[1,128,2048]{2,1,0:T(8,128)(2,1)} %g_hbm.1) | copy-start | bytes 1572868
  28.1 7.9 %collective-permute-start = (bf16[32,24,128]{2,1,0:T(8,128)(2,1)S(1)}, bf16[32,24,128]{2,1,0:T(8,128)(2,1)S(1)}, u32[]{:S(2)}, u32[]{:S(2)}) collective-permute-start(bf16[32,24,128]{2,1,0:T(8,128)(2,1)S(1)} %slice.8.a_ref), channel_id=1, source_target_pairs={{0,6},{1,7},{2,4},{3,5},{4,2},{5,3},{6,0},{7,1},{8,14},{9,15},{10,... | collective-permute-start | bytes 589832 | tf_op jit(solution)/shard_map/ppermute | solution.py:288
  30.0 7.0 %collective-permute-start.6 = (bf16[32,16,128]{2,1,0:T(8,128)(2,1)S(1)}, bf16[32,16,128]{2,1,0:T(8,128)(2,1)S(1)}, u32[]{:S(2)}, u32[]{:S(2)}) collective-permute-start(bf16[32,16,128]{2,1,0:T(8,128)(2,1)S(1)} %slice.9.b_ref), channel_id=1, source_target_pairs={{0,1},{1,192},{2,3},{3,194},{4,5},{5,196},{6,7},{7,198},{8,9},{9,2... | collective-permute-start | bytes 393224 | tf_op jit(solution)/shard_map/ppermute | solution.py:288
  34.3 22.3 %collective-permute-start.7 = (bf16[1,128,2048]{2,1,0:T(8,128)(2,1)S(1)}, bf16[1,128,2048]{2,1,0:T(8,128)(2,1)S(1)}, u32[]{:S(2)}, u32[]{:S(2)}) collective-permute-start(bf16[1,128,2048]{2,1,0:T(8,128)(2,1)S(1)} %copy-done.8), channel_id=1, source_target_pairs={{0,192},{1,193},{2,194},{3,195},{4,196},{5,197},{6,198},{7,199},{8... | collective-permute-start | bytes 1572872 | tf_op jit(solution)/shard_map/ppermute | solution.py:288
  34.8 6.8 %collective-permute-start.1 = (bf16[32,16,128]{2,1,0:T(8,128)(2,1)S(1)}, bf16[32,16,128]{2,1,0:T(8,128)(2,1)S(1)}, u32[]{:S(2)}, u32[]{:S(2)}) collective-permute-start(bf16[32,16,128]{2,1,0:T(8,128)(2,1)S(1)} %slice.9.b_ref), channel_id=1, source_target_pairs={{0,6},{1,199},{2,4},{3,197},{4,2},{5,195},{6,0},{7,193},{8,14},{9,... | collective-permute-start | bytes 393224 | tf_op jit(solution)/shard_map/ppermute | solution.py:288
  35.5 14.7 %collective-permute-start.4 = (bf16[32,24,128]{2,1,0:T(8,128)(2,1)S(1)}, bf16[32,24,128]{2,1,0:T(8,128)(2,1)S(1)}, u32[]{:S(2)}, u32[]{:S(2)}) collective-permute-start(bf16[32,24,128]{2,1,0:T(8,128)(2,1)S(1)} %slice.8.a_ref), channel_id=1, source_target_pairs={{0,1},{1,0},{2,3},{3,2},{4,5},{5,4},{6,7},{7,6},{8,9},{9,8},{10,11... | collective-permute-start | bytes 589832 | tf_op jit(solution)/shard_map/ppermute | solution.py:288
  36.0 15.4 %collective-permute-start.2 = (bf16[32,24,128]{2,1,0:T(8,128)(2,1)S(1)}, bf16[32,24,128]{2,1,0:T(8,128)(2,1)S(1)}, u32[]{:S(2)}, u32[]{:S(2)}) collective-permute-start(bf16[32,24,128]{2,1,0:T(8,128)(2,1)S(1)} %collective-permute-done.a_ref), channel_id=1, source_target_pairs={{0,1},{1,0},{2,3},{3,2},{4,5},{5,4},{6,7},{7,6},{8,9},{9,8},{10,11... | collective-permute-start | bytes 589832 | tf_op jit(solution)/shard_map/ppermute | solution.py:288
  37.0 13.3 %collective-permute-start.5 = (bf16[32,16,128]{2,1,0:T(8,128)(2,1)S(1)}, bf16[32,16,128]{2,1,0:T(8,128)(2,1)S(1)}, u32[]{:S(2)}, u32[]{:S(2)}) collective-permute-start(bf16[32,16,128]{2,1,0:T(8,128)(2,1)S(1)} %slice.9.b_ref), channel_id=1, source_target_pairs={{1,193},{3,195},{5,197},{7,199},{9,201},{11,203},{13,205},{15,207}... | collective-permute-start | bytes 393224 | tf_op jit(solution)/shard_map/ppermute | solution.py:288
  41.6 9.7 %collective-permute-start.3 = (bf16[32,16,128]{2,1,0:T(8,128)(2,1)S(1)}, bf16[32,16,128]{2,1,0:T(8,128)(2,1)S(1)}, u32[]{:S(2)}, u32[]{:S(2)}) collective-permute-start(bf16[32,16,128]{2,1,0:T(8,128)(2,1)S(1)} %collective-permute-done.1.b_ref), channel_id=1, source_target_pairs={{0,1},{1,0},{2,3},{3,2},{4,5},{5,4},{6,7},{7,6},{8,9},{9,8},{10,11... | collective-permute-start | bytes 393224 | tf_op jit(solution)/shard_map/ppermute | solution.py:288
  51.3 6.1 %copy-start = (bf16[1,128,2048]{2,1,0:T(8,128)(2,1)S(1)}, bf16[1,128,2048]{2,1,0:T(8,128)(2,1)}, u32[]{:S(2)}) copy-start(bf16[1,128,2048]{2,1,0:T(8,128)(2,1)} %q_ref.1) | copy-start | bytes 1572868
  51.3 6.1 %copy-start.1 = (bf16[1,128,2048]{2,1,0:T(8,128)(2,1)S(1)}, bf16[1,128,2048]{2,1,0:T(8,128)(2,1)}, u32[]{:S(2)}) copy-start(bf16[1,128,2048]{2,1,0:T(8,128)(2,1)} %k_ref.1) | copy-start | bytes 1572868
  51.4 6.1 %copy-start.2 = (bf16[1,128,2048]{2,1,0:T(8,128)(2,1)S(1)}, bf16[1,128,2048]{2,1,0:T(8,128)(2,1)}, u32[]{:S(2)}) copy-start(bf16[1,128,2048]{2,1,0:T(8,128)(2,1)} %v_ref.1) | copy-start | bytes 1572868
  52.9 4.6 %copy-start.3 = (bf16[1,16,128]{2,1,0:T(8,128)(2,1)S(1)}, bf16[1,16,128]{2,1,0:T(8,128)(2,1)}, u32[]{:S(2)}) copy-start(bf16[1,16,128]{2,1,0:T(8,128)(2,1)} %l_ref.1) | copy-start | bytes 12292
  52.9 4.6 %copy-start.4 = (bf16[1,16,128]{2,1,0:T(8,128)(2,1)S(1)}, bf16[1,16,128]{2,1,0:T(8,128)(2,1)}, u32[]{:S(2)}) copy-start(bf16[1,16,128]{2,1,0:T(8,128)(2,1)} %d_ref.1) | copy-start | bytes 12292
  52.9 4.6 %copy-start.5 = (s32[1,16]{1,0:T(1,128)S(1)}, s32[1,16]{1,0:T(1,128)}, u32[]{:S(2)}) copy-start(s32[1,16]{1,0:T(1,128)} %off_ref.1) | copy-start | bytes 196
  52.9 13.2 %all-to-all-start.1 = ((bf16[32,24,128]{2,1,0:T(8,128)(2,1)}), bf16[32,24,128]{2,1,0:T(8,128)(2,1)S(1)}, u32[]{:S(2)}, u32[]{:S(2)}) async-start(bf16[32,24,128]{2,1,0:T(8,128)(2,1)} %far_grads.1), calls=%async_computation.1 | async-start | bytes 393216 | tf_op jit(solution)/shard_map/all_to_all | solution.py:292
  56.7 0.8 %copy-start.6 = (bf16[1,128,2048]{2,1,0:T(8,128)(2,1)}, bf16[1,128,2048]{2,1,0:T(8,128)(2,1)S(1)}, u32[]{:S(2)}) copy-start(bf16[1,128,2048]{2,1,0:T(8,128)(2,1)S(1)} %collective-permute-done.7.g_ref) | copy-start | bytes 1572868
  57.5 1.0 %copy-start.7 = (bf16[1,128,2048]{2,1,0:T(8,128)(2,1)S(1)}, bf16[1,128,2048]{2,1,0:T(8,128)(2,1)}, u32[]{:S(2)}) copy-start(bf16[1,128,2048]{2,1,0:T(8,128)(2,1)} %copy-done.6) | copy-start | bytes 1572868

commit v4 on v3

--- a/solution.py
+++ b/solution.py
@@ -36,10 +36,10 @@
     return lax.dot_general(a, b, (((0,), (0,)), ((), ())), preferred_element_type=F32)
 
 
-def pick(x, off):
-    t = x.astype(F32).reshape(PICK, RATE, HD)
-    row = lax.broadcasted_iota(jnp.int32, (PICK, RATE, HD), 1)
-    return jnp.sum(jnp.where(row == off, t, 0.0), axis=1).astype(BF)
+def chooser(off):
+    row = lax.broadcasted_iota(jnp.int32, (PICK, TOK), 0)
+    tok = lax.broadcasted_iota(jnp.int32, (PICK, TOK), 1)
+    return jnp.where(tok == row * RATE + off, 1.0, 0.0).astype(BF)
 
 
 def small(mib=12):
@@ -68,11 +68,12 @@
     dst = lax.broadcasted_iota(jnp.int32, (TOK, TOK), 1)
     place = jnp.where(dst == (n % 8) * PICK + src // RATE, 1.0, 0.0).astype(BF)
     loads[0].wait()
+    choose = [chooser(off_ref[0, h]) for h in range(HEADS)]
     for part, core, first in ((0, 0, 0), (1, 0, MAIN), (2, 1, 0), (3, 1, MAIN)):
         loads[1 + part].wait()
         for h in range(HEADS):
-            rows = pick(x_ref[part, :, h * HD:(h + 1) * HD], off_ref[0, h])
-            o_ref[2 * h + core, first:first + 16] = rows
+            rows = dot(choose[h], x_ref[part, :, h * HD:(h + 1) * HD])
+            o_ref[2 * h + core, first:first + 16] = rows.astype(BF)
     loads[5].wait()
     loads[6].wait()
     head = lax.broadcasted_iota(jnp.int32, (HEADS, TOK), 0)
@@ -171,12 +172,11 @@
 
 def whole(core, mine_a, mine_b, other_a, other_b):
     zero = core == 0
-    q = jnp.where(zero, mine_a[:, 0:16], other_a[:, 0:16])
-    v = jnp.where(zero, other_a[:, 0:16], mine_a[:, 0:16])
-    st = jnp.sum(jnp.where(zero, mine_a[:, 16:MAIN], other_a[:, 16:MAIN]).astype(F32), axis=0)
-    k = jnp.where(zero, mine_b[...], other_b[...])
-    g = jnp.where(zero, other_b[...], mine_b[...])
-    return flat(q), flat(k), flat(v), flat(g), st
+    q = jnp.where(zero, mine_a, other_a)
+    v = jnp.where(zero, other_a, mine_a)
+    k = jnp.where(zero, mine_b, other_b)
+    g = jnp.where(zero, other_b, mine_b)
+    return flat(q), flat(k), flat(v), flat(g)
 
 
 def share(core, rows):
@@ -185,10 +185,11 @@
     return jnp.where(core == 0, t[:, 0], t[:, 1]).reshape(HALF, width)
 
 
-def near_kernel(core_ref, a_ref, b_ref, oa_ref, hop_ref, cross_ref, sub_ref, col_ref, dq_ref, dk_ref, dv_ref):
+def near_kernel(core_ref, a_ref, b_ref, st_ref, oa_ref, ost_ref, hop_ref, cross_ref, sub_ref, col_ref, dq_ref, dk_ref, dv_ref):
     core = core_ref[0]
     mine_b = jnp.where(core == 0, b_ref[...], hop_ref[...])
-    q, k, v, g, stats = whole(core, a_ref, mine_b, oa_ref, cross_ref)
+    q, k, v, g = whole(core, a_ref[...], mine_b, oa_ref[...], cross_ref[...])
+    stats = jnp.where(core == 0, st_ref[...], ost_ref[...]).astype(F32)
     turned = jnp.transpose(jnp.concatenate([stats, jnp.zeros((HD - 8, HD), F32)], axis=0))
     lse = share(core, jnp.concatenate([turned[:, i:i + 1] for i in range(4)], axis=0))
     dlt = share(core, jnp.concatenate([turned[:, i:i + 1] for i in range(4, 8)], axis=0))
@@ -201,11 +202,26 @@
     dk_ref[...], dv_ref[...] = key_side(sk, sv, q, g, stats)
 
 
+def stats_kernel(m_ref, o_ref):
+    o_ref[...] = jnp.sum(m_ref[:, 16:MAIN, :].astype(F32), axis=0).astype(BF)
+
+
+def gather_stats(rows):
+    return pl.pallas_call(
+        stats_kernel,
+        in_specs=[VM],
+        out_specs=VM,
+        out_shape=jax.ShapeDtypeStruct((8, HD), BF),
+        compiler_params=small(),
+        name="gather_stats",
+    )(rows)
+
+
 def near_grads(*args):
     part = jax.ShapeDtypeStruct((HALF, HD), F32)
     return pl.pallas_call(
         near_kernel,
-        in_specs=[SM] + [VM] * 5,
+        in_specs=[SM] + [VM] * 7,
         out_specs=[VM] * 5,
         out_shape=[jax.ShapeDtypeStruct((4, HALF, HD), BF)] + [part] * 4,
         compiler_params=small(),
@@ -214,9 +230,10 @@
     )(*args)
 
 
-def far_kernel(core_ref, a_ref, b_ref, oa_ref, ob_ref, sub_ref, col_ref, dq_ref, dk_ref, dv_ref, o_ref):
+def far_kernel(core_ref, a_ref, b_ref, st_ref, oa_ref, ob_ref, ost_ref, sub_ref, col_ref, dq_ref, dk_ref, dv_ref, o_ref):
     core = core_ref[0]
-    q, k, v, g, stats = whole(core, a_ref, b_ref, oa_ref, ob_ref)
+    q, k, v, g = whole(core, a_ref[...], b_ref[...], oa_ref[...], ob_ref[...])
+    stats = jnp.where(core == 0, st_ref[...], ost_ref[...]).astype(F32)
     lse, dlt = col_ref[:, 0:1], col_ref[:, 1:2]
     dq = dq_ref[...] + query_side(sub_ref[0], sub_ref[3], k, v, lse, dlt)
     dk, dv = key_side(sub_ref[1], sub_ref[2], q, g, stats)
@@ -228,7 +245,7 @@
 def far_grads(*args):
     return pl.pallas_call(
         far_kernel,
-        in_specs=[SM] + [VM] * 9,
+        in_specs=[SM] + [VM] * 11,
         out_specs=VM,
         out_shape=jax.ShapeDtypeStruct((GROUP, 24, HD), BF),
         compiler_params=small(),
@@ -269,7 +286,7 @@
 
 
 GROUPS = [
-    [place_of(z, column(half, p), c) for z in range(NZ) for p in range(2) for c in range(NC)]
+    [place_of(z, column(half, p), c) for z in reversed(range(NZ)) for p in range(2) for c in range(NC)]
     for half in range(2)
 ]
 
@@ -296,21 +313,25 @@
     seat = lax.axis_index("seq").astype(jnp.int32)
     x = seat // NC % NX
     core = (seat % NC).reshape(1)
-    pos = (seat // (NX * NC) * 4 + jnp.where(x < 2, x, NX - 1 - x) * 2 + seat % NC).reshape(1)
-    grad = move(grad_out, lambda s, x, c: (s - 1, x, c))
+    pos = ((NZ - 1 - seat // (NX * NC)) * 4 + jnp.where(x < 2, x, NX - 1 - x) * 2 + seat % NC).reshape(1)
     picked = pick_all(pos, offsets, log_sums, deltas, queries, key_rows, value_rows, grad_out)
     mine = swap(picked)
-    a, b = mine[:, :MAIN], mine[:, MAIN:]
+    a, b = mine[:, :16], mine[:, MAIN:]
     far_a = move(a, lambda s, x, c: (s, 3 - x, c))
     far_b = move(b, lambda s, x, c: (s - c, 3 - x, c))
     hop = move(b, lambda s, x, c: (s - 1, x, 1) if c == 1 else None)
     cross = move(b, lambda s, x, c: (s - c, x, 1 - c))
+    st = gather_stats(mine)
+    far_st = move(st, lambda s, x, c: (s, 3 - x, c))
     other_a = move(a, lambda s, x, c: (s, x, 1 - c))
+    other_st = move(st, lambda s, x, c: (s, x, 1 - c))
+    grad = move(grad_out, lambda s, x, c: (s - 1, x, c))
+    other_far_st = move(far_st, lambda s, x, c: (s, x, 1 - c))
     other_far_a = move(far_a, lambda s, x, c: (s, x, 1 - c))
     other_far_b = move(far_b, lambda s, x, c: (s, x, 1 - c))
     local = local_grads(offsets, queries, key_rows, value_rows, grad, log_sums, deltas)
-    part = near_grads(core, a, b, other_a, hop, cross)
-    back = swap(far_grads(core, far_a, far_b, other_far_a, other_far_b, *part))
+    part = near_grads(core, a, b, st, other_a, other_st, hop, cross)
+    back = swap(far_grads(core, far_a, far_b, far_st, other_far_a, other_far_b, other_far_st, *part))
     return tuple(combine(back, local))
 
 

time: 68.1 us -> 63.5 us (0.932)
  waiting for transfers between devices: 11.3 us -> 6.99 us
  starting transfers between devices: 17.2 us -> 19.3 us
  blocking collectives: 23.8 us -> 21.8 us
    ppermute x8 -> x11, waiting for transfers between devices: 8.77 us -> 6.23 us  [move(): return lax.ppermute(value, ('section', 'seq'), pairs)]
    all_to_all x1, starting transfers between devices: 3.78 us -> 6.31 us  [swap(): lax.all_to_all(value, 'seq', 0, 0, axis_index_groups=GROUPS, tiled=True)]
    all_to_all x1, blocking collectives: 23.8 us -> 21.8 us  [swap(): lax.all_to_all(value, 'seq', 0, 0, axis_index_groups=GROUPS, tiled=True)]
    all_to_all x1, waiting for transfers between devices: 2.56 us -> 0.76 us  [swap(): lax.all_to_all(value, 'seq', 0, 0, axis_index_groups=GROUPS, tiled=True)]
    ppermute x8 -> x11, starting transfers between devices: 13.4 us -> 13 us  [move(): return lax.ppermute(value, ('section', 'seq'), pairs)]
    pallas_call x2 -> x3, Pallas kernels: 2.52 us -> 2.46 us  [the longest x1 1.51 us: far_grads(): pl.pallas_call(far_kernel, in_specs=[SM] + [VM] * 11, out_specs=VM, out_s...]
  transfers between devices with their start and end apart: 9 -> 12, of which waited for: 3 -> 5; matrix products, arithmetic and copies ran while one was open for 0% -> 0% of each run, Pallas kernels for 11% -> 12%
where the time goes in v4:
time: 63.5 us; the launch traced here: 62.9 us
  blocking collectives  21.8 us (34%)
  starting transfers between devices  19.3 us (30%)
  Pallas kernels  12.1 us (19%)
  waiting for transfers between devices  6.99 us (11%)
  local copies, waits for them, and re-layouts  1.88 us (3%)
  between operations  0.85 us (1%)
    all_to_all x1, blocking collectives, swap(): lax.all_to_all(value, 'seq', 0, 0, axis_index_groups=GROUPS, tiled=True)  21.8 us
    ppermute x11, starting transfers between devices, move(): return lax.ppermute(value, ('section', 'seq'), pairs)  13 us
    all_to_all x1, starting transfers between devices, swap(): lax.all_to_all(value, 'seq', 0, 0, axis_index_groups=GROUPS, tiled=True)  6.31 us
    ppermute x11, waiting for transfers between devices, move(): return lax.ppermute(value, ('section', 'seq'), pairs)  6.23 us
    pallas_call x1, Pallas kernels, local_grads(): pl.pallas_call(local_kernel, grid=(4,), in_specs=[SM, wide, wide, wide, w...  4.99 us
    pallas_call x1, Pallas kernels, pick_all(): pl.pallas_call(pick_kernel, in_specs=[SM] + [raw] * 7, out_specs=VM, out_...  3 us
    unnamed x18, local copies, waits for them, and re-layouts  1.86 us
    pallas_call x1, Pallas kernels, combine(): pl.pallas_call(combine_kernel, in_specs=[VM] * 5, out_specs=[VM] * 3, out...  1.64 us
  transfers between devices with their start and end apart: 12, of which 5 were waited for; matrix products, arithmetic and copies ran while one was open for 0% of the time, Pallas kernels for 12%

profile of v4, /device:TPU:1, one launch (start us, length us, event | category | flops | bytes accessed | tf_op | source)
XLA Modules:
  0.0 62.9 jit_solution(1494781661971601534)
XLA Ops:
  0.7 3.0 %pick_all.1 = bf16[32,40,128]{2,1,0:T(8,128)(2,1)} custom-call(s32[1]{0:T(128)} %bitcast.1.pos_ref, s32[1,16]{1,0:T(1,128)} %off_ref.1, bf16[1,16,128]{2,1,0:T(8,128)(2,1)} %l_ref.1, bf16[1,16,128]{2,1,0:T(8,128)(2,1)} %d_ref.1, bf16[1,128,2048]{2,1,0:T(8,128)(2,1)} %q_ref.1, bf16[1,128,2048]{2,1,0:T(8,128)(2,1)} %k_ref.1, bf16[1,128,2048]{2,1,0:T(8,128)(2,1)} %v_ref.1, ...), custom_call_target="tpu_custom_call" | custom-call | tf_op jit(solution)/shard_map/pick_all/pallas_call | solution.py:98
  3.7 21.8 %all_to_all.10.m_ref = bf16[32,40,128]{2,1,0:T(8,128)(2,1)S(1)} all-to-all(bf16[32,40,128]{2,1,0:T(8,128)(2,1)} %pick_all.1), channel_id=1, replica_groups={{56,57,58,59,48,49,50,51,40,41,42,43,32,33,34,35,24,25,26,27,16,17,18,1..., dimensions={0} | all-to-all | bytes 655360 | tf_op jit(solution)/shard_map/all_to_all | solution.py:309
  25.5 0.5 collective-permute-start.6
  26.0 2.7 %collective-permute-start.10 = (bf16[1,128,2048]{2,1,0:T(8,128)(2,1)S(1)}, bf16[1,128,2048]{2,1,0:T(8,128)(2,1)S(1)}, u32[]{:S(2)}, u32[]{:S(2)}) collective-permute-start(bf16[1,128,2048]{2,1,0:T(8,128)(2,1)S(1)} %copy-done.8), channel_id=1, source_target_pairs={{0,192},{1,193},{2,194},{3,195},{4,196},{5,197},{6,198},{7,199},{8... | collective-permute-start | bytes 1572872 | tf_op jit(solution)/shard_map/ppermute | solution.py:305
  28.8 1.8 %collective-permute-start = (bf16[32,16,128]{2,1,0:T(8,128)(2,1)S(1)}, bf16[32,16,128]{2,1,0:T(8,128)(2,1)S(1)}, u32[]{:S(2)}, u32[]{:S(2)}) collective-permute-start(bf16[32,16,128]{2,1,0:T(8,128)(2,1)S(1)} %get-tuple-element.22.a_ref), channel_id=1, source_target_pairs={{0,6},{1,7},{2,4},{3,5},{4,2},{5,3},{6,0},{7,1},{8,14},{9,15},{10,... | collective-permute-start | bytes 393224 | tf_op jit(solution)/shard_map/ppermute | solution.py:305
  30.6 1.1 %collective-permute-start.1 = (bf16[32,16,128]{2,1,0:T(8,128)(2,1)S(1)}, bf16[32,16,128]{2,1,0:T(8,128)(2,1)S(1)}, u32[]{:S(2)}, u32[]{:S(2)}) collective-permute-start(bf16[32,16,128]{2,1,0:T(8,128)(2,1)S(1)} %get-tuple-element.21.b_ref), channel_id=1, source_target_pairs={{0,6},{1,199},{2,4},{3,197},{4,2},{5,195},{6,0},{7,193},{8,14},{9,... | collective-permute-start | bytes 393224 | tf_op jit(solution)/shard_map/ppermute | solution.py:305
  31.7 0.8 %collective-permute-start.7 = (bf16[8,128]{1,0:T(8,128)(2,1)S(1)}, bf16[8,128]{1,0:T(8,128)(2,1)S(1)}, u32[]{:S(2)}, u32[]{:S(2)}) collective-permute-start(bf16[8,128]{1,0:T(8,128)(2,1)S(1)} %gather_stats.1.st_ref), channel_id=1, source_target_pairs={{0,1},{1,0},{2,3},{3,2},{4,5},{5,4},{6,7},{7,6},{8,9},{9,8},{10,11... | collective-permute-start | bytes 6152 | tf_op jit(solution)/shard_map/ppermute | solution.py:305
  32.5 0.8 %collective-permute-done.7.ost_ref = bf16[8,128]{1,0:T(8,128)(2,1)S(1)} collective-permute-done((bf16[8,128]{1,0:T(8,128)(2,1)S(1)}, bf16[8,128]{1,0:T(8,128)(2,1)S(1)}, u32[]{:S(2)}, u32[]{:S(2)}) %collective-permute-start.7) | collective-permute-done | bytes 2080 | tf_op jit(solution)/shard_map/ppermute | solution.py:305
  33.3 1.8 %collective-permute-start.2 = (bf16[8,128]{1,0:T(8,128)(2,1)S(1)}, bf16[8,128]{1,0:T(8,128)(2,1)S(1)}, u32[]{:S(2)}, u32[]{:S(2)}) collective-permute-start(bf16[8,128]{1,0:T(8,128)(2,1)S(1)} %gather_stats.1.st_ref), channel_id=1, source_target_pairs={{0,6},{1,7},{2,4},{3,5},{4,2},{5,3},{6,0},{7,1},{8,14},{9,15},{10,... | collective-permute-start | bytes 6152 | tf_op jit(solution)/shard_map/ppermute | solution.py:305
  35.1 2.4 %collective-permute-done.2.st_ref = bf16[8,128]{1,0:T(8,128)(2,1)S(1)} collective-permute-done((bf16[8,128]{1,0:T(8,128)(2,1)S(1)}, bf16[8,128]{1,0:T(8,128)(2,1)S(1)}, u32[]{:S(2)}, u32[]{:S(2)}) %collective-permute-start.2) | collective-permute-done | bytes 2080 | tf_op jit(solution)/shard_map/ppermute | solution.py:305
  37.5 1.6 %collective-permute-start.9 = (bf16[32,16,128]{2,1,0:T(8,128)(2,1)S(1)}, bf16[32,16,128]{2,1,0:T(8,128)(2,1)S(1)}, u32[]{:S(2)}, u32[]{:S(2)}) collective-permute-start(bf16[32,16,128]{2,1,0:T(8,128)(2,1)S(1)} %get-tuple-element.21.b_ref), channel_id=1, source_target_pairs={{0,1},{1,192},{2,3},{3,194},{4,5},{5,196},{6,7},{7,198},{8,9},{9,2... | collective-permute-start | bytes 393224 | tf_op jit(solution)/shard_map/ppermute | solution.py:305
  39.1 2.1 %collective-permute-start.8 = (bf16[32,16,128]{2,1,0:T(8,128)(2,1)S(1)}, bf16[32,16,128]{2,1,0:T(8,128)(2,1)S(1)}, u32[]{:S(2)}, u32[]{:S(2)}) collective-permute-start(bf16[32,16,128]{2,1,0:T(8,128)(2,1)S(1)} %get-tuple-element.21.b_ref), channel_id=1, source_target_pairs={{1,193},{3,195},{5,197},{7,199},{9,201},{11,203},{13,205},{15,207}... | collective-permute-start | bytes 393224 | tf_op jit(solution)/shard_map/ppermute | solution.py:305
  41.2 0.1 collective-permute-start.3
  41.3 0.5 collective-permute-start.4
  41.8 1.5 %collective-permute-done.9.cross_ref = bf16[32,16,128]{2,1,0:T(8,128)(2,1)S(1)} collective-permute-done((bf16[32,16,128]{2,1,0:T(8,128)(2,1)S(1)}, bf16[32,16,128]{2,1,0:T(8,128)(2,1)S(1)}, u32[]{:S(2)}, u32[]{:S(2)}) %collective-permute-start.9) | collective-permute-done | bytes 131104 | tf_op jit(solution)/shard_map/ppermute | solution.py:305
  43.3 1.5 %collective-permute-done.8.hop_ref = bf16[32,16,128]{2,1,0:T(8,128)(2,1)S(1)} collective-permute-done((bf16[32,16,128]{2,1,0:T(8,128)(2,1)S(1)}, bf16[32,16,128]{2,1,0:T(8,128)(2,1)S(1)}, u32[]{:S(2)}, u32[]{:S(2)}) %collective-permute-start.8) | collective-permute-done | bytes 131104 | tf_op jit(solution)/shard_map/ppermute | solution.py:305
  44.8 0.9 %near_grads.1 = (bf16[4,256,128]{2,1,0:T(8,128)(2,1)S(1)}, f32[256,128]{1,0:T(8,128)S(1)}, f32[256,128]{1,0:T(8,128)S(1)}, f32[256,128]{1,0:T(8,128)S(1)}, f32[256,128]{1,0:T(8,128)S(1)}) custom-call(s32[1]{0:T(128)} %bitcast.core_ref, bf16[32,16,128]{2,1,0:T(8,128)(2,1)S(1)} %get-tuple-element.22.a_ref, bf16[32,16,128]{2,1,0:T(8,128)(2,1)S(1)} %get-tuple-element.21.b_ref, ...), custom_call_target="tpu_custom_call" | custom-call | flops 469762048 | bytes 1572864 | tf_op jit(solution)/shard_map/near_grads/pallas_call | solution.py:222
  45.8 1.5 %far_grads.1 = bf16[32,24,128]{2,1,0:T(8,128)(2,1)} custom-call(s32[1]{0:T(128)} %bitcast.core_ref, bf16[32,16,128]{2,1,0:T(8,128)(2,1)S(1)} %collective-permute-done.a_ref, bf16[32,16,128]{2,1,0:T(8,128)(2,1)S(1)} %collective-permute-done.1.b_ref, bf16[8,128]{1,0:T(8,128)(2,1)S(1)} %collective-permute-done.2.st_ref, ...), custom_call_target="tpu_custom_call" | custom-call | tf_op jit(solution)/shard_map/far_grads/pallas_call | solution.py:246
  47.3 6.3 %all-to-all-start.1 = ((bf16[32,24,128]{2,1,0:T(8,128)(2,1)}), bf16[32,24,128]{2,1,0:T(8,128)(2,1)S(1)}, u32[]{:S(2)}, u32[]{:S(2)}) async-start(bf16[32,24,128]{2,1,0:T(8,128)(2,1)} %far_grads.1), calls=%async_computation.1 | async-start | bytes 393216 | tf_op jit(solution)/shard_map/all_to_all | solution.py:309
  53.6 0.8 %copy-done.6 = bf16[1,128,2048]{2,1,0:T(8,128)(2,1)} copy-done((bf16[1,128,2048]{2,1,0:T(8,128)(2,1)}, bf16[1,128,2048]{2,1,0:T(8,128)(2,1)S(1)}, u32[]{:S(2)}) %copy-start.6) | copy-done | bytes 524312
  54.5 1.0 %copy-done.7 = bf16[1,128,2048]{2,1,0:T(8,128)(2,1)S(1)} copy-done((bf16[1,128,2048]{2,1,0:T(8,128)(2,1)S(1)}, bf16[1,128,2048]{2,1,0:T(8,128)(2,1)}, u32[]{:S(2)}) %copy-start.7) | copy-done | bytes 524312
  55.5 5.0 %local_grads.1 = (bf16[128,2048]{1,0:T(8,128)(2,1)S(1)}, bf16[128,2048]{1,0:T(8,128)(2,1)S(1)}, bf16[128,2048]{1,0:T(8,128)(2,1)S(1)}, s32[16,128]{1,0:T(8,128)S(1)}) custom-call(s32[1,16]{1,0:T(1,128)S(1)} %copy-done.5, bf16[1,128,2048]{2,1,0:T(8,128)(2,1)S(1)} %copy-done, bf16[1,128,2048]{2,1,0:T(8,128)(2,1)S(1)} %copy-done.1, ...), custom_call_target="tpu_custom_call" | custom-call | flops 1342177280 | bytes 3670016 | tf_op jit(solution)/shard_map/local_grads/pallas_call | solution.py:142
  60.5 0.8 %all-to-all-done.1.w_ref = bf16[32,24,128]{2,1,0:T(8,128)(2,1)S(1)} async-done(((bf16[32,24,128]{2,1,0:T(8,128)(2,1)}), bf16[32,24,128]{2,1,0:T(8,128)(2,1)S(1)}, u32[]{:S(2)}, u32[]{:S(2)}) %all-to-all-start.1) | async-done | bytes 196640 | tf_op jit(solution)/shard_map/all_to_all | solution.py:309
  61.3 1.6 %combine.1 = (bf16[1,128,2048]{2,1,0:T(8,128)(2,1)}, bf16[1,128,2048]{2,1,0:T(8,128)(2,1)}, bf16[1,128,2048]{2,1,0:T(8,128)(2,1)}) custom-call(bf16[32,24,128]{2,1,0:T(8,128)(2,1)S(1)} %all-to-all-done.1.w_ref, bf16[128,2048]{1,0:T(8,128)(2,1)S(1)} %get-tuple-element.17.dq_ref, bf16[128,2048]{1,0:T(8,128)(2,1)S(1)} %get-tuple-element.18.dk_ref, ...), custom_call_target="tpu_custom_call" | custom-call | tf_op jit(solution)/shard_map/combine/pallas_call | solution.py:270
  (26 shorter events, 0.1 us)
Async XLA Ops:
  3.7 22.4 %copy-start.8 = (bf16[1,128,2048]{2,1,0:T(8,128)(2,1)S(1)}, bf16[1,128,2048]{2,1,0:T(8,128)(2,1)}, u32[]{:S(2)}) copy-start(bf16[1,128,2048]{2,1,0:T(8,128)(2,1)} %g_hbm.1) | copy-start | bytes 1572868
  25.5 13.6 %collective-permute-start.6 = (bf16[32,16,128]{2,1,0:T(8,128)(2,1)S(1)}, bf16[32,16,128]{2,1,0:T(8,128)(2,1)S(1)}, u32[]{:S(2)}, u32[]{:S(2)}) collective-permute-start(bf16[32,16,128]{2,1,0:T(8,128)(2,1)S(1)} %get-tuple-element.22.a_ref), channel_id=1, source_target_pairs={{0,1},{1,0},{2,3},{3,2},{4,5},{5,4},{6,7},{7,6},{8,9},{9,8},{10,11... | collective-permute-start | bytes 393224 | tf_op jit(solution)/shard_map/ppermute | solution.py:305
  26.0 27.6 %collective-permute-start.10 = (bf16[1,128,2048]{2,1,0:T(8,128)(2,1)S(1)}, bf16[1,128,2048]{2,1,0:T(8,128)(2,1)S(1)}, u32[]{:S(2)}, u32[]{:S(2)}) collective-permute-start(bf16[1,128,2048]{2,1,0:T(8,128)(2,1)S(1)} %copy-done.8), channel_id=1, source_target_pairs={{0,192},{1,193},{2,194},{3,195},{4,196},{5,197},{6,198},{7,199},{8... | collective-permute-start | bytes 1572872 | tf_op jit(solution)/shard_map/ppermute | solution.py:305
  28.8 12.4 %collective-permute-start = (bf16[32,16,128]{2,1,0:T(8,128)(2,1)S(1)}, bf16[32,16,128]{2,1,0:T(8,128)(2,1)S(1)}, u32[]{:S(2)}, u32[]{:S(2)}) collective-permute-start(bf16[32,16,128]{2,1,0:T(8,128)(2,1)S(1)} %get-tuple-element.22.a_ref), channel_id=1, source_target_pairs={{0,6},{1,7},{2,4},{3,5},{4,2},{5,3},{6,0},{7,1},{8,14},{9,15},{10,... | collective-permute-start | bytes 393224 | tf_op jit(solution)/shard_map/ppermute | solution.py:305
  30.6 10.7 %collective-permute-start.1 = (bf16[32,16,128]{2,1,0:T(8,128)(2,1)S(1)}, bf16[32,16,128]{2,1,0:T(8,128)(2,1)S(1)}, u32[]{:S(2)}, u32[]{:S(2)}) collective-permute-start(bf16[32,16,128]{2,1,0:T(8,128)(2,1)S(1)} %get-tuple-element.21.b_ref), channel_id=1, source_target_pairs={{0,6},{1,199},{2,4},{3,197},{4,2},{5,195},{6,0},{7,193},{8,14},{9,... | collective-permute-start | bytes 393224 | tf_op jit(solution)/shard_map/ppermute | solution.py:305
  31.7 1.7 %collective-permute-start.7 = (bf16[8,128]{1,0:T(8,128)(2,1)S(1)}, bf16[8,128]{1,0:T(8,128)(2,1)S(1)}, u32[]{:S(2)}, u32[]{:S(2)}) collective-permute-start(bf16[8,128]{1,0:T(8,128)(2,1)S(1)} %gather_stats.1.st_ref), channel_id=1, source_target_pairs={{0,1},{1,0},{2,3},{3,2},{4,5},{5,4},{6,7},{7,6},{8,9},{9,8},{10,11... | collective-permute-start | bytes 6152 | tf_op jit(solution)/shard_map/ppermute | solution.py:305
  33.3 4.2 %collective-permute-start.2 = (bf16[8,128]{1,0:T(8,128)(2,1)S(1)}, bf16[8,128]{1,0:T(8,128)(2,1)S(1)}, u32[]{:S(2)}, u32[]{:S(2)}) collective-permute-start(bf16[8,128]{1,0:T(8,128)(2,1)S(1)} %gather_stats.1.st_ref), channel_id=1, source_target_pairs={{0,6},{1,7},{2,4},{3,5},{4,2},{5,3},{6,0},{7,1},{8,14},{9,15},{10,... | collective-permute-start | bytes 6152 | tf_op jit(solution)/shard_map/ppermute | solution.py:305
  37.5 5.8 %collective-permute-start.9 = (bf16[32,16,128]{2,1,0:T(8,128)(2,1)S(1)}, bf16[32,16,128]{2,1,0:T(8,128)(2,1)S(1)}, u32[]{:S(2)}, u32[]{:S(2)}) collective-permute-start(bf16[32,16,128]{2,1,0:T(8,128)(2,1)S(1)} %get-tuple-element.21.b_ref), channel_id=1, source_target_pairs={{0,1},{1,192},{2,3},{3,194},{4,5},{5,196},{6,7},{7,198},{8,9},{9,2... | collective-permute-start | bytes 393224 | tf_op jit(solution)/shard_map/ppermute | solution.py:305
  39.1 5.7 %collective-permute-start.8 = (bf16[32,16,128]{2,1,0:T(8,128)(2,1)S(1)}, bf16[32,16,128]{2,1,0:T(8,128)(2,1)S(1)}, u32[]{:S(2)}, u32[]{:S(2)}) collective-permute-start(bf16[32,16,128]{2,1,0:T(8,128)(2,1)S(1)} %get-tuple-element.21.b_ref), channel_id=1, source_target_pairs={{1,193},{3,195},{5,197},{7,199},{9,201},{11,203},{13,205},{15,207}... | collective-permute-start | bytes 393224 | tf_op jit(solution)/shard_map/ppermute | solution.py:305
  41.2 4.5 %collective-permute-start.3 = (bf16[32,16,128]{2,1,0:T(8,128)(2,1)S(1)}, bf16[32,16,128]{2,1,0:T(8,128)(2,1)S(1)}, u32[]{:S(2)}, u32[]{:S(2)}) collective-permute-start(bf16[32,16,128]{2,1,0:T(8,128)(2,1)S(1)} %collective-permute-done.a_ref), channel_id=1, source_target_pairs={{0,1},{1,0},{2,3},{3,2},{4,5},{5,4},{6,7},{7,6},{8,9},{9,8},{10,11... | collective-permute-start | bytes 393224 | tf_op jit(solution)/shard_map/ppermute | solution.py:305
  41.3 4.4 %collective-permute-start.4 = (bf16[32,16,128]{2,1,0:T(8,128)(2,1)S(1)}, bf16[32,16,128]{2,1,0:T(8,128)(2,1)S(1)}, u32[]{:S(2)}, u32[]{:S(2)}) collective-permute-start(bf16[32,16,128]{2,1,0:T(8,128)(2,1)S(1)} %collective-permute-done.1.b_ref), channel_id=1, source_target_pairs={{0,1},{1,0},{2,3},{3,2},{4,5},{5,4},{6,7},{7,6},{8,9},{9,8},{10,11... | collective-permute-start | bytes 393224 | tf_op jit(solution)/shard_map/ppermute | solution.py:305
  43.3 2.4 %collective-permute-start.5 = (bf16[8,128]{1,0:T(8,128)(2,1)S(1)}, bf16[8,128]{1,0:T(8,128)(2,1)S(1)}, u32[]{:S(2)}, u32[]{:S(2)}) collective-permute-start(bf16[8,128]{1,0:T(8,128)(2,1)S(1)} %collective-permute-done.2.st_ref), channel_id=1, source_target_pairs={{0,1},{1,0},{2,3},{3,2},{4,5},{5,4},{6,7},{7,6},{8,9},{9,8},{10,11... | collective-permute-start | bytes 6152 | tf_op jit(solution)/shard_map/ppermute | solution.py:305
  45.7 8.7 %copy-start = (bf16[1,128,2048]{2,1,0:T(8,128)(2,1)S(1)}, bf16[1,128,2048]{2,1,0:T(8,128)(2,1)}, u32[]{:S(2)}) copy-start(bf16[1,128,2048]{2,1,0:T(8,128)(2,1)} %q_ref.1) | copy-start | bytes 1572868
  45.8 8.7 %copy-start.1 = (bf16[1,128,2048]{2,1,0:T(8,128)(2,1)S(1)}, bf16[1,128,2048]{2,1,0:T(8,128)(2,1)}, u32[]{:S(2)}) copy-start(bf16[1,128,2048]{2,1,0:T(8,128)(2,1)} %k_ref.1) | copy-start | bytes 1572868
  45.8 8.7 %copy-start.2 = (bf16[1,128,2048]{2,1,0:T(8,128)(2,1)S(1)}, bf16[1,128,2048]{2,1,0:T(8,128)(2,1)}, u32[]{:S(2)}) copy-start(bf16[1,128,2048]{2,1,0:T(8,128)(2,1)} %v_ref.1) | copy-start | bytes 1572868
  47.3 7.1 %copy-start.3 = (bf16[1,16,128]{2,1,0:T(8,128)(2,1)S(1)}, bf16[1,16,128]{2,1,0:T(8,128)(2,1)}, u32[]{:S(2)}) copy-start(bf16[1,16,128]{2,1,0:T(8,128)(2,1)} %l_ref.1) | copy-start | bytes 12292
  47.3 7.1 %copy-start.4 = (bf16[1,16,128]{2,1,0:T(8,128)(2,1)S(1)}, bf16[1,16,128]{2,1,0:T(8,128)(2,1)}, u32[]{:S(2)}) copy-start(bf16[1,16,128]{2,1,0:T(8,128)(2,1)} %d_ref.1) | copy-start | bytes 12292
  47.3 7.2 %copy-start.5 = (s32[1,16]{1,0:T(1,128)S(1)}, s32[1,16]{1,0:T(1,128)}, u32[]{:S(2)}) copy-start(s32[1,16]{1,0:T(1,128)} %off_ref.1) | copy-start | bytes 196
  47.3 14.0 %all-to-all-start.1 = ((bf16[32,24,128]{2,1,0:T(8,128)(2,1)}), bf16[32,24,128]{2,1,0:T(8,128)(2,1)S(1)}, u32[]{:S(2)}, u32[]{:S(2)}) async-start(bf16[32,24,128]{2,1,0:T(8,128)(2,1)} %far_grads.1), calls=%async_computation.1 | async-start | bytes 393216 | tf_op jit(solution)/shard_map/all_to_all | solution.py:309
  53.6 0.8 %copy-start.6 = (bf16[1,128,2048]{2,1,0:T(8,128)(2,1)}, bf16[1,128,2048]{2,1,0:T(8,128)(2,1)S(1)}, u32[]{:S(2)}) copy-start(bf16[1,128,2048]{2,1,0:T(8,128)(2,1)S(1)} %collective-permute-done.10.g_ref) | copy-start | bytes 1572868
  54.5 1.0 %copy-start.7 = (bf16[1,128,2048]{2,1,0:T(8,128)(2,1)S(1)}, bf16[1,128,2048]{2,1,0:T(8,128)(2,1)}, u32[]{:S(2)}) copy-start(bf16[1,128,2048]{2,1,0:T(8,128)(2,1)} %copy-done.6) | copy-start | bytes 1572868

commit v5 on v3

--- a/solution.py
+++ b/solution.py
@@ -36,10 +36,10 @@
     return lax.dot_general(a, b, (((0,), (0,)), ((), ())), preferred_element_type=F32)
 
 
-def pick(x, off):
-    t = x.astype(F32).reshape(PICK, RATE, HD)
-    row = lax.broadcasted_iota(jnp.int32, (PICK, RATE, HD), 1)
-    return jnp.sum(jnp.where(row == off, t, 0.0), axis=1).astype(BF)
+def chooser(off):
+    row = lax.broadcasted_iota(jnp.int32, (PICK, TOK), 0)
+    tok = lax.broadcasted_iota(jnp.int32, (PICK, TOK), 1)
+    return jnp.where(tok == row * RATE + off, 1.0, 0.0).astype(BF)
 
 
 def small(mib=12):
@@ -68,11 +68,12 @@
     dst = lax.broadcasted_iota(jnp.int32, (TOK, TOK), 1)
     place = jnp.where(dst == (n % 8) * PICK + src // RATE, 1.0, 0.0).astype(BF)
     loads[0].wait()
+    choose = [chooser(off_ref[0, h]) for h in range(HEADS)]
     for part, core, first in ((0, 0, 0), (1, 0, MAIN), (2, 1, 0), (3, 1, MAIN)):
         loads[1 + part].wait()
         for h in range(HEADS):
-            rows = pick(x_ref[part, :, h * HD:(h + 1) * HD], off_ref[0, h])
-            o_ref[2 * h + core, first:first + 16] = rows
+            rows = dot(choose[h], x_ref[part, :, h * HD:(h + 1) * HD])
+            o_ref[2 * h + core, first:first + 16] = rows.astype(BF)
     loads[5].wait()
     loads[6].wait()
     head = lax.broadcasted_iota(jnp.int32, (HEADS, TOK), 0)
@@ -110,30 +111,56 @@
     )(pos, offsets, lse, delta, query, key, value, grad)
 
 
-def local_kernel(off_ref, q_ref, k_ref, v_ref, g_ref, l_ref, d_ref, dq_ref, dk_ref, dv_ref, offs_ref, st_ref):
+def score_kernel(off_ref, q_ref, k_ref, l_ref, p_ref, offs_ref, st_ref):
     step = pl.program_id(0)
 
     @pl.when(step == 0)
     def _():
-        st_ref[0] = l_ref[0].astype(F32)
-        st_ref[1] = d_ref[0].astype(F32)
+        st_ref[...] = l_ref[0].astype(F32)
         for h in range(HEADS):
             offs_ref[h:h + 1, :] = jnp.full((1, TOK), off_ref[0, h], jnp.int32)
 
-    base = pl.multiple_of(step * 4, 4)
-    lses = st_ref[0, pl.ds(base, 4), :]
-    dlts = st_ref[1, pl.ds(base, 4), :]
+    lses = st_ref[pl.ds(pl.multiple_of(step * 4, 4), 4), :]
+    for i in range(4):
+        cols = slice(i * HD, (i + 1) * HD)
+        p_ref[i] = jnp.exp(dot_t(k_ref[0, :, cols], q_ref[0, :, cols]) * SCALE - lses[i:i + 1])
+
+
+def local_scores(offsets, query, key, lse):
+    wide = pl.BlockSpec((1, TOK, 4 * HD), lambda i: (0, 0, i))
+    stat = pl.BlockSpec((1, HEADS, TOK), lambda i: (0, 0, 0))
+    return pl.pallas_call(
+        score_kernel,
+        grid=(4,),
+        in_specs=[SM, wide, wide, stat],
+        out_specs=[pl.BlockSpec((4, TOK, TOK), lambda i: (i, 0, 0)), pl.BlockSpec((HEADS, TOK), lambda i: (0, 0))],
+        out_shape=[jax.ShapeDtypeStruct((HEADS, TOK, TOK), F32), jax.ShapeDtypeStruct((HEADS, TOK), jnp.int32)],
+        scratch_shapes=[pltpu.VMEM((HEADS, TOK), F32)],
+        compiler_params=small(),
+        cost_estimate=pl.CostEstimate(flops=16 * 2 * 128 ** 3 * 4, bytes_accessed=2097152, transcendentals=262144),
+        name="local_scores",
+    )(offsets, query, key, lse)
+
+
+def local_kernel(p_ref, q_ref, k_ref, v_ref, g_ref, d_ref, dq_ref, dk_ref, dv_ref, st_ref):
+    step = pl.program_id(0)
+
+    @pl.when(step == 0)
+    def _():
+        st_ref[...] = d_ref[0].astype(F32)
+
+    dlts = st_ref[pl.ds(pl.multiple_of(step * 4, 4), 4), :]
     for i in range(4):
         cols = slice(i * HD, (i + 1) * HD)
         q, k, v, g = q_ref[0, :, cols], k_ref[0, :, cols], v_ref[0, :, cols], g_ref[0, :, cols]
-        p = jnp.exp(dot_t(k, q) * SCALE - lses[i:i + 1])
+        p = p_ref[i]
         ds = (p * (dot_t(v, g) - dlts[i:i + 1])).astype(BF)
         dv_ref[:, cols] = dot(p.astype(BF), g).astype(BF)
         dk_ref[:, cols] = (dot(ds, q) * SCALE).astype(BF)
         dq_ref[:, cols] = (dot_l(ds, k) * SCALE).astype(BF)
 
 
-def local_grads(offsets, query, key, value, grad, lse, delta):
+def local_grads(probs, query, key, value, grad, delta):
     wide = pl.BlockSpec((1, TOK, 4 * HD), lambda i: (0, 0, i))
     out = pl.BlockSpec((TOK, 4 * HD), lambda i: (0, i))
     stat = pl.BlockSpec((1, HEADS, TOK), lambda i: (0, 0, 0))
@@ -141,14 +168,14 @@
     return pl.pallas_call(
         local_kernel,
         grid=(4,),
-        in_specs=[SM, wide, wide, wide, wide, stat, stat],
-        out_specs=[out, out, out, pl.BlockSpec((HEADS, TOK), lambda i: (0, 0))],
-        out_shape=[shape, shape, shape, jax.ShapeDtypeStruct((HEADS, TOK), jnp.int32)],
-        scratch_shapes=[pltpu.VMEM((2, HEADS, TOK), F32)],
-        compiler_params=small(),
-        cost_estimate=pl.CostEstimate(flops=16 * 5 * 2 * 128 ** 3 * 4, bytes_accessed=3670016, transcendentals=262144),
+        in_specs=[pl.BlockSpec((4, TOK, TOK), lambda i: (i, 0, 0)), wide, wide, wide, wide, stat],
+        out_specs=[out, out, out],
+        out_shape=[shape, shape, shape],
+        scratch_shapes=[pltpu.VMEM((HEADS, TOK), F32)],
+        compiler_params=small(),
+        cost_estimate=pl.CostEstimate(flops=16 * 4 * 2 * 128 ** 3 * 4, bytes_accessed=4718592, transcendentals=0),
         name="local_grads",
-    )(offsets, query, key, value, grad, lse, delta)
+    )(probs, query, key, value, grad, delta)
 
 
 def query_side(q, g, k, v, lse, dlt):
@@ -171,12 +198,15 @@
 
 def whole(core, mine_a, mine_b, other_a, other_b):
     zero = core == 0
-    q = jnp.where(zero, mine_a[:, 0:16], other_a[:, 0:16])
-    v = jnp.where(zero, other_a[:, 0:16], mine_a[:, 0:16])
-    st = jnp.sum(jnp.where(zero, mine_a[:, 16:MAIN], other_a[:, 16:MAIN]).astype(F32), axis=0)
-    k = jnp.where(zero, mine_b[...], other_b[...])
-    g = jnp.where(zero, other_b[...], mine_b[...])
-    return flat(q), flat(k), flat(v), flat(g), st
+    q = jnp.where(zero, mine_a, other_a)
+    v = jnp.where(zero, other_a, mine_a)
+    k = jnp.where(zero, mine_b, other_b)
+    g = jnp.where(zero, other_b, mine_b)
+    return flat(q), flat(k), flat(v), flat(g)
+
+
+def stats_of(core, mine_a, other_a):
+    return jnp.sum(jnp.where(core == 0, mine_a[:, 16:MAIN], other_a[:, 16:MAIN]).astype(F32), axis=0)
 
 
 def share(core, rows):
@@ -188,7 +218,8 @@
 def near_kernel(core_ref, a_ref, b_ref, oa_ref, hop_ref, cross_ref, sub_ref, col_ref, dq_ref, dk_ref, dv_ref):
     core = core_ref[0]
     mine_b = jnp.where(core == 0, b_ref[...], hop_ref[...])
-    q, k, v, g, stats = whole(core, a_ref, mine_b, oa_ref, cross_ref)
+    q, k, v, g = whole(core, a_ref[:, 0:16], mine_b, oa_ref[:, 0:16], cross_ref[...])
+    stats = stats_of(core, a_ref, oa_ref)
     turned = jnp.transpose(jnp.concatenate([stats, jnp.zeros((HD - 8, HD), F32)], axis=0))
     lse = share(core, jnp.concatenate([turned[:, i:i + 1] for i in range(4)], axis=0))
     dlt = share(core, jnp.concatenate([turned[:, i:i + 1] for i in range(4, 8)], axis=0))
@@ -216,7 +247,8 @@
 
 def far_kernel(core_ref, a_ref, b_ref, oa_ref, ob_ref, sub_ref, col_ref, dq_ref, dk_ref, dv_ref, o_ref):
     core = core_ref[0]
-    q, k, v, g, stats = whole(core, a_ref, b_ref, oa_ref, ob_ref)
+    q, k, v, g = whole(core, a_ref[:, 0:16], b_ref[...], oa_ref[:, 0:16], ob_ref[...])
+    stats = stats_of(core, a_ref, oa_ref)
     lse, dlt = col_ref[:, 0:1], col_ref[:, 1:2]
     dq = dq_ref[...] + query_side(sub_ref[0], sub_ref[3], k, v, lse, dlt)
     dk, dv = key_side(sub_ref[1], sub_ref[2], q, g, stats)
@@ -269,7 +301,7 @@
 
 
 GROUPS = [
-    [place_of(z, column(half, p), c) for z in range(NZ) for p in range(2) for c in range(NC)]
+    [place_of(z, column(half, p), c) for z in reversed(range(NZ)) for p in range(2) for c in range(NC)]
     for half in range(2)
 ]
 
@@ -296,22 +328,23 @@
     seat = lax.axis_index("seq").astype(jnp.int32)
     x = seat // NC % NX
     core = (seat % NC).reshape(1)
-    pos = (seat // (NX * NC) * 4 + jnp.where(x < 2, x, NX - 1 - x) * 2 + seat % NC).reshape(1)
-    grad = move(grad_out, lambda s, x, c: (s - 1, x, c))
+    pos = ((NZ - 1 - seat // (NX * NC)) * 4 + jnp.where(x < 2, x, NX - 1 - x) * 2 + seat % NC).reshape(1)
     picked = pick_all(pos, offsets, log_sums, deltas, queries, key_rows, value_rows, grad_out)
     mine = swap(picked)
+    grad = move(grad_out, lambda s, x, c: (s - 1, x, c))
+    probs, offs = local_scores(offsets, queries, key_rows, log_sums)
     a, b = mine[:, :MAIN], mine[:, MAIN:]
     far_a = move(a, lambda s, x, c: (s, 3 - x, c))
     far_b = move(b, lambda s, x, c: (s - c, 3 - x, c))
+    other_a = move(a, lambda s, x, c: (s, x, 1 - c))
     hop = move(b, lambda s, x, c: (s - 1, x, 1) if c == 1 else None)
     cross = move(b, lambda s, x, c: (s - c, x, 1 - c))
-    other_a = move(a, lambda s, x, c: (s, x, 1 - c))
     other_far_a = move(far_a, lambda s, x, c: (s, x, 1 - c))
     other_far_b = move(far_b, lambda s, x, c: (s, x, 1 - c))
-    local = local_grads(offsets, queries, key_rows, value_rows, grad, log_sums, deltas)
+    local = local_grads(probs, queries, key_rows, value_rows, grad, deltas)
     part = near_grads(core, a, b, other_a, hop, cross)
     back = swap(far_grads(core, far_a, far_b, other_far_a, other_far_b, *part))
-    return tuple(combine(back, local))
+    return tuple(combine(back, (*local, offs)))
 
 
 def solution(mesh):

time: 68.1 us -> 65.3 us (0.959)
  starting transfers between devices: 17.2 us -> 20 us
  blocking collectives: 23.8 us -> 21.8 us
  local copies, waits for them, and re-layouts: 1.89 us -> 0.07 us
  waiting for transfers between devices: 11.3 us -> 9.7 us
    all_to_all x1, starting transfers between devices: 3.78 us -> 6.24 us  [swap(): lax.all_to_all(value, 'seq', 0, 0, axis_index_groups=GROUPS, tiled=True)]
    all_to_all x1, blocking collectives: 23.8 us -> 21.8 us  [swap(): lax.all_to_all(value, 'seq', 0, 0, axis_index_groups=GROUPS, tiled=True)]
    unnamed x18 -> x14, local copies, waits for them, and re-layouts: 1.86 us -> 0.04 us
    ppermute x8, waiting for transfers between devices: 8.77 us -> 7.44 us  [move(): return lax.ppermute(value, ('section', 'seq'), pairs)]
    pallas_call x1 -> x2, Pallas kernels: 4.99 us -> 5.26 us  [the longest x1 3.64 us: local_grads(): pl.pallas_call(local_kernel, grid=(4,), in_specs=[pl.BlockSpec((4, TOK, T...]
  transfers between devices with their start and end apart: 9 -> 9, of which waited for: 3 -> 3; matrix products, arithmetic and copies ran while one was open for 0% -> 0% of each run, Pallas kernels for 11% -> 12%
where the time goes in v5:
time: 65.3 us; the launch traced here: 64.9 us
  blocking collectives  21.8 us (33%)
  starting transfers between devices  20 us (31%)
  Pallas kernels  12.4 us (19%)
  waiting for transfers between devices  9.7 us (15%)
  between operations  0.86 us (1%)
    all_to_all x1, blocking collectives, swap(): lax.all_to_all(value, 'seq', 0, 0, axis_index_groups=GROUPS, tiled=True)  21.8 us
    ppermute x8, starting transfers between devices, move(): return lax.ppermute(value, ('section', 'seq'), pairs)  13.8 us
    ppermute x8, waiting for transfers between devices, move(): return lax.ppermute(value, ('section', 'seq'), pairs)  7.44 us
    all_to_all x1, starting transfers between devices, swap(): lax.all_to_all(value, 'seq', 0, 0, axis_index_groups=GROUPS, tiled=True)  6.24 us
    pallas_call x1, Pallas kernels, local_grads(): pl.pallas_call(local_kernel, grid=(4,), in_specs=[pl.BlockSpec((4, TOK, T...  3.64 us
    pallas_call x1, Pallas kernels, pick_all(): pl.pallas_call(pick_kernel, in_specs=[SM] + [raw] * 7, out_specs=VM, out_...  3 us
    all_to_all x1, waiting for transfers between devices, swap(): lax.all_to_all(value, 'seq', 0, 0, axis_index_groups=GROUPS, tiled=True)  2.27 us
    pallas_call x1, Pallas kernels, combine(): pl.pallas_call(combine_kernel, in_specs=[VM] * 5, out_specs=[VM] * 3, out...  1.65 us
  transfers between devices with their start and end apart: 9, of which 3 were waited for; matrix products, arithmetic and copies ran while one was open for 0% of the time, Pallas kernels for 12%

profile of v5, /device:TPU:1, one launch (start us, length us, event | category | flops | bytes accessed | tf_op | source)
XLA Modules:
  0.0 64.9 jit_solution(18015286311400103267)
XLA Ops:
  0.7 3.0 %pick_all.1 = bf16[32,40,128]{2,1,0:T(8,128)(2,1)} custom-call(s32[1]{0:T(128)} %bitcast.1.pos_ref, s32[1,16]{1,0:T(1,128)} %off_ref.1, bf16[1,16,128]{2,1,0:T(8,128)(2,1)} %l_ref.1, bf16[1,16,128]{2,1,0:T(8,128)(2,1)} %d_ref.1, bf16[1,128,2048]{2,1,0:T(8,128)(2,1)} %q_ref.3, bf16[1,128,2048]{2,1,0:T(8,128)(2,1)} %k_ref.3, bf16[1,128,2048]{2,1,0:T(8,128)(2,1)} %v_ref.1, ...), custom_call_target="tpu_custom_call" | custom-call | tf_op jit(solution)/shard_map/pick_all/pallas_call | solution.py:98
  3.7 0.0 copy-start.6
  3.7 21.8 %all_to_all.10 = bf16[32,40,128]{2,1,0:T(8,128)(2,1)S(1)} all-to-all(bf16[32,40,128]{2,1,0:T(8,128)(2,1)} %pick_all.1), channel_id=1, replica_groups={{56,57,58,59,48,49,50,51,40,41,42,43,32,33,34,35,24,25,26,27,16,17,18,1..., dimensions={0} | all-to-all | bytes 655360 | tf_op jit(solution)/shard_map/all_to_all | solution.py:324
  25.5 1.9 %collective-permute-start = (bf16[32,24,128]{2,1,0:T(8,128)(2,1)S(1)}, bf16[32,24,128]{2,1,0:T(8,128)(2,1)S(1)}, u32[]{:S(2)}, u32[]{:S(2)}) collective-permute-start(bf16[32,24,128]{2,1,0:T(8,128)(2,1)S(1)} %slice.8.a_ref), channel_id=1, source_target_pairs={{0,6},{1,7},{2,4},{3,5},{4,2},{5,3},{6,0},{7,1},{8,14},{9,15},{10,... | collective-permute-start | bytes 589832 | tf_op jit(solution)/shard_map/ppermute | solution.py:320
  27.5 3.4 %collective-permute-start.6 = (bf16[32,16,128]{2,1,0:T(8,128)(2,1)S(1)}, bf16[32,16,128]{2,1,0:T(8,128)(2,1)S(1)}, u32[]{:S(2)}, u32[]{:S(2)}) collective-permute-start(bf16[32,16,128]{2,1,0:T(8,128)(2,1)S(1)} %slice.9.b_ref), channel_id=1, source_target_pairs={{0,1},{1,192},{2,3},{3,194},{4,5},{5,196},{6,7},{7,198},{8,9},{9,2... | collective-permute-start | bytes 393224 | tf_op jit(solution)/shard_map/ppermute | solution.py:320
  30.8 1.1 %collective-permute-start.1 = (bf16[32,16,128]{2,1,0:T(8,128)(2,1)S(1)}, bf16[32,16,128]{2,1,0:T(8,128)(2,1)S(1)}, u32[]{:S(2)}, u32[]{:S(2)}) collective-permute-start(bf16[32,16,128]{2,1,0:T(8,128)(2,1)S(1)} %slice.9.b_ref), channel_id=1, source_target_pairs={{0,6},{1,199},{2,4},{3,197},{4,2},{5,195},{6,0},{7,193},{8,14},{9,... | collective-permute-start | bytes 393224 | tf_op jit(solution)/shard_map/ppermute | solution.py:320
  31.9 0.2 collective-permute-start.7
  32.1 0.4 collective-permute-start.4
  32.5 0.4 collective-permute-done.a_ref
  32.9 1.3 %collective-permute-start.2 = (bf16[32,24,128]{2,1,0:T(8,128)(2,1)S(1)}, bf16[32,24,128]{2,1,0:T(8,128)(2,1)S(1)}, u32[]{:S(2)}, u32[]{:S(2)}) collective-permute-start(bf16[32,24,128]{2,1,0:T(8,128)(2,1)S(1)} %collective-permute-done.a_ref), channel_id=1, source_target_pairs={{0,1},{1,0},{2,3},{3,2},{4,5},{5,4},{6,7},{7,6},{8,9},{9,8},{10,11... | collective-permute-start | bytes 589832 | tf_op jit(solution)/shard_map/ppermute | solution.py:320
  34.2 5.5 %collective-permute-start.5 = (bf16[32,16,128]{2,1,0:T(8,128)(2,1)S(1)}, bf16[32,16,128]{2,1,0:T(8,128)(2,1)S(1)}, u32[]{:S(2)}, u32[]{:S(2)}) collective-permute-start(bf16[32,16,128]{2,1,0:T(8,128)(2,1)S(1)} %slice.9.b_ref), channel_id=1, source_target_pairs={{1,193},{3,195},{5,197},{7,199},{9,201},{11,203},{13,205},{15,207}... | collective-permute-start | bytes 393224 | tf_op jit(solution)/shard_map/ppermute | solution.py:320
  39.7 0.1 collective-permute-start.3
  39.8 7.0 %collective-permute-done.5.hop_ref = bf16[32,16,128]{2,1,0:T(8,128)(2,1)S(1)} collective-permute-done((bf16[32,16,128]{2,1,0:T(8,128)(2,1)S(1)}, bf16[32,16,128]{2,1,0:T(8,128)(2,1)S(1)}, u32[]{:S(2)}, u32[]{:S(2)}) %collective-permute-start.5) | collective-permute-done | bytes 131104 | tf_op jit(solution)/shard_map/ppermute | solution.py:320
  46.8 1.0 %near_grads.1 = (bf16[4,256,128]{2,1,0:T(8,128)(2,1)S(1)}, f32[256,128]{1,0:T(8,128)S(1)}, f32[256,128]{1,0:T(8,128)S(1)}, f32[256,128]{1,0:T(8,128)S(1)}, f32[256,128]{1,0:T(8,128)S(1)}) custom-call(s32[1]{0:T(128)} %bitcast.core_ref, bf16[32,24,128]{2,1,0:T(8,128)(2,1)S(1)} %slice.8.a_ref, bf16[32,16,128]{2,1,0:T(8,128)(2,1)S(1)} %slice.9.b_ref, ...), custom_call_target="tpu_custom_call" | custom-call | flops 469762048 | bytes 1572864 | tf_op jit(solution)/shard_map/near_grads/pallas_call | solution.py:237
  47.8 0.0 copy-start
  47.8 0.0 copy-start.1
  47.9 1.5 %far_grads.1 = bf16[32,24,128]{2,1,0:T(8,128)(2,1)} custom-call(s32[1]{0:T(128)} %bitcast.core_ref, bf16[32,24,128]{2,1,0:T(8,128)(2,1)S(1)} %collective-permute-done.a_ref, bf16[32,16,128]{2,1,0:T(8,128)(2,1)S(1)} %collective-permute-done.1.b_ref, bf16[32,24,128]{2,1,0:T(8,128)(2,1)S(1)} %collective-permute-done.2.oa_ref, ...), custom_call_target="tpu_custom_call" | custom-call | tf_op jit(solution)/shard_map/far_grads/pallas_call | solution.py:261
  49.4 6.2 %all-to-all-start.1 = ((bf16[32,24,128]{2,1,0:T(8,128)(2,1)}), bf16[32,24,128]{2,1,0:T(8,128)(2,1)S(1)}, u32[]{:S(2)}, u32[]{:S(2)}) async-start(bf16[32,24,128]{2,1,0:T(8,128)(2,1)} %far_grads.1), calls=%async_computation.1 | async-start | bytes 393216 | tf_op jit(solution)/shard_map/all_to_all | solution.py:324
  55.7 0.0 copy-start.2
  55.7 0.0 copy-start.4
  55.7 1.6 %local_scores.1 = (f32[16,128,128]{2,1,0:T(8,128)S(1)}, s32[16,128]{1,0:T(8,128)S(1)}) custom-call(s32[1,16]{1,0:T(1,128)S(1)} %copy-done.5, bf16[1,128,2048]{2,1,0:T(8,128)(2,1)S(1)} %copy-done, bf16[1,128,2048]{2,1,0:T(8,128)(2,1)S(1)} %copy-done.1, bf16[1,16,128]{2,1,0:T(8,128)(2,1)S(1)} %copy-done.3), custom_call_target="tpu_custom_call" | custom-call | flops 268435456 | bytes 2097152 | tf_op jit(solution)/shard_map/local_scores/pallas_call | solution.py:132
  57.3 3.6 %local_grads.1 = (bf16[128,2048]{1,0:T(8,128)(2,1)S(1)}, bf16[128,2048]{1,0:T(8,128)(2,1)S(1)}, bf16[128,2048]{1,0:T(8,128)(2,1)S(1)}) custom-call(f32[16,128,128]{2,1,0:T(8,128)S(1)} %get-tuple-element.18.p_ref, bf16[1,128,2048]{2,1,0:T(8,128)(2,1)S(1)} %copy-done, bf16[1,128,2048]{2,1,0:T(8,128)(2,1)S(1)} %copy-done.1, ...), custom_call_target="tpu_custom_call" | custom-call | flops 1073741824 | bytes 4718592 | tf_op jit(solution)/shard_map/local_grads/pallas_call | solution.py:168
  61.0 2.3 %all-to-all-done.1.w_ref = bf16[32,24,128]{2,1,0:T(8,128)(2,1)S(1)} async-done(((bf16[32,24,128]{2,1,0:T(8,128)(2,1)}), bf16[32,24,128]{2,1,0:T(8,128)(2,1)S(1)}, u32[]{:S(2)}, u32[]{:S(2)}) %all-to-all-start.1) | async-done | bytes 196640 | tf_op jit(solution)/shard_map/all_to_all | solution.py:324
  63.3 1.6 %combine.1 = (bf16[1,128,2048]{2,1,0:T(8,128)(2,1)}, bf16[1,128,2048]{2,1,0:T(8,128)(2,1)}, bf16[1,128,2048]{2,1,0:T(8,128)(2,1)}) custom-call(bf16[32,24,128]{2,1,0:T(8,128)(2,1)S(1)} %all-to-all-done.1.w_ref, bf16[128,2048]{1,0:T(8,128)(2,1)S(1)} %get-tuple-element.19.dq_ref, bf16[128,2048]{1,0:T(8,128)(2,1)S(1)} %get-tuple-element.20.dk_ref, ...), custom_call_target="tpu_custom_call" | custom-call | tf_op jit(solution)/shard_map/combine/pallas_call | solution.py:285
  (17 shorter events, 0.1 us)
Async XLA Ops:
  3.7 28.2 %copy-start.6 = (bf16[1,128,2048]{2,1,0:T(8,128)(2,1)S(1)}, bf16[1,128,2048]{2,1,0:T(8,128)(2,1)}, u32[]{:S(2)}) copy-start(bf16[1,128,2048]{2,1,0:T(8,128)(2,1)} %g_hbm.1) | copy-start | bytes 1572868
  25.5 7.3 %collective-permute-start = (bf16[32,24,128]{2,1,0:T(8,128)(2,1)S(1)}, bf16[32,24,128]{2,1,0:T(8,128)(2,1)S(1)}, u32[]{:S(2)}, u32[]{:S(2)}) collective-permute-start(bf16[32,24,128]{2,1,0:T(8,128)(2,1)S(1)} %slice.8.a_ref), channel_id=1, source_target_pairs={{0,6},{1,7},{2,4},{3,5},{4,2},{5,3},{6,0},{7,1},{8,14},{9,15},{10,... | collective-permute-start | bytes 589832 | tf_op jit(solution)/shard_map/ppermute | solution.py:320
  27.5 6.7 %collective-permute-start.6 = (bf16[32,16,128]{2,1,0:T(8,128)(2,1)S(1)}, bf16[32,16,128]{2,1,0:T(8,128)(2,1)S(1)}, u32[]{:S(2)}, u32[]{:S(2)}) collective-permute-start(bf16[32,16,128]{2,1,0:T(8,128)(2,1)S(1)} %slice.9.b_ref), channel_id=1, source_target_pairs={{0,1},{1,192},{2,3},{3,194},{4,5},{5,196},{6,7},{7,198},{8,9},{9,2... | collective-permute-start | bytes 393224 | tf_op jit(solution)/shard_map/ppermute | solution.py:320
  30.8 8.8 %collective-permute-start.1 = (bf16[32,16,128]{2,1,0:T(8,128)(2,1)S(1)}, bf16[32,16,128]{2,1,0:T(8,128)(2,1)S(1)}, u32[]{:S(2)}, u32[]{:S(2)}) collective-permute-start(bf16[32,16,128]{2,1,0:T(8,128)(2,1)S(1)} %slice.9.b_ref), channel_id=1, source_target_pairs={{0,6},{1,199},{2,4},{3,197},{4,2},{5,195},{6,0},{7,193},{8,14},{9,... | collective-permute-start | bytes 393224 | tf_op jit(solution)/shard_map/ppermute | solution.py:320
  31.9 25.4 %collective-permute-start.7 = (bf16[1,128,2048]{2,1,0:T(8,128)(2,1)S(1)}, bf16[1,128,2048]{2,1,0:T(8,128)(2,1)S(1)}, u32[]{:S(2)}, u32[]{:S(2)}) collective-permute-start(bf16[1,128,2048]{2,1,0:T(8,128)(2,1)S(1)} %copy-done.6), channel_id=1, source_target_pairs={{0,192},{1,193},{2,194},{3,195},{4,196},{5,197},{6,198},{7,199},{8... | collective-permute-start | bytes 1572872 | tf_op jit(solution)/shard_map/ppermute | solution.py:320
  32.1 14.7 %collective-permute-start.4 = (bf16[32,24,128]{2,1,0:T(8,128)(2,1)S(1)}, bf16[32,24,128]{2,1,0:T(8,128)(2,1)S(1)}, u32[]{:S(2)}, u32[]{:S(2)}) collective-permute-start(bf16[32,24,128]{2,1,0:T(8,128)(2,1)S(1)} %slice.8.a_ref), channel_id=1, source_target_pairs={{0,1},{1,0},{2,3},{3,2},{4,5},{5,4},{6,7},{7,6},{8,9},{9,8},{10,11... | collective-permute-start | bytes 589832 | tf_op jit(solution)/shard_map/ppermute | solution.py:320
  32.9 14.9 %collective-permute-start.2 = (bf16[32,24,128]{2,1,0:T(8,128)(2,1)S(1)}, bf16[32,24,128]{2,1,0:T(8,128)(2,1)S(1)}, u32[]{:S(2)}, u32[]{:S(2)}) collective-permute-start(bf16[32,24,128]{2,1,0:T(8,128)(2,1)S(1)} %collective-permute-done.a_ref), channel_id=1, source_target_pairs={{0,1},{1,0},{2,3},{3,2},{4,5},{5,4},{6,7},{7,6},{8,9},{9,8},{10,11... | collective-permute-start | bytes 589832 | tf_op jit(solution)/shard_map/ppermute | solution.py:320
  34.2 12.6 %collective-permute-start.5 = (bf16[32,16,128]{2,1,0:T(8,128)(2,1)S(1)}, bf16[32,16,128]{2,1,0:T(8,128)(2,1)S(1)}, u32[]{:S(2)}, u32[]{:S(2)}) collective-permute-start(bf16[32,16,128]{2,1,0:T(8,128)(2,1)S(1)} %slice.9.b_ref), channel_id=1, source_target_pairs={{1,193},{3,195},{5,197},{7,199},{9,201},{11,203},{13,205},{15,207}... | collective-permute-start | bytes 393224 | tf_op jit(solution)/shard_map/ppermute | solution.py:320
  39.7 8.1 %collective-permute-start.3 = (bf16[32,16,128]{2,1,0:T(8,128)(2,1)S(1)}, bf16[32,16,128]{2,1,0:T(8,128)(2,1)S(1)}, u32[]{:S(2)}, u32[]{:S(2)}) collective-permute-start(bf16[32,16,128]{2,1,0:T(8,128)(2,1)S(1)} %collective-permute-done.1.b_ref), channel_id=1, source_target_pairs={{0,1},{1,0},{2,3},{3,2},{4,5},{5,4},{6,7},{7,6},{8,9},{9,8},{10,11... | collective-permute-start | bytes 393224 | tf_op jit(solution)/shard_map/ppermute | solution.py:320
  47.8 7.8 %copy-start = (bf16[1,128,2048]{2,1,0:T(8,128)(2,1)S(1)}, bf16[1,128,2048]{2,1,0:T(8,128)(2,1)}, u32[]{:S(2)}) copy-start(bf16[1,128,2048]{2,1,0:T(8,128)(2,1)} %q_ref.3) | copy-start | bytes 1572868
  47.8 7.8 %copy-start.1 = (bf16[1,128,2048]{2,1,0:T(8,128)(2,1)S(1)}, bf16[1,128,2048]{2,1,0:T(8,128)(2,1)}, u32[]{:S(2)}) copy-start(bf16[1,128,2048]{2,1,0:T(8,128)(2,1)} %k_ref.3) | copy-start | bytes 1572868
  49.4 6.3 %copy-start.3 = (bf16[1,16,128]{2,1,0:T(8,128)(2,1)S(1)}, bf16[1,16,128]{2,1,0:T(8,128)(2,1)}, u32[]{:S(2)}) copy-start(bf16[1,16,128]{2,1,0:T(8,128)(2,1)} %l_ref.1) | copy-start | bytes 12292
  49.4 6.3 %copy-start.5 = (s32[1,16]{1,0:T(1,128)S(1)}, s32[1,16]{1,0:T(1,128)}, u32[]{:S(2)}) copy-start(s32[1,16]{1,0:T(1,128)} %off_ref.1) | copy-start | bytes 196
  49.4 13.9 %all-to-all-start.1 = ((bf16[32,24,128]{2,1,0:T(8,128)(2,1)}), bf16[32,24,128]{2,1,0:T(8,128)(2,1)S(1)}, u32[]{:S(2)}, u32[]{:S(2)}) async-start(bf16[32,24,128]{2,1,0:T(8,128)(2,1)} %far_grads.1), calls=%async_computation.1 | async-start | bytes 393216 | tf_op jit(solution)/shard_map/all_to_all | solution.py:324
  55.7 1.7 %copy-start.2 = (bf16[1,128,2048]{2,1,0:T(8,128)(2,1)S(1)}, bf16[1,128,2048]{2,1,0:T(8,128)(2,1)}, u32[]{:S(2)}) copy-start(bf16[1,128,2048]{2,1,0:T(8,128)(2,1)} %v_ref.1) | copy-start | bytes 1572868
  55.7 1.7 %copy-start.4 = (bf16[1,16,128]{2,1,0:T(8,128)(2,1)S(1)}, bf16[1,16,128]{2,1,0:T(8,128)(2,1)}, u32[]{:S(2)}) copy-start(bf16[1,16,128]{2,1,0:T(8,128)(2,1)} %d_ref.1) | copy-start | bytes 12292

commit v6 on v5

--- a/solution.py
+++ b/solution.py
@@ -46,36 +46,26 @@
     return pltpu.CompilerParams(vmem_limit_bytes=mib << 20)
 
 
-def pick_kernel(pos_ref, off_hbm, l_hbm, d_hbm, q_hbm, k_hbm, v_hbm, g_hbm, o_ref, off_ref, l_ref, d_ref, x_ref, sems):
-    loads = [
+def pick_kernel(pos_ref, off_hbm, l_hbm, d_hbm, q_hbm, k_hbm, v_hbm, g_hbm, o_hbm, off_ref, l_ref, d_ref, x_ref, o_ref, sems, load_sems, store_sems):
+    small_loads = [
         pltpu.make_async_copy(src, dst, sems.at[i])
-        for i, (src, dst) in enumerate(
-            (
-                (off_hbm, off_ref),
-                (q_hbm.at[0], x_ref.at[0]),
-                (k_hbm.at[0], x_ref.at[1]),
-                (v_hbm.at[0], x_ref.at[2]),
-                (g_hbm.at[0], x_ref.at[3]),
-                (l_hbm.at[0], l_ref),
-                (d_hbm.at[0], d_ref),
-            )
-        )
+        for i, (src, dst) in enumerate(((off_hbm, off_ref), (l_hbm.at[0], l_ref), (d_hbm.at[0], d_ref)))
     ]
-    for load in loads:
+    for load in small_loads:
         load.start()
+    loads = []
+    for group in range(4):
+        cols = pl.ds(group * 4 * HD, 4 * HD)
+        for part, src in enumerate((q_hbm, k_hbm, v_hbm, g_hbm)):
+            load = pltpu.make_async_copy(src.at[0, :, cols], x_ref.at[part, :, cols], load_sems.at[group, part])
+            load.start()
+            loads.append(load)
     n = pos_ref[0]
     src = lax.broadcasted_iota(jnp.int32, (TOK, TOK), 0)
     dst = lax.broadcasted_iota(jnp.int32, (TOK, TOK), 1)
     place = jnp.where(dst == (n % 8) * PICK + src // RATE, 1.0, 0.0).astype(BF)
-    loads[0].wait()
-    choose = [chooser(off_ref[0, h]) for h in range(HEADS)]
-    for part, core, first in ((0, 0, 0), (1, 0, MAIN), (2, 1, 0), (3, 1, MAIN)):
-        loads[1 + part].wait()
-        for h in range(HEADS):
-            rows = dot(choose[h], x_ref[part, :, h * HD:(h + 1) * HD])
-            o_ref[2 * h + core, first:first + 16] = rows.astype(BF)
-    loads[5].wait()
-    loads[6].wait()
+    for load in small_loads:
+        load.wait()
     head = lax.broadcasted_iota(jnp.int32, (HEADS, TOK), 0)
     lane = lax.broadcasted_iota(jnp.int32, (HEADS, TOK), 1)
     off = jnp.zeros((HEADS, TOK), jnp.int32)
@@ -85,12 +75,26 @@
     lses = dot(jnp.where(hit, l_ref[...].astype(F32), 0.0).astype(BF), place)
     dlts = dot(jnp.where(hit, d_ref[...].astype(F32), 0.0).astype(BF), place)
     row = lax.broadcasted_iota(jnp.int32, (8, HD), 0)
-    for h in range(HEADS):
-        lse = jnp.broadcast_to(lses[h:h + 1], (8, HD))
-        dlt = jnp.broadcast_to(dlts[h:h + 1], (8, HD))
-        stats = jnp.where(row == n // 8, lse, jnp.where(row == 4 + n // 8, dlt, 0.0))
-        o_ref[2 * h, 16:MAIN] = stats.astype(BF)
-        o_ref[2 * h + 1, 16:MAIN] = jnp.zeros((8, HD), BF)
+    stores = []
+    for group in range(4):
+        for load in loads[4 * group:4 * group + 4]:
+            load.wait()
+        for h in range(4 * group, 4 * group + 4):
+            choose = chooser(off_ref[0, h])
+            for part, core, first in ((0, 0, 0), (1, 0, MAIN), (2, 1, 0), (3, 1, MAIN)):
+                rows = dot(choose, x_ref[part, :, h * HD:(h + 1) * HD])
+                o_ref[2 * h + core, first:first + 16] = rows.astype(BF)
+            lse = jnp.broadcast_to(lses[h:h + 1], (8, HD))
+            dlt = jnp.broadcast_to(dlts[h:h + 1], (8, HD))
+            stats = jnp.where(row == n // 8, lse, jnp.where(row == 4 + n // 8, dlt, 0.0))
+            o_ref[2 * h, 16:MAIN] = stats.astype(BF)
+            o_ref[2 * h + 1, 16:MAIN] = jnp.zeros((8, HD), BF)
+        out = pl.ds(8 * group, 8)
+        store = pltpu.make_async_copy(o_ref.at[out], o_hbm.at[out], store_sems.at[group])
+        store.start()
+        stores.append(store)
+    for store in stores:
+        store.wait()
 
 
 def pick_all(pos, offsets, lse, delta, query, key, value, grad):
@@ -98,14 +102,17 @@
     return pl.pallas_call(
         pick_kernel,
         in_specs=[SM] + [raw] * 7,
-        out_specs=VM,
+        out_specs=raw,
         out_shape=jax.ShapeDtypeStruct((GROUP, ROWS, HD), BF),
         scratch_shapes=[
             pltpu.SMEM((1, HEADS), jnp.int32),
             pltpu.VMEM((HEADS, TOK), BF),
             pltpu.VMEM((HEADS, TOK), BF),
             pltpu.VMEM((4, TOK, HEADS * HD), BF),
-            pltpu.SemaphoreType.DMA((7,)),
+            pltpu.VMEM((GROUP, ROWS, HD), BF),
+            pltpu.SemaphoreType.DMA((3,)),
+            pltpu.SemaphoreType.DMA((4, 4)),
+            pltpu.SemaphoreType.DMA((4,)),
         ],
         name="pick_all",
     )(pos, offsets, lse, delta, query, key, value, grad)
@@ -252,9 +259,12 @@
     lse, dlt = col_ref[:, 0:1], col_ref[:, 1:2]
     dq = dq_ref[...] + query_side(sub_ref[0], sub_ref[3], k, v, lse, dlt)
     dk, dv = key_side(sub_ref[1], sub_ref[2], q, g, stats)
-    o_ref[:, 0:8, :] = (dq * SCALE).reshape(GROUP, 8, HD).astype(BF)
-    o_ref[:, 8:16, :] = ((dk_ref[...] + dk) * SCALE).reshape(GROUP, 8, HD).astype(BF)
-    o_ref[:, 16:24, :] = (dv_ref[...] + dv).reshape(GROUP, 8, HD).astype(BF)
+    parts = (dq * SCALE, (dk_ref[...] + dk) * SCALE, dv_ref[...] + dv)
+    for i, part in enumerate(parts):
+        rows = part.reshape(GROUP, 8, HD).astype(BF)
+        for to, z in enumerate(OUT_ORDER):
+            at = IN_ORDER.index(z) * 4
+            o_ref[4 * to:4 * to + 4, 8 * i:8 * i + 8, :] = rows[at:at + 4]
 
 
 def far_grads(*args):
@@ -268,16 +278,26 @@
     )(*args)
 
 
-def combine_kernel(w_ref, dq_ref, dk_ref, dv_ref, off_ref, oq_ref, ok_ref, ov_ref):
+def combine_kernel(w_ref, dq_ref, dk_ref, dv_ref, off_ref, oq_hbm, ok_hbm, ov_hbm, out_ref, sems):
     row = lax.broadcasted_iota(jnp.int32, (PICK, RATE, HD), 1)
-    for h in range(HEADS):
-        hit = row == off_ref[h:h + 1, :].reshape(1, 1, TOK)
-        for part, (src, out) in enumerate(((dq_ref, oq_ref), (dk_ref, ok_ref), (dv_ref, ov_ref))):
-            rows = slice(part * 8, (part + 1) * 8)
-            w = jnp.concatenate([w_ref[2 * h, rows, :].astype(F32), w_ref[2 * h + 1, rows, :].astype(F32)], axis=0)
-            local = src[:, h * HD:(h + 1) * HD].astype(F32).reshape(PICK, RATE, HD)
-            total = local + jnp.where(hit, w[:, None, :], 0.0)
-            out[0, :, h * HD:(h + 1) * HD] = total.reshape(TOK, HD).astype(BF)
+    stores = []
+    for group in range(4):
+        for h in range(4 * group, 4 * group + 4):
+            hit = row == off_ref[h:h + 1, :].reshape(1, 1, TOK)
+            first = OUT_ORDER.index(IN_ORDER[h // 2]) * 4 + h % 2 * 2
+            for part, src in enumerate((dq_ref, dk_ref, dv_ref)):
+                rows = slice(part * 8, (part + 1) * 8)
+                w = jnp.concatenate([w_ref[first, rows, :].astype(F32), w_ref[first + 1, rows, :].astype(F32)], axis=0)
+                local = src[:, h * HD:(h + 1) * HD].astype(F32).reshape(PICK, RATE, HD)
+                total = local + jnp.where(hit, w[:, None, :], 0.0)
+                out_ref[part, :, h * HD:(h + 1) * HD] = total.reshape(TOK, HD).astype(BF)
+        cols = pl.ds(group * 4 * HD, 4 * HD)
+        for part, dst in enumerate((oq_hbm, ok_hbm, ov_hbm)):
+            store = pltpu.make_async_copy(out_ref.at[part, :, cols], dst.at[0, :, cols], sems.at[group, part])
+            store.start()
+            stores.append(store)
+    for store in stores:
+        store.wait()
 
 
 def combine(wide, local):
@@ -285,8 +305,9 @@
     return pl.pallas_call(
         combine_kernel,
         in_specs=[VM] * 5,
-        out_specs=[VM] * 3,
+        out_specs=[pl.BlockSpec(memory_space=pltpu.HBM)] * 3,
         out_shape=[shape, shape, shape],
+        scratch_shapes=[pltpu.VMEM((3, TOK, HEADS * HD), BF), pltpu.SemaphoreType.DMA((4, 3))],
         compiler_params=small(),
         name="combine",
     )(wide, *local)
@@ -300,10 +321,12 @@
     return place if half == 0 else NX - 1 - place
 
 
-GROUPS = [
-    [place_of(z, column(half, p), c) for z in reversed(range(NZ)) for p in range(2) for c in range(NC)]
-    for half in range(2)
-]
+def groups_of(order):
+    return [[place_of(z, column(half, p), c) for z in order for p in range(2) for c in range(NC)] for half in range(2)]
+
+
+IN_ORDER = (7, 6, 5, 4, 3, 2, 1, 0)
+OUT_ORDER = (7, 6, 5, 4, 0, 1, 2, 3)
 
 
 def move(value, route):
@@ -320,8 +343,8 @@
     return lax.ppermute(value, ("section", "seq"), pairs)
 
 
-def swap(value):
-    return lax.all_to_all(value, "seq", 0, 0, axis_index_groups=GROUPS, tiled=True)
+def swap(value, order):
+    return lax.all_to_all(value, "seq", 0, 0, axis_index_groups=groups_of(order), tiled=True)
 
 
 def body(queries, key_rows, value_rows, grad_out, log_sums, deltas, offsets):
@@ -330,7 +353,7 @@
     core = (seat % NC).reshape(1)
     pos = ((NZ - 1 - seat // (NX * NC)) * 4 + jnp.where(x < 2, x, NX - 1 - x) * 2 + seat % NC).reshape(1)
     picked = pick_all(pos, offsets, log_sums, deltas, queries, key_rows, value_rows, grad_out)
-    mine = swap(picked)
+    mine = swap(picked, IN_ORDER)
     grad = move(grad_out, lambda s, x, c: (s - 1, x, c))
     probs, offs = local_scores(offsets, queries, key_rows, log_sums)
     a, b = mine[:, :MAIN], mine[:, MAIN:]
@@ -343,7 +366,7 @@
     other_far_b = move(far_b, lambda s, x, c: (s, x, 1 - c))
     local = local_grads(probs, queries, key_rows, value_rows, grad, deltas)
     part = near_grads(core, a, b, other_a, hop, cross)
-    back = swap(far_grads(core, far_a, far_b, other_far_a, other_far_b, *part))
+    back = swap(far_grads(core, far_a, far_b, other_far_a, other_far_b, *part), OUT_ORDER)
     return tuple(combine(back, (*local, offs)))
 
 

time: 65.3 us -> 66.4 us (1.017)
  waiting for transfers between devices: 9.7 us -> 10.7 us
    all_to_all x1, waiting for transfers between devices: 2.27 us -> 3.21 us  [swap(): lax.all_to_all(value, 'seq', 0, 0, axis_index_groups=groups_of(order), ti...]
where the time goes in v6:
time: 66.4 us; the launch traced here: 66.1 us
  blocking collectives  21.8 us (33%)
  starting transfers between devices  19.9 us (30%)
  Pallas kernels  12.7 us (19%)
  waiting for transfers between devices  10.7 us (16%)
  between operations  0.86 us (1%)
    all_to_all x1, blocking collectives, swap(): lax.all_to_all(value, 'seq', 0, 0, axis_index_groups=groups_of(order), ti...  21.8 us
    ppermute x8, starting transfers between devices, move(): return lax.ppermute(value, ('section', 'seq'), pairs)  13.8 us
    ppermute x8, waiting for transfers between devices, move(): return lax.ppermute(value, ('section', 'seq'), pairs)  7.44 us
    all_to_all x1, starting transfers between devices, swap(): lax.all_to_all(value, 'seq', 0, 0, axis_index_groups=groups_of(order), ti...  6.17 us
    pallas_call x1, Pallas kernels, local_grads(): pl.pallas_call(local_kernel, grid=(4,), in_specs=[pl.BlockSpec((4, TOK, T...  3.64 us
    pallas_call x1, Pallas kernels, pick_all(): pl.pallas_call(pick_kernel, in_specs=[SM] + [raw] * 7, out_specs=raw, out...  3.4 us
    all_to_all x1, waiting for transfers between devices, swap(): lax.all_to_all(value, 'seq', 0, 0, axis_index_groups=groups_of(order), ti...  3.21 us
    pallas_call x1, Pallas kernels, local_scores(): pl.pallas_call(score_kernel, grid=(4,), in_specs=[SM, wide, wide, stat],...  1.63 us
  transfers between devices with their start and end apart: 9, of which 3 were waited for; matrix products, arithmetic and copies ran while one was open for 0% of the time, Pallas kernels for 12%

profile of v6, /device:TPU:1, one launch (start us, length us, event | category | flops | bytes accessed | tf_op | source)
XLA Modules:
  0.0 66.1 jit_solution(4949045959863802400)
XLA Ops:
  0.7 3.4 %pick_all.1 = bf16[32,40,128]{2,1,0:T(8,128)(2,1)} custom-call(s32[1]{0:T(128)} %bitcast.1.pos_ref, s32[1,16]{1,0:T(1,128)} %off_ref.1, bf16[1,16,128]{2,1,0:T(8,128)(2,1)} %l_ref.1, bf16[1,16,128]{2,1,0:T(8,128)(2,1)} %d_ref.1, bf16[1,128,2048]{2,1,0:T(8,128)(2,1)} %q_ref.3, bf16[1,128,2048]{2,1,0:T(8,128)(2,1)} %k_ref.3, bf16[1,128,2048]{2,1,0:T(8,128)(2,1)} %v_ref.1, ...), custom_call_target="tpu_custom_call" | custom-call | tf_op jit(solution)/shard_map/pick_all/pallas_call | solution.py:102
  4.1 0.0 copy-start.6
  4.1 21.8 %all_to_all.10 = bf16[32,40,128]{2,1,0:T(8,128)(2,1)S(1)} all-to-all(bf16[32,40,128]{2,1,0:T(8,128)(2,1)} %pick_all.1), channel_id=1, replica_groups={{56,57,58,59,48,49,50,51,40,41,42,43,32,33,34,35,24,25,26,27,16,17,18,1..., dimensions={0} | all-to-all | bytes 655360 | tf_op jit(solution)/shard_map/all_to_all | solution.py:347
  25.9 1.9 %collective-permute-start = (bf16[32,24,128]{2,1,0:T(8,128)(2,1)S(1)}, bf16[32,24,128]{2,1,0:T(8,128)(2,1)S(1)}, u32[]{:S(2)}, u32[]{:S(2)}) collective-permute-start(bf16[32,24,128]{2,1,0:T(8,128)(2,1)S(1)} %slice.8.a_ref), channel_id=1, source_target_pairs={{0,6},{1,7},{2,4},{3,5},{4,2},{5,3},{6,0},{7,1},{8,14},{9,15},{10,... | collective-permute-start | bytes 589832 | tf_op jit(solution)/shard_map/ppermute | solution.py:343
  27.9 3.4 %collective-permute-start.6 = (bf16[32,16,128]{2,1,0:T(8,128)(2,1)S(1)}, bf16[32,16,128]{2,1,0:T(8,128)(2,1)S(1)}, u32[]{:S(2)}, u32[]{:S(2)}) collective-permute-start(bf16[32,16,128]{2,1,0:T(8,128)(2,1)S(1)} %slice.9.b_ref), channel_id=1, source_target_pairs={{0,1},{1,192},{2,3},{3,194},{4,5},{5,196},{6,7},{7,198},{8,9},{9,2... | collective-permute-start | bytes 393224 | tf_op jit(solution)/shard_map/ppermute | solution.py:343
  31.2 1.1 %collective-permute-start.1 = (bf16[32,16,128]{2,1,0:T(8,128)(2,1)S(1)}, bf16[32,16,128]{2,1,0:T(8,128)(2,1)S(1)}, u32[]{:S(2)}, u32[]{:S(2)}) collective-permute-start(bf16[32,16,128]{2,1,0:T(8,128)(2,1)S(1)} %slice.9.b_ref), channel_id=1, source_target_pairs={{0,6},{1,199},{2,4},{3,197},{4,2},{5,195},{6,0},{7,193},{8,14},{9,... | collective-permute-start | bytes 393224 | tf_op jit(solution)/shard_map/ppermute | solution.py:343
  32.3 0.2 collective-permute-start.7
  32.5 0.4 collective-permute-start.4
  32.9 0.4 collective-permute-done.a_ref
  33.3 1.3 %collective-permute-start.2 = (bf16[32,24,128]{2,1,0:T(8,128)(2,1)S(1)}, bf16[32,24,128]{2,1,0:T(8,128)(2,1)S(1)}, u32[]{:S(2)}, u32[]{:S(2)}) collective-permute-start(bf16[32,24,128]{2,1,0:T(8,128)(2,1)S(1)} %collective-permute-done.a_ref), channel_id=1, source_target_pairs={{0,1},{1,0},{2,3},{3,2},{4,5},{5,4},{6,7},{7,6},{8,9},{9,8},{10,11... | collective-permute-start | bytes 589832 | tf_op jit(solution)/shard_map/ppermute | solution.py:343
  34.6 5.5 %collective-permute-start.5 = (bf16[32,16,128]{2,1,0:T(8,128)(2,1)S(1)}, bf16[32,16,128]{2,1,0:T(8,128)(2,1)S(1)}, u32[]{:S(2)}, u32[]{:S(2)}) collective-permute-start(bf16[32,16,128]{2,1,0:T(8,128)(2,1)S(1)} %slice.9.b_ref), channel_id=1, source_target_pairs={{1,193},{3,195},{5,197},{7,199},{9,201},{11,203},{13,205},{15,207}... | collective-permute-start | bytes 393224 | tf_op jit(solution)/shard_map/ppermute | solution.py:343
  40.1 0.1 collective-permute-start.3
  40.2 7.0 %collective-permute-done.5.hop_ref = bf16[32,16,128]{2,1,0:T(8,128)(2,1)S(1)} collective-permute-done((bf16[32,16,128]{2,1,0:T(8,128)(2,1)S(1)}, bf16[32,16,128]{2,1,0:T(8,128)(2,1)S(1)}, u32[]{:S(2)}, u32[]{:S(2)}) %collective-permute-start.5) | collective-permute-done | bytes 131104 | tf_op jit(solution)/shard_map/ppermute | solution.py:343
  47.2 1.0 %near_grads.1 = (bf16[4,256,128]{2,1,0:T(8,128)(2,1)S(1)}, f32[256,128]{1,0:T(8,128)S(1)}, f32[256,128]{1,0:T(8,128)S(1)}, f32[256,128]{1,0:T(8,128)S(1)}, f32[256,128]{1,0:T(8,128)S(1)}) custom-call(s32[1]{0:T(128)} %bitcast.core_ref, bf16[32,24,128]{2,1,0:T(8,128)(2,1)S(1)} %slice.8.a_ref, bf16[32,16,128]{2,1,0:T(8,128)(2,1)S(1)} %slice.9.b_ref, ...), custom_call_target="tpu_custom_call" | custom-call | flops 469762048 | bytes 1572864 | tf_op jit(solution)/shard_map/near_grads/pallas_call | solution.py:244
  48.2 0.0 copy-start
  48.2 0.0 copy-start.1
  48.3 1.5 %far_grads.1 = bf16[32,24,128]{2,1,0:T(8,128)(2,1)} custom-call(s32[1]{0:T(128)} %bitcast.core_ref, bf16[32,24,128]{2,1,0:T(8,128)(2,1)S(1)} %collective-permute-done.a_ref, bf16[32,16,128]{2,1,0:T(8,128)(2,1)S(1)} %collective-permute-done.1.b_ref, bf16[32,24,128]{2,1,0:T(8,128)(2,1)S(1)} %collective-permute-done.2.oa_ref, ...), custom_call_target="tpu_custom_call" | custom-call | tf_op jit(solution)/shard_map/far_grads/pallas_call | solution.py:271
  49.8 6.2 %all-to-all-start.1 = ((bf16[32,24,128]{2,1,0:T(8,128)(2,1)}), bf16[32,24,128]{2,1,0:T(8,128)(2,1)S(1)}, u32[]{:S(2)}, u32[]{:S(2)}) async-start(bf16[32,24,128]{2,1,0:T(8,128)(2,1)} %far_grads.1), calls=%async_computation.1 | async-start | bytes 393216 | tf_op jit(solution)/shard_map/all_to_all | solution.py:347
  56.0 0.0 copy-start.2
  56.0 0.0 copy-start.4
  56.0 1.6 %local_scores.1 = (f32[16,128,128]{2,1,0:T(8,128)S(1)}, s32[16,128]{1,0:T(8,128)S(1)}) custom-call(s32[1,16]{1,0:T(1,128)S(1)} %copy-done.5, bf16[1,128,2048]{2,1,0:T(8,128)(2,1)S(1)} %copy-done, bf16[1,128,2048]{2,1,0:T(8,128)(2,1)S(1)} %copy-done.1, bf16[1,16,128]{2,1,0:T(8,128)(2,1)S(1)} %copy-done.3), custom_call_target="tpu_custom_call" | custom-call | flops 268435456 | bytes 2097152 | tf_op jit(solution)/shard_map/local_scores/pallas_call | solution.py:139
  57.7 3.6 %local_grads.1 = (bf16[128,2048]{1,0:T(8,128)(2,1)S(1)}, bf16[128,2048]{1,0:T(8,128)(2,1)S(1)}, bf16[128,2048]{1,0:T(8,128)(2,1)S(1)}) custom-call(f32[16,128,128]{2,1,0:T(8,128)S(1)} %get-tuple-element.18.p_ref, bf16[1,128,2048]{2,1,0:T(8,128)(2,1)S(1)} %copy-done, bf16[1,128,2048]{2,1,0:T(8,128)(2,1)S(1)} %copy-done.1, ...), custom_call_target="tpu_custom_call" | custom-call | flops 1073741824 | bytes 4718592 | tf_op jit(solution)/shard_map/local_grads/pallas_call | solution.py:175
  61.3 3.2 %all-to-all-done.1.w_ref = bf16[32,24,128]{2,1,0:T(8,128)(2,1)S(1)} async-done(((bf16[32,24,128]{2,1,0:T(8,128)(2,1)}), bf16[32,24,128]{2,1,0:T(8,128)(2,1)S(1)}, u32[]{:S(2)}, u32[]{:S(2)}) %all-to-all-start.1) | async-done | bytes 196640 | tf_op jit(solution)/shard_map/all_to_all | solution.py:347
  64.5 1.5 %combine.1 = (bf16[1,128,2048]{2,1,0:T(8,128)(2,1)}, bf16[1,128,2048]{2,1,0:T(8,128)(2,1)}, bf16[1,128,2048]{2,1,0:T(8,128)(2,1)}) custom-call(bf16[32,24,128]{2,1,0:T(8,128)(2,1)S(1)} %all-to-all-done.1.w_ref, bf16[128,2048]{1,0:T(8,128)(2,1)S(1)} %get-tuple-element.19.dq_ref, bf16[128,2048]{1,0:T(8,128)(2,1)S(1)} %get-tuple-element.20.dk_ref, ...), custom_call_target="tpu_custom_call" | custom-call | tf_op jit(solution)/shard_map/combine/pallas_call | solution.py:305
  (17 shorter events, 0.1 us)
Async XLA Ops:
  4.1 28.2 %copy-start.6 = (bf16[1,128,2048]{2,1,0:T(8,128)(2,1)S(1)}, bf16[1,128,2048]{2,1,0:T(8,128)(2,1)}, u32[]{:S(2)}) copy-start(bf16[1,128,2048]{2,1,0:T(8,128)(2,1)} %g_hbm.1) | copy-start | bytes 1572868
  25.9 7.3 %collective-permute-start = (bf16[32,24,128]{2,1,0:T(8,128)(2,1)S(1)}, bf16[32,24,128]{2,1,0:T(8,128)(2,1)S(1)}, u32[]{:S(2)}, u32[]{:S(2)}) collective-permute-start(bf16[32,24,128]{2,1,0:T(8,128)(2,1)S(1)} %slice.8.a_ref), channel_id=1, source_target_pairs={{0,6},{1,7},{2,4},{3,5},{4,2},{5,3},{6,0},{7,1},{8,14},{9,15},{10,... | collective-permute-start | bytes 589832 | tf_op jit(solution)/shard_map/ppermute | solution.py:343
  27.9 6.7 %collective-permute-start.6 = (bf16[32,16,128]{2,1,0:T(8,128)(2,1)S(1)}, bf16[32,16,128]{2,1,0:T(8,128)(2,1)S(1)}, u32[]{:S(2)}, u32[]{:S(2)}) collective-permute-start(bf16[32,16,128]{2,1,0:T(8,128)(2,1)S(1)} %slice.9.b_ref), channel_id=1, source_target_pairs={{0,1},{1,192},{2,3},{3,194},{4,5},{5,196},{6,7},{7,198},{8,9},{9,2... | collective-permute-start | bytes 393224 | tf_op jit(solution)/shard_map/ppermute | solution.py:343
  31.2 8.8 %collective-permute-start.1 = (bf16[32,16,128]{2,1,0:T(8,128)(2,1)S(1)}, bf16[32,16,128]{2,1,0:T(8,128)(2,1)S(1)}, u32[]{:S(2)}, u32[]{:S(2)}) collective-permute-start(bf16[32,16,128]{2,1,0:T(8,128)(2,1)S(1)} %slice.9.b_ref), channel_id=1, source_target_pairs={{0,6},{1,199},{2,4},{3,197},{4,2},{5,195},{6,0},{7,193},{8,14},{9,... | collective-permute-start | bytes 393224 | tf_op jit(solution)/shard_map/ppermute | solution.py:343
  32.3 25.4 %collective-permute-start.7 = (bf16[1,128,2048]{2,1,0:T(8,128)(2,1)S(1)}, bf16[1,128,2048]{2,1,0:T(8,128)(2,1)S(1)}, u32[]{:S(2)}, u32[]{:S(2)}) collective-permute-start(bf16[1,128,2048]{2,1,0:T(8,128)(2,1)S(1)} %copy-done.6), channel_id=1, source_target_pairs={{0,192},{1,193},{2,194},{3,195},{4,196},{5,197},{6,198},{7,199},{8... | collective-permute-start | bytes 1572872 | tf_op jit(solution)/shard_map/ppermute | solution.py:343
  32.5 14.7 %collective-permute-start.4 = (bf16[32,24,128]{2,1,0:T(8,128)(2,1)S(1)}, bf16[32,24,128]{2,1,0:T(8,128)(2,1)S(1)}, u32[]{:S(2)}, u32[]{:S(2)}) collective-permute-start(bf16[32,24,128]{2,1,0:T(8,128)(2,1)S(1)} %slice.8.a_ref), channel_id=1, source_target_pairs={{0,1},{1,0},{2,3},{3,2},{4,5},{5,4},{6,7},{7,6},{8,9},{9,8},{10,11... | collective-permute-start | bytes 589832 | tf_op jit(solution)/shard_map/ppermute | solution.py:343
  33.3 14.9 %collective-permute-start.2 = (bf16[32,24,128]{2,1,0:T(8,128)(2,1)S(1)}, bf16[32,24,128]{2,1,0:T(8,128)(2,1)S(1)}, u32[]{:S(2)}, u32[]{:S(2)}) collective-permute-start(bf16[32,24,128]{2,1,0:T(8,128)(2,1)S(1)} %collective-permute-done.a_ref), channel_id=1, source_target_pairs={{0,1},{1,0},{2,3},{3,2},{4,5},{5,4},{6,7},{7,6},{8,9},{9,8},{10,11... | collective-permute-start | bytes 589832 | tf_op jit(solution)/shard_map/ppermute | solution.py:343
  34.6 12.6 %collective-permute-start.5 = (bf16[32,16,128]{2,1,0:T(8,128)(2,1)S(1)}, bf16[32,16,128]{2,1,0:T(8,128)(2,1)S(1)}, u32[]{:S(2)}, u32[]{:S(2)}) collective-permute-start(bf16[32,16,128]{2,1,0:T(8,128)(2,1)S(1)} %slice.9.b_ref), channel_id=1, source_target_pairs={{1,193},{3,195},{5,197},{7,199},{9,201},{11,203},{13,205},{15,207}... | collective-permute-start | bytes 393224 | tf_op jit(solution)/shard_map/ppermute | solution.py:343
  40.1 8.1 %collective-permute-start.3 = (bf16[32,16,128]{2,1,0:T(8,128)(2,1)S(1)}, bf16[32,16,128]{2,1,0:T(8,128)(2,1)S(1)}, u32[]{:S(2)}, u32[]{:S(2)}) collective-permute-start(bf16[32,16,128]{2,1,0:T(8,128)(2,1)S(1)} %collective-permute-done.1.b_ref), channel_id=1, source_target_pairs={{0,1},{1,0},{2,3},{3,2},{4,5},{5,4},{6,7},{7,6},{8,9},{9,8},{10,11... | collective-permute-start | bytes 393224 | tf_op jit(solution)/shard_map/ppermute | solution.py:343
  48.2 7.7 %copy-start = (bf16[1,128,2048]{2,1,0:T(8,128)(2,1)S(1)}, bf16[1,128,2048]{2,1,0:T(8,128)(2,1)}, u32[]{:S(2)}) copy-start(bf16[1,128,2048]{2,1,0:T(8,128)(2,1)} %q_ref.3) | copy-start | bytes 1572868
  48.2 7.7 %copy-start.1 = (bf16[1,128,2048]{2,1,0:T(8,128)(2,1)S(1)}, bf16[1,128,2048]{2,1,0:T(8,128)(2,1)}, u32[]{:S(2)}) copy-start(bf16[1,128,2048]{2,1,0:T(8,128)(2,1)} %k_ref.3) | copy-start | bytes 1572868
  49.8 6.2 %copy-start.3 = (bf16[1,16,128]{2,1,0:T(8,128)(2,1)S(1)}, bf16[1,16,128]{2,1,0:T(8,128)(2,1)}, u32[]{:S(2)}) copy-start(bf16[1,16,128]{2,1,0:T(8,128)(2,1)} %l_ref.1) | copy-start | bytes 12292
  49.8 6.2 %copy-start.5 = (s32[1,16]{1,0:T(1,128)S(1)}, s32[1,16]{1,0:T(1,128)}, u32[]{:S(2)}) copy-start(s32[1,16]{1,0:T(1,128)} %off_ref.1) | copy-start | bytes 196
  49.8 14.8 %all-to-all-start.1 = ((bf16[32,24,128]{2,1,0:T(8,128)(2,1)}), bf16[32,24,128]{2,1,0:T(8,128)(2,1)S(1)}, u32[]{:S(2)}, u32[]{:S(2)}) async-start(bf16[32,24,128]{2,1,0:T(8,128)(2,1)} %far_grads.1), calls=%async_computation.1 | async-start | bytes 393216 | tf_op jit(solution)/shard_map/all_to_all | solution.py:347
  56.0 1.7 %copy-start.2 = (bf16[1,128,2048]{2,1,0:T(8,128)(2,1)S(1)}, bf16[1,128,2048]{2,1,0:T(8,128)(2,1)}, u32[]{:S(2)}) copy-start(bf16[1,128,2048]{2,1,0:T(8,128)(2,1)} %v_ref.1) | copy-start | bytes 1572868
  56.0 1.7 %copy-start.4 = (bf16[1,16,128]{2,1,0:T(8,128)(2,1)S(1)}, bf16[1,16,128]{2,1,0:T(8,128)(2,1)}, u32[]{:S(2)}) copy-start(bf16[1,16,128]{2,1,0:T(8,128)(2,1)} %d_ref.1) | copy-start | bytes 12292

commit v7 on v5

--- a/solution.py
+++ b/solution.py
@@ -215,10 +215,9 @@
     return jnp.where(core == 0, t[:, 0], t[:, 1]).reshape(HALF, width)
 
 
-def near_kernel(core_ref, a_ref, b_ref, oa_ref, hop_ref, cross_ref, sub_ref, col_ref, dq_ref, dk_ref, dv_ref):
+def near_kernel(core_ref, a_ref, b_ref, oa_ref, ob_ref, sub_ref, col_ref, dq_ref, dk_ref, dv_ref):
     core = core_ref[0]
-    mine_b = jnp.where(core == 0, b_ref[...], hop_ref[...])
-    q, k, v, g = whole(core, a_ref[:, 0:16], mine_b, oa_ref[:, 0:16], cross_ref[...])
+    q, k, v, g = whole(core, a_ref[:, 0:16], b_ref[...], oa_ref[:, 0:16], ob_ref[...])
     stats = stats_of(core, a_ref, oa_ref)
     turned = jnp.transpose(jnp.concatenate([stats, jnp.zeros((HD - 8, HD), F32)], axis=0))
     lse = share(core, jnp.concatenate([turned[:, i:i + 1] for i in range(4)], axis=0))
@@ -236,7 +235,7 @@
     part = jax.ShapeDtypeStruct((HALF, HD), F32)
     return pl.pallas_call(
         near_kernel,
-        in_specs=[SM] + [VM] * 5,
+        in_specs=[SM] + [VM] * 4,
         out_specs=[VM] * 5,
         out_shape=[jax.ShapeDtypeStruct((4, HALF, HD), BF)] + [part] * 4,
         compiler_params=small(),
@@ -252,9 +251,12 @@
     lse, dlt = col_ref[:, 0:1], col_ref[:, 1:2]
     dq = dq_ref[...] + query_side(sub_ref[0], sub_ref[3], k, v, lse, dlt)
     dk, dv = key_side(sub_ref[1], sub_ref[2], q, g, stats)
-    o_ref[:, 0:8, :] = (dq * SCALE).reshape(GROUP, 8, HD).astype(BF)
-    o_ref[:, 8:16, :] = ((dk_ref[...] + dk) * SCALE).reshape(GROUP, 8, HD).astype(BF)
-    o_ref[:, 16:24, :] = (dv_ref[...] + dv).reshape(GROUP, 8, HD).astype(BF)
+    parts = (dq * SCALE, (dk_ref[...] + dk) * SCALE, dv_ref[...] + dv)
+    for i, part in enumerate(parts):
+        rows = part.reshape(GROUP, 8, HD).astype(BF)
+        for to, z in enumerate(OUT_ORDER):
+            at = IN_ORDER.index(z) * 4
+            o_ref[4 * to:4 * to + 4, 8 * i:8 * i + 8, :] = rows[at:at + 4]
 
 
 def far_grads(*args):
@@ -268,16 +270,26 @@
     )(*args)
 
 
-def combine_kernel(w_ref, dq_ref, dk_ref, dv_ref, off_ref, oq_ref, ok_ref, ov_ref):
+def combine_kernel(w_ref, dq_ref, dk_ref, dv_ref, off_ref, oq_hbm, ok_hbm, ov_hbm, out_ref, sems):
     row = lax.broadcasted_iota(jnp.int32, (PICK, RATE, HD), 1)
-    for h in range(HEADS):
-        hit = row == off_ref[h:h + 1, :].reshape(1, 1, TOK)
-        for part, (src, out) in enumerate(((dq_ref, oq_ref), (dk_ref, ok_ref), (dv_ref, ov_ref))):
-            rows = slice(part * 8, (part + 1) * 8)
-            w = jnp.concatenate([w_ref[2 * h, rows, :].astype(F32), w_ref[2 * h + 1, rows, :].astype(F32)], axis=0)
-            local = src[:, h * HD:(h + 1) * HD].astype(F32).reshape(PICK, RATE, HD)
-            total = local + jnp.where(hit, w[:, None, :], 0.0)
-            out[0, :, h * HD:(h + 1) * HD] = total.reshape(TOK, HD).astype(BF)
+    stores = []
+    for group in range(4):
+        for h in range(4 * group, 4 * group + 4):
+            hit = row == off_ref[h:h + 1, :].reshape(1, 1, TOK)
+            first = OUT_ORDER.index(IN_ORDER[h // 2]) * 4 + h % 2 * 2
+            for part, src in enumerate((dq_ref, dk_ref, dv_ref)):
+                rows = slice(part * 8, (part + 1) * 8)
+                w = jnp.concatenate([w_ref[first, rows, :].astype(F32), w_ref[first + 1, rows, :].astype(F32)], axis=0)
+                local = src[:, h * HD:(h + 1) * HD].astype(F32).reshape(PICK, RATE, HD)
+                total = local + jnp.where(hit, w[:, None, :], 0.0)
+                out_ref[part, :, h * HD:(h + 1) * HD] = total.reshape(TOK, HD).astype(BF)
+        cols = pl.ds(group * 4 * HD, 4 * HD)
+        for part, dst in enumerate((oq_hbm, ok_hbm, ov_hbm)):
+            store = pltpu.make_async_copy(out_ref.at[part, :, cols], dst.at[0, :, cols], sems.at[group, part])
+            store.start()
+            stores.append(store)
+    for store in stores:
+        store.wait()
 
 
 def combine(wide, local):
@@ -285,8 +297,9 @@
     return pl.pallas_call(
         combine_kernel,
         in_specs=[VM] * 5,
-        out_specs=[VM] * 3,
+        out_specs=[pl.BlockSpec(memory_space=pltpu.HBM)] * 3,
         out_shape=[shape, shape, shape],
+        scratch_shapes=[pltpu.VMEM((3, TOK, HEADS * HD), BF), pltpu.SemaphoreType.DMA((4, 3))],
         compiler_params=small(),
         name="combine",
     )(wide, *local)
@@ -300,10 +313,12 @@
     return place if half == 0 else NX - 1 - place
 
 
-GROUPS = [
-    [place_of(z, column(half, p), c) for z in reversed(range(NZ)) for p in range(2) for c in range(NC)]
-    for half in range(2)
-]
+def groups_of(order):
+    return [[place_of(z, column(half, p), c) for z in order for p in range(2) for c in range(NC)] for half in range(2)]
+
+
+IN_ORDER = (5, 4, 3, 2, 1, 0, 7, 6)
+OUT_ORDER = IN_ORDER
 
 
 def move(value, route):
@@ -320,30 +335,32 @@
     return lax.ppermute(value, ("section", "seq"), pairs)
 
 
-def swap(value):
-    return lax.all_to_all(value, "seq", 0, 0, axis_index_groups=GROUPS, tiled=True)
+def swap(value, order):
+    return lax.all_to_all(value, "seq", 0, 0, axis_index_groups=groups_of(order), tiled=True)
 
 
 def body(queries, key_rows, value_rows, grad_out, log_sums, deltas, offsets):
     seat = lax.axis_index("seq").astype(jnp.int32)
     x = seat // NC % NX
     core = (seat % NC).reshape(1)
-    pos = ((NZ - 1 - seat // (NX * NC)) * 4 + jnp.where(x < 2, x, NX - 1 - x) * 2 + seat % NC).reshape(1)
+    z = seat // (NX * NC)
+    turn = sum(jnp.where(z == at, i, 0) for i, at in enumerate(IN_ORDER))
+    pos = (turn * 4 + jnp.where(x < 2, x, NX - 1 - x) * 2 + seat % NC).reshape(1)
     picked = pick_all(pos, offsets, log_sums, deltas, queries, key_rows, value_rows, grad_out)
-    mine = swap(picked)
+    mine = swap(picked, IN_ORDER)
     grad = move(grad_out, lambda s, x, c: (s - 1, x, c))
     probs, offs = local_scores(offsets, queries, key_rows, log_sums)
     a, b = mine[:, :MAIN], mine[:, MAIN:]
     far_a = move(a, lambda s, x, c: (s, 3 - x, c))
     far_b = move(b, lambda s, x, c: (s - c, 3 - x, c))
     other_a = move(a, lambda s, x, c: (s, x, 1 - c))
-    hop = move(b, lambda s, x, c: (s - 1, x, 1) if c == 1 else None)
-    cross = move(b, lambda s, x, c: (s - c, x, 1 - c))
+    own_b = move(b, lambda s, x, c: (s - c, x, c))
+    other_b = move(own_b, lambda s, x, c: (s, x, 1 - c))
     other_far_a = move(far_a, lambda s, x, c: (s, x, 1 - c))
     other_far_b = move(far_b, lambda s, x, c: (s, x, 1 - c))
     local = local_grads(probs, queries, key_rows, value_rows, grad, deltas)
-    part = near_grads(core, a, b, other_a, hop, cross)
-    back = swap(far_grads(core, far_a, far_b, other_far_a, other_far_b, *part))
+    part = near_grads(core, a, own_b, other_a, other_b)
+    back = swap(far_grads(core, far_a, far_b, other_far_a, other_far_b, *part), OUT_ORDER)
     return tuple(combine(back, (*local, offs)))
 
 

time: 65.3 us -> 57.4 us (0.88)
  starting transfers between devices: 20 us -> 15.5 us
  waiting for transfers between devices: 9.7 us -> 6.67 us
    ppermute x8, starting transfers between devices: 13.8 us -> 8.59 us  [move(): return lax.ppermute(value, ('section', 'seq'), pairs)]
    ppermute x8, waiting for transfers between devices: 7.44 us -> 4.83 us  [move(): return lax.ppermute(value, ('section', 'seq'), pairs)]
  transfers between devices with their start and end apart: 9 -> 9, of which waited for: 3 -> 4; matrix products, arithmetic and copies ran while one was open for 0% -> 0% of each run, Pallas kernels for 12% -> 14%
where the time goes in v7:
time: 57.4 us; the launch traced here: 57.1 us
  blocking collectives  21.7 us (38%)
  starting transfers between devices  15.5 us (27%)
  Pallas kernels  12.3 us (21%)
  waiting for transfers between devices  6.67 us (12%)
  between operations  0.85 us (1%)
    all_to_all x1, blocking collectives, swap(): lax.all_to_all(value, 'seq', 0, 0, axis_index_groups=groups_of(order), ti...  21.7 us
    ppermute x8, starting transfers between devices, move(): return lax.ppermute(value, ('section', 'seq'), pairs)  8.59 us
    all_to_all x1, starting transfers between devices, swap(): lax.all_to_all(value, 'seq', 0, 0, axis_index_groups=groups_of(order), ti...  6.87 us
    ppermute x8, waiting for transfers between devices, move(): return lax.ppermute(value, ('section', 'seq'), pairs)  4.83 us
    pallas_call x1, Pallas kernels, local_grads(): pl.pallas_call(local_kernel, grid=(4,), in_specs=[pl.BlockSpec((4, TOK, T...  3.64 us
    pallas_call x1, Pallas kernels, pick_all(): pl.pallas_call(pick_kernel, in_specs=[SM] + [raw] * 7, out_specs=VM, out_...  3 us
    all_to_all x1, waiting for transfers between devices, swap(): lax.all_to_all(value, 'seq', 0, 0, axis_index_groups=groups_of(order), ti...  1.85 us
    pallas_call x1, Pallas kernels, local_scores(): pl.pallas_call(score_kernel, grid=(4,), in_specs=[SM, wide, wide, stat],...  1.63 us
  transfers between devices with their start and end apart: 9, of which 4 were waited for; matrix products, arithmetic and copies ran while one was open for 0% of the time, Pallas kernels for 14%

profile of v7, /device:TPU:1, one launch (start us, length us, event | category | flops | bytes accessed | tf_op | source)
XLA Modules:
  0.0 57.1 jit_solution(12975400171764777606)
XLA Ops:
  0.7 3.0 %pick_all.1 = bf16[32,40,128]{2,1,0:T(8,128)(2,1)} custom-call(s32[1]{0:T(128)} %bitcast.1.pos_ref, s32[1,16]{1,0:T(1,128)} %off_ref.1, bf16[1,16,128]{2,1,0:T(8,128)(2,1)} %l_ref.1, bf16[1,16,128]{2,1,0:T(8,128)(2,1)} %d_ref.1, bf16[1,128,2048]{2,1,0:T(8,128)(2,1)} %q_ref.3, bf16[1,128,2048]{2,1,0:T(8,128)(2,1)} %k_ref.3, bf16[1,128,2048]{2,1,0:T(8,128)(2,1)} %v_ref.1, ...), custom_call_target="tpu_custom_call" | custom-call | tf_op jit(solution)/shard_map/pick_all/pallas_call | solution.py:98
  3.7 0.0 copy-start.6
  3.7 21.7 %all_to_all.10 = bf16[32,40,128]{2,1,0:T(8,128)(2,1)S(1)} all-to-all(bf16[32,40,128]{2,1,0:T(8,128)(2,1)} %pick_all.1), channel_id=1, replica_groups={{40,41,42,43,32,33,34,35,24,25,26,27,16,17,18,19,8,9,10,11,0,1,2,3,56,5..., dimensions={0} | all-to-all | bytes 655360 | tf_op jit(solution)/shard_map/all_to_all | solution.py:339
  25.5 2.3 %collective-permute-start = (bf16[32,24,128]{2,1,0:T(8,128)(2,1)S(1)}, bf16[32,24,128]{2,1,0:T(8,128)(2,1)S(1)}, u32[]{:S(2)}, u32[]{:S(2)}) collective-permute-start(bf16[32,24,128]{2,1,0:T(8,128)(2,1)S(1)} %slice.8.a_ref), channel_id=1, source_target_pairs={{0,6},{1,7},{2,4},{3,5},{4,2},{5,3},{6,0},{7,1},{8,14},{9,15},{10,... | collective-permute-start | bytes 589832 | tf_op jit(solution)/shard_map/ppermute | solution.py:335
  27.8 4.6 %collective-permute-start.4 = (bf16[32,16,128]{2,1,0:T(8,128)(2,1)S(1)}, bf16[32,16,128]{2,1,0:T(8,128)(2,1)S(1)}, u32[]{:S(2)}, u32[]{:S(2)}) collective-permute-start(bf16[32,16,128]{2,1,0:T(8,128)(2,1)S(1)} %slice.9), channel_id=1, source_target_pairs={{0,0},{1,193},{2,2},{3,195},{4,4},{5,197},{6,6},{7,199},{8,8},{9,2... | collective-permute-start | bytes 393224 | tf_op jit(solution)/shard_map/ppermute | solution.py:335
  32.5 0.7 %collective-permute-start.1 = (bf16[32,16,128]{2,1,0:T(8,128)(2,1)S(1)}, bf16[32,16,128]{2,1,0:T(8,128)(2,1)S(1)}, u32[]{:S(2)}, u32[]{:S(2)}) collective-permute-start(bf16[32,16,128]{2,1,0:T(8,128)(2,1)S(1)} %slice.9), channel_id=1, source_target_pairs={{0,6},{1,199},{2,4},{3,197},{4,2},{5,195},{6,0},{7,193},{8,14},{9,... | collective-permute-start | bytes 393224 | tf_op jit(solution)/shard_map/ppermute | solution.py:335
  33.2 0.2 collective-permute-start.7
  33.3 0.0 collective-permute-start.5
  33.3 0.0 collective-permute-done.a_ref
  33.3 0.8 %collective-permute-start.2 = (bf16[32,24,128]{2,1,0:T(8,128)(2,1)S(1)}, bf16[32,24,128]{2,1,0:T(8,128)(2,1)S(1)}, u32[]{:S(2)}, u32[]{:S(2)}) collective-permute-start(bf16[32,24,128]{2,1,0:T(8,128)(2,1)S(1)} %collective-permute-done.a_ref), channel_id=1, source_target_pairs={{0,1},{1,0},{2,3},{3,2},{4,5},{5,4},{6,7},{7,6},{8,9},{9,8},{10,11... | collective-permute-start | bytes 589832 | tf_op jit(solution)/shard_map/ppermute | solution.py:335
  34.1 1.3 %collective-permute-done.4.b_ref = bf16[32,16,128]{2,1,0:T(8,128)(2,1)S(1)} collective-permute-done((bf16[32,16,128]{2,1,0:T(8,128)(2,1)S(1)}, bf16[32,16,128]{2,1,0:T(8,128)(2,1)S(1)}, u32[]{:S(2)}, u32[]{:S(2)}) %collective-permute-start.4) | collective-permute-done | bytes 131104 | tf_op jit(solution)/shard_map/ppermute | solution.py:335
  35.4 0.0 collective-permute-start.6
  35.4 3.1 %collective-permute-done.1.b_ref = bf16[32,16,128]{2,1,0:T(8,128)(2,1)S(1)} collective-permute-done((bf16[32,16,128]{2,1,0:T(8,128)(2,1)S(1)}, bf16[32,16,128]{2,1,0:T(8,128)(2,1)S(1)}, u32[]{:S(2)}, u32[]{:S(2)}) %collective-permute-start.1) | collective-permute-done | bytes 131104 | tf_op jit(solution)/shard_map/ppermute | solution.py:335
  38.6 0.0 collective-permute-start.3
  38.6 1.0 %near_grads.1 = (bf16[4,256,128]{2,1,0:T(8,128)(2,1)S(1)}, f32[256,128]{1,0:T(8,128)S(1)}, f32[256,128]{1,0:T(8,128)S(1)}, f32[256,128]{1,0:T(8,128)S(1)}, f32[256,128]{1,0:T(8,128)S(1)}) custom-call(s32[1]{0:T(128)} %bitcast.core_ref, bf16[32,24,128]{2,1,0:T(8,128)(2,1)S(1)} %slice.8.a_ref, bf16[32,16,128]{2,1,0:T(8,128)(2,1)S(1)} %collective-permute-done.4.b_ref, ...), custom_call_target="tpu_custom_call" | custom-call | flops 469762048 | bytes 1572864 | tf_op jit(solution)/shard_map/near_grads/pallas_call | solution.py:236
  39.6 0.3 collective-permute-done.3.ob_ref
  39.9 1.5 %far_grads.1 = bf16[32,24,128]{2,1,0:T(8,128)(2,1)} custom-call(s32[1]{0:T(128)} %bitcast.core_ref, bf16[32,24,128]{2,1,0:T(8,128)(2,1)S(1)} %collective-permute-done.a_ref, bf16[32,16,128]{2,1,0:T(8,128)(2,1)S(1)} %collective-permute-done.1.b_ref, bf16[32,24,128]{2,1,0:T(8,128)(2,1)S(1)} %collective-permute-done.2.oa_ref, ...), custom_call_target="tpu_custom_call" | custom-call | tf_op jit(solution)/shard_map/far_grads/pallas_call | solution.py:263
  41.4 6.9 %all-to-all-start.1 = ((bf16[32,24,128]{2,1,0:T(8,128)(2,1)}), bf16[32,24,128]{2,1,0:T(8,128)(2,1)S(1)}, u32[]{:S(2)}, u32[]{:S(2)}) async-start(bf16[32,24,128]{2,1,0:T(8,128)(2,1)} %far_grads.1), calls=%async_computation.1 | async-start | bytes 393216 | tf_op jit(solution)/shard_map/all_to_all | solution.py:339
  48.4 0.0 copy-start.2
  48.4 0.0 copy-start.4
  48.4 1.6 %local_scores.1 = (f32[16,128,128]{2,1,0:T(8,128)S(1)}, s32[16,128]{1,0:T(8,128)S(1)}) custom-call(s32[1,16]{1,0:T(1,128)S(1)} %copy-done.5, bf16[1,128,2048]{2,1,0:T(8,128)(2,1)S(1)} %copy-done, bf16[1,128,2048]{2,1,0:T(8,128)(2,1)S(1)} %copy-done.1, bf16[1,16,128]{2,1,0:T(8,128)(2,1)S(1)} %copy-done.3), custom_call_target="tpu_custom_call" | custom-call | flops 268435456 | bytes 2097152 | tf_op jit(solution)/shard_map/local_scores/pallas_call | solution.py:132
  50.1 3.6 %local_grads.1 = (bf16[128,2048]{1,0:T(8,128)(2,1)S(1)}, bf16[128,2048]{1,0:T(8,128)(2,1)S(1)}, bf16[128,2048]{1,0:T(8,128)(2,1)S(1)}) custom-call(f32[16,128,128]{2,1,0:T(8,128)S(1)} %get-tuple-element.18.p_ref, bf16[1,128,2048]{2,1,0:T(8,128)(2,1)S(1)} %copy-done, bf16[1,128,2048]{2,1,0:T(8,128)(2,1)S(1)} %copy-done.1, ...), custom_call_target="tpu_custom_call" | custom-call | flops 1073741824 | bytes 4718592 | tf_op jit(solution)/shard_map/local_grads/pallas_call | solution.py:168
  53.7 1.8 %all-to-all-done.1.w_ref = bf16[32,24,128]{2,1,0:T(8,128)(2,1)S(1)} async-done(((bf16[32,24,128]{2,1,0:T(8,128)(2,1)}), bf16[32,24,128]{2,1,0:T(8,128)(2,1)S(1)}, u32[]{:S(2)}, u32[]{:S(2)}) %all-to-all-start.1) | async-done | bytes 196640 | tf_op jit(solution)/shard_map/all_to_all | solution.py:339
  55.5 1.5 %combine.1 = (bf16[1,128,2048]{2,1,0:T(8,128)(2,1)}, bf16[1,128,2048]{2,1,0:T(8,128)(2,1)}, bf16[1,128,2048]{2,1,0:T(8,128)(2,1)}) custom-call(bf16[32,24,128]{2,1,0:T(8,128)(2,1)S(1)} %all-to-all-done.1.w_ref, bf16[128,2048]{1,0:T(8,128)(2,1)S(1)} %get-tuple-element.19.dq_ref, bf16[128,2048]{1,0:T(8,128)(2,1)S(1)} %get-tuple-element.20.dk_ref, ...), custom_call_target="tpu_custom_call" | custom-call | tf_op jit(solution)/shard_map/combine/pallas_call | solution.py:297
  (17 shorter events, 0.1 us)
Async XLA Ops:
  3.7 29.4 %copy-start.6 = (bf16[1,128,2048]{2,1,0:T(8,128)(2,1)S(1)}, bf16[1,128,2048]{2,1,0:T(8,128)(2,1)}, u32[]{:S(2)}) copy-start(bf16[1,128,2048]{2,1,0:T(8,128)(2,1)} %g_hbm.1) | copy-start | bytes 1572868
  25.5 7.9 %collective-permute-start = (bf16[32,24,128]{2,1,0:T(8,128)(2,1)S(1)}, bf16[32,24,128]{2,1,0:T(8,128)(2,1)S(1)}, u32[]{:S(2)}, u32[]{:S(2)}) collective-permute-start(bf16[32,24,128]{2,1,0:T(8,128)(2,1)S(1)} %slice.8.a_ref), channel_id=1, source_target_pairs={{0,6},{1,7},{2,4},{3,5},{4,2},{5,3},{6,0},{7,1},{8,14},{9,15},{10,... | collective-permute-start | bytes 589832 | tf_op jit(solution)/shard_map/ppermute | solution.py:335
  27.8 7.6 %collective-permute-start.4 = (bf16[32,16,128]{2,1,0:T(8,128)(2,1)S(1)}, bf16[32,16,128]{2,1,0:T(8,128)(2,1)S(1)}, u32[]{:S(2)}, u32[]{:S(2)}) collective-permute-start(bf16[32,16,128]{2,1,0:T(8,128)(2,1)S(1)} %slice.9), channel_id=1, source_target_pairs={{0,0},{1,193},{2,2},{3,195},{4,4},{5,197},{6,6},{7,199},{8,8},{9,2... | collective-permute-start | bytes 393224 | tf_op jit(solution)/shard_map/ppermute | solution.py:335
  32.5 6.1 %collective-permute-start.1 = (bf16[32,16,128]{2,1,0:T(8,128)(2,1)S(1)}, bf16[32,16,128]{2,1,0:T(8,128)(2,1)S(1)}, u32[]{:S(2)}, u32[]{:S(2)}) collective-permute-start(bf16[32,16,128]{2,1,0:T(8,128)(2,1)S(1)} %slice.9), channel_id=1, source_target_pairs={{0,6},{1,199},{2,4},{3,197},{4,2},{5,195},{6,0},{7,193},{8,14},{9,... | collective-permute-start | bytes 393224 | tf_op jit(solution)/shard_map/ppermute | solution.py:335
  33.2 16.9 %collective-permute-start.7 = (bf16[1,128,2048]{2,1,0:T(8,128)(2,1)S(1)}, bf16[1,128,2048]{2,1,0:T(8,128)(2,1)S(1)}, u32[]{:S(2)}, u32[]{:S(2)}) collective-permute-start(bf16[1,128,2048]{2,1,0:T(8,128)(2,1)S(1)} %copy-done.6), channel_id=1, source_target_pairs={{0,192},{1,193},{2,194},{3,195},{4,196},{5,197},{6,198},{7,199},{8... | collective-permute-start | bytes 1572872 | tf_op jit(solution)/shard_map/ppermute | solution.py:335
  33.3 5.3 %collective-permute-start.5 = (bf16[32,24,128]{2,1,0:T(8,128)(2,1)S(1)}, bf16[32,24,128]{2,1,0:T(8,128)(2,1)S(1)}, u32[]{:S(2)}, u32[]{:S(2)}) collective-permute-start(bf16[32,24,128]{2,1,0:T(8,128)(2,1)S(1)} %slice.8.a_ref), channel_id=1, source_target_pairs={{0,1},{1,0},{2,3},{3,2},{4,5},{5,4},{6,7},{7,6},{8,9},{9,8},{10,11... | collective-permute-start | bytes 589832 | tf_op jit(solution)/shard_map/ppermute | solution.py:335
  33.3 6.6 %collective-permute-start.2 = (bf16[32,24,128]{2,1,0:T(8,128)(2,1)S(1)}, bf16[32,24,128]{2,1,0:T(8,128)(2,1)S(1)}, u32[]{:S(2)}, u32[]{:S(2)}) collective-permute-start(bf16[32,24,128]{2,1,0:T(8,128)(2,1)S(1)} %collective-permute-done.a_ref), channel_id=1, source_target_pairs={{0,1},{1,0},{2,3},{3,2},{4,5},{5,4},{6,7},{7,6},{8,9},{9,8},{10,11... | collective-permute-start | bytes 589832 | tf_op jit(solution)/shard_map/ppermute | solution.py:335
  35.4 3.2 %collective-permute-start.6 = (bf16[32,16,128]{2,1,0:T(8,128)(2,1)S(1)}, bf16[32,16,128]{2,1,0:T(8,128)(2,1)S(1)}, u32[]{:S(2)}, u32[]{:S(2)}) collective-permute-start(bf16[32,16,128]{2,1,0:T(8,128)(2,1)S(1)} %collective-permute-done.4.b_ref), channel_id=1, source_target_pairs={{0,1},{1,0},{2,3},{3,2},{4,5},{5,4},{6,7},{7,6},{8,9},{9,8},{10,11... | collective-permute-start | bytes 393224 | tf_op jit(solution)/shard_map/ppermute | solution.py:335
  38.6 1.3 %collective-permute-start.3 = (bf16[32,16,128]{2,1,0:T(8,128)(2,1)S(1)}, bf16[32,16,128]{2,1,0:T(8,128)(2,1)S(1)}, u32[]{:S(2)}, u32[]{:S(2)}) collective-permute-start(bf16[32,16,128]{2,1,0:T(8,128)(2,1)S(1)} %collective-permute-done.1.b_ref), channel_id=1, source_target_pairs={{0,1},{1,0},{2,3},{3,2},{4,5},{5,4},{6,7},{7,6},{8,9},{9,8},{10,11... | collective-permute-start | bytes 393224 | tf_op jit(solution)/shard_map/ppermute | solution.py:335
  39.9 8.4 %copy-start = (bf16[1,128,2048]{2,1,0:T(8,128)(2,1)S(1)}, bf16[1,128,2048]{2,1,0:T(8,128)(2,1)}, u32[]{:S(2)}) copy-start(bf16[1,128,2048]{2,1,0:T(8,128)(2,1)} %q_ref.3) | copy-start | bytes 1572868
  39.9 8.4 %copy-start.1 = (bf16[1,128,2048]{2,1,0:T(8,128)(2,1)S(1)}, bf16[1,128,2048]{2,1,0:T(8,128)(2,1)}, u32[]{:S(2)}) copy-start(bf16[1,128,2048]{2,1,0:T(8,128)(2,1)} %k_ref.3) | copy-start | bytes 1572868
  41.4 6.9 %copy-start.3 = (bf16[1,16,128]{2,1,0:T(8,128)(2,1)S(1)}, bf16[1,16,128]{2,1,0:T(8,128)(2,1)}, u32[]{:S(2)}) copy-start(bf16[1,16,128]{2,1,0:T(8,128)(2,1)} %l_ref.1) | copy-start | bytes 12292
  41.4 6.9 %copy-start.5 = (s32[1,16]{1,0:T(1,128)S(1)}, s32[1,16]{1,0:T(1,128)}, u32[]{:S(2)}) copy-start(s32[1,16]{1,0:T(1,128)} %off_ref.1) | copy-start | bytes 196
  41.4 14.1 %all-to-all-start.1 = ((bf16[32,24,128]{2,1,0:T(8,128)(2,1)}), bf16[32,24,128]{2,1,0:T(8,128)(2,1)S(1)}, u32[]{:S(2)}, u32[]{:S(2)}) async-start(bf16[32,24,128]{2,1,0:T(8,128)(2,1)} %far_grads.1), calls=%async_computation.1 | async-start | bytes 393216 | tf_op jit(solution)/shard_map/all_to_all | solution.py:339
  48.4 1.7 %copy-start.2 = (bf16[1,128,2048]{2,1,0:T(8,128)(2,1)S(1)}, bf16[1,128,2048]{2,1,0:T(8,128)(2,1)}, u32[]{:S(2)}) copy-start(bf16[1,128,2048]{2,1,0:T(8,128)(2,1)} %v_ref.1) | copy-start | bytes 1572868
  48.4 1.7 %copy-start.4 = (bf16[1,16,128]{2,1,0:T(8,128)(2,1)S(1)}, bf16[1,16,128]{2,1,0:T(8,128)(2,1)}, u32[]{:S(2)}) copy-start(bf16[1,16,128]{2,1,0:T(8,128)(2,1)} %d_ref.1) | copy-start | bytes 12292

commit v8 on v7

--- a/solution.py
+++ b/solution.py
@@ -46,18 +46,18 @@
     return pltpu.CompilerParams(vmem_limit_bytes=mib << 20)
 
 
-def pick_kernel(pos_ref, off_hbm, l_hbm, d_hbm, q_hbm, k_hbm, v_hbm, g_hbm, o_ref, off_ref, l_ref, d_ref, x_ref, sems):
+def pick_kernel(pos_ref, off_hbm, l_hbm, d_hbm, q_hbm, k_hbm, v_hbm, g_hbm, o_hbm, off_ref, l_ref, d_ref, x_ref, o_ref, sems, out_sems):
     loads = [
         pltpu.make_async_copy(src, dst, sems.at[i])
         for i, (src, dst) in enumerate(
             (
                 (off_hbm, off_ref),
+                (l_hbm.at[0], l_ref),
+                (d_hbm.at[0], d_ref),
                 (q_hbm.at[0], x_ref.at[0]),
                 (k_hbm.at[0], x_ref.at[1]),
                 (v_hbm.at[0], x_ref.at[2]),
                 (g_hbm.at[0], x_ref.at[3]),
-                (l_hbm.at[0], l_ref),
-                (d_hbm.at[0], d_ref),
             )
         )
     ]
@@ -67,15 +67,8 @@
     src = lax.broadcasted_iota(jnp.int32, (TOK, TOK), 0)
     dst = lax.broadcasted_iota(jnp.int32, (TOK, TOK), 1)
     place = jnp.where(dst == (n % 8) * PICK + src // RATE, 1.0, 0.0).astype(BF)
-    loads[0].wait()
-    choose = [chooser(off_ref[0, h]) for h in range(HEADS)]
-    for part, core, first in ((0, 0, 0), (1, 0, MAIN), (2, 1, 0), (3, 1, MAIN)):
-        loads[1 + part].wait()
-        for h in range(HEADS):
-            rows = dot(choose[h], x_ref[part, :, h * HD:(h + 1) * HD])
-            o_ref[2 * h + core, first:first + 16] = rows.astype(BF)
-    loads[5].wait()
-    loads[6].wait()
+    for load in loads[:3]:
+        load.wait()
     head = lax.broadcasted_iota(jnp.int32, (HEADS, TOK), 0)
     lane = lax.broadcasted_iota(jnp.int32, (HEADS, TOK), 1)
     off = jnp.zeros((HEADS, TOK), jnp.int32)
@@ -89,8 +82,21 @@
         lse = jnp.broadcast_to(lses[h:h + 1], (8, HD))
         dlt = jnp.broadcast_to(dlts[h:h + 1], (8, HD))
         stats = jnp.where(row == n // 8, lse, jnp.where(row == 4 + n // 8, dlt, 0.0))
-        o_ref[2 * h, 16:MAIN] = stats.astype(BF)
-        o_ref[2 * h + 1, 16:MAIN] = jnp.zeros((8, HD), BF)
+        o_ref[h, 0, 16:MAIN] = stats.astype(BF)
+        o_ref[h, 1, 16:MAIN] = jnp.zeros((8, HD), BF)
+    choose = [chooser(off_ref[0, h]) for h in range(HEADS)]
+    stores = []
+    for core in range(2):
+        for part, first in ((2 * core, 0), (2 * core + 1, MAIN)):
+            loads[3 + part].wait()
+            for h in range(HEADS):
+                rows = dot(choose[h], x_ref[part, :, h * HD:(h + 1) * HD])
+                o_ref[h, core, first:first + 16] = rows.astype(BF)
+        store = pltpu.make_async_copy(o_ref.at[:, core], o_hbm.at[:, core], out_sems.at[core])
+        store.start()
+        stores.append(store)
+    for store in stores:
+        store.wait()
 
 
 def pick_all(pos, offsets, lse, delta, query, key, value, grad):
@@ -98,17 +104,19 @@
     return pl.pallas_call(
         pick_kernel,
         in_specs=[SM] + [raw] * 7,
-        out_specs=VM,
-        out_shape=jax.ShapeDtypeStruct((GROUP, ROWS, HD), BF),
+        out_specs=raw,
+        out_shape=jax.ShapeDtypeStruct((HEADS, 2, ROWS, HD), BF),
         scratch_shapes=[
             pltpu.SMEM((1, HEADS), jnp.int32),
             pltpu.VMEM((HEADS, TOK), BF),
             pltpu.VMEM((HEADS, TOK), BF),
             pltpu.VMEM((4, TOK, HEADS * HD), BF),
+            pltpu.VMEM((HEADS, 2, ROWS, HD), BF),
             pltpu.SemaphoreType.DMA((7,)),
+            pltpu.SemaphoreType.DMA((2,)),
         ],
         name="pick_all",
-    )(pos, offsets, lse, delta, query, key, value, grad)
+    )(pos, offsets, lse, delta, query, key, value, grad).reshape(GROUP, ROWS, HD)
 
 
 def score_kernel(off_ref, q_ref, k_ref, l_ref, p_ref, offs_ref, st_ref):
@@ -142,7 +150,7 @@
     )(offsets, query, key, lse)
 
 
-def local_kernel(p_ref, q_ref, k_ref, v_ref, g_ref, d_ref, dq_ref, dk_ref, dv_ref, st_ref):
+def local_kernel(p_ref, q_ref, k_ref, v_ref, g0_ref, g1_ref, d_ref, dq_ref, dk_ref, dv_ref, st_ref):
     step = pl.program_id(0)
 
     @pl.when(step == 0)
@@ -152,7 +160,8 @@
     dlts = st_ref[pl.ds(pl.multiple_of(step * 4, 4), 4), :]
     for i in range(4):
         cols = slice(i * HD, (i + 1) * HD)
-        q, k, v, g = q_ref[0, :, cols], k_ref[0, :, cols], v_ref[0, :, cols], g_ref[0, :, cols]
+        q, k, v = q_ref[0, :, cols], k_ref[0, :, cols], v_ref[0, :, cols]
+        g = jnp.concatenate([g0_ref[0, :, cols], g1_ref[0, :, cols]], axis=0)
         p = p_ref[i]
         ds = (p * (dot_t(v, g) - dlts[i:i + 1])).astype(BF)
         dv_ref[:, cols] = dot(p.astype(BF), g).astype(BF)
@@ -160,22 +169,23 @@
         dq_ref[:, cols] = (dot_l(ds, k) * SCALE).astype(BF)
 
 
-def local_grads(probs, query, key, value, grad, delta):
+def local_grads(probs, query, key, value, grad0, grad1, delta):
     wide = pl.BlockSpec((1, TOK, 4 * HD), lambda i: (0, 0, i))
+    half = pl.BlockSpec((1, TOK // 2, 4 * HD), lambda i: (0, 0, i))
     out = pl.BlockSpec((TOK, 4 * HD), lambda i: (0, i))
     stat = pl.BlockSpec((1, HEADS, TOK), lambda i: (0, 0, 0))
     shape = jax.ShapeDtypeStruct((TOK, HEADS * HD), BF)
     return pl.pallas_call(
         local_kernel,
         grid=(4,),
-        in_specs=[pl.BlockSpec((4, TOK, TOK), lambda i: (i, 0, 0)), wide, wide, wide, wide, stat],
+        in_specs=[pl.BlockSpec((4, TOK, TOK), lambda i: (i, 0, 0)), wide, wide, wide, half, half, stat],
         out_specs=[out, out, out],
         out_shape=[shape, shape, shape],
         scratch_shapes=[pltpu.VMEM((HEADS, TOK), F32)],
         compiler_params=small(),
         cost_estimate=pl.CostEstimate(flops=16 * 4 * 2 * 128 ** 3 * 4, bytes_accessed=4718592, transcendentals=0),
         name="local_grads",
-    )(probs, query, key, value, grad, delta)
+    )(probs, query, key, value, grad0, grad1, delta)
 
 
 def query_side(q, g, k, v, lse, dlt):
@@ -348,7 +358,8 @@
     pos = (turn * 4 + jnp.where(x < 2, x, NX - 1 - x) * 2 + seat % NC).reshape(1)
     picked = pick_all(pos, offsets, log_sums, deltas, queries, key_rows, value_rows, grad_out)
     mine = swap(picked, IN_ORDER)
-    grad = move(grad_out, lambda s, x, c: (s - 1, x, c))
+    grad0 = move(grad_out[:, :TOK // 2], lambda s, x, c: (s - 1, x, c))
+    grad1 = move(grad_out[:, TOK // 2:], lambda s, x, c: (s - 1, x, c))
     probs, offs = local_scores(offsets, queries, key_rows, log_sums)
     a, b = mine[:, :MAIN], mine[:, MAIN:]
     far_a = move(a, lambda s, x, c: (s, 3 - x, c))
@@ -358,7 +369,7 @@
     other_b = move(own_b, lambda s, x, c: (s, x, 1 - c))
     other_far_a = move(far_a, lambda s, x, c: (s, x, 1 - c))
     other_far_b = move(far_b, lambda s, x, c: (s, x, 1 - c))
-    local = local_grads(probs, queries, key_rows, value_rows, grad, deltas)
+    local = local_grads(probs, queries, key_rows, value_rows, grad0, grad1, deltas)
     part = near_grads(core, a, own_b, other_a, other_b)
     back = swap(far_grads(core, far_a, far_b, other_far_a, other_far_b, *part), OUT_ORDER)
     return tuple(combine(back, (*local, offs)))

time: 57.4 us -> 66.7 us (1.16)
  waiting for transfers between devices: 6.67 us -> 14.4 us
  starting transfers between devices: 15.5 us -> 17.3 us
    ppermute x8 -> x9, waiting for transfers between devices: 4.83 us -> 14.4 us  [move(): return lax.ppermute(value, ('section', 'seq'), pairs)]
    all_to_all x1, waiting for transfers between devices: 1.85 us -> 0.01 us  [swap(): lax.all_to_all(value, 'seq', 0, 0, axis_index_groups=groups_of(order), ti...]
    ppermute x8 -> x9, starting transfers between devices: 8.59 us -> 10.4 us  [move(): return lax.ppermute(value, ('section', 'seq'), pairs)]
  transfers between devices with their start and end apart: 9 -> 10, of which waited for: 4 -> 5; matrix products, arithmetic and copies ran while one was open for 0% -> 0% of each run, Pallas kernels for 14% -> 9%
where the time goes in v8:
time: 66.7 us; the launch traced here: 66.4 us
  blocking collectives  21.6 us (32%)
  starting transfers between devices  17.3 us (26%)
  waiting for transfers between devices  14.4 us (22%)
  Pallas kernels  12.2 us (18%)
  between operations  0.83 us (1%)
    all_to_all x1, blocking collectives, swap(): lax.all_to_all(value, 'seq', 0, 0, axis_index_groups=groups_of(order), ti...  21.6 us
    ppermute x9, waiting for transfers between devices, move(): return lax.ppermute(value, ('section', 'seq'), pairs)  14.4 us
    ppermute x9, starting transfers between devices, move(): return lax.ppermute(value, ('section', 'seq'), pairs)  10.4 us
    all_to_all x1, starting transfers between devices, swap(): lax.all_to_all(value, 'seq', 0, 0, axis_index_groups=groups_of(order), ti...  6.85 us
    pallas_call x1, Pallas kernels, local_grads(): pl.pallas_call(local_kernel, grid=(4,), in_specs=[pl.BlockSpec((4, TOK, T...  3.65 us
    pallas_call x1, Pallas kernels, pick_all(): pl.pallas_call(pick_kernel, in_specs=[SM] + [raw] * 7, out_specs=raw, out...  2.84 us
    pallas_call x1, Pallas kernels, local_scores(): pl.pallas_call(score_kernel, grid=(4,), in_specs=[SM, wide, wide, stat],...  1.63 us
    pallas_call x1, Pallas kernels, combine(): pl.pallas_call(combine_kernel, in_specs=[VM] * 5, out_specs=[pl.BlockSpec...  1.54 us
  transfers between devices with their start and end apart: 10, of which 5 were waited for; matrix products, arithmetic and copies ran while one was open for 0% of the time, Pallas kernels for 9%

profile of v8, /device:TPU:1, one launch (start us, length us, event | category | flops | bytes accessed | tf_op | source)
XLA Modules:
  0.0 66.4 jit_solution(3778621301685933769)
XLA Ops:
  0.7 2.8 %pick_all.1 = bf16[16,2,40,128]{3,2,1,0:T(8,128)(2,1)} custom-call(s32[1]{0:T(128)} %bitcast.1.pos_ref, s32[1,16]{1,0:T(1,128)} %off_ref.1, bf16[1,16,128]{2,1,0:T(8,128)(2,1)} %l_ref.1, bf16[1,16,128]{2,1,0:T(8,128)(2,1)} %d_ref.1, bf16[1,128,2048]{2,1,0:T(8,128)(2,1)} %q_ref.3, bf16[1,128,2048]{2,1,0:T(8,128)(2,1)} %k_ref.3, bf16[1,128,2048]{2,1,0:T(8,128)(2,1)} %v_ref.1, ...), custom_call_target="tpu_custom_call" | custom-call | tf_op jit(solution)/shard_map/pick_all/pallas_call | solution.py:104
  3.6 21.6 %all_to_all.10 = bf16[32,40,128]{2,1,0:T(8,128)(2,1)S(1)} all-to-all(bf16[32,40,128]{2,1,0:T(8,128)(2,1)} %bitcast.3), channel_id=1, replica_groups={{40,41,42,43,32,33,34,35,24,25,26,27,16,17,18,19,8,9,10,11,0,1,2,3,56,5..., dimensions={0} | all-to-all | bytes 655360 | tf_op jit(solution)/shard_map/all_to_all | solution.py:349
  25.2 2.3 %collective-permute-start = (bf16[32,24,128]{2,1,0:T(8,128)(2,1)S(1)}, bf16[32,24,128]{2,1,0:T(8,128)(2,1)S(1)}, u32[]{:S(2)}, u32[]{:S(2)}) collective-permute-start(bf16[32,24,128]{2,1,0:T(8,128)(2,1)S(1)} %slice.16.a_ref), channel_id=1, source_target_pairs={{0,6},{1,7},{2,4},{3,5},{4,2},{5,3},{6,0},{7,1},{8,14},{9,15},{10,... | collective-permute-start | bytes 589832 | tf_op jit(solution)/shard_map/ppermute | solution.py:345
  27.5 4.6 %collective-permute-start.4 = (bf16[32,16,128]{2,1,0:T(8,128)(2,1)S(1)}, bf16[32,16,128]{2,1,0:T(8,128)(2,1)S(1)}, u32[]{:S(2)}, u32[]{:S(2)}) collective-permute-start(bf16[32,16,128]{2,1,0:T(8,128)(2,1)S(1)} %slice.17), channel_id=1, source_target_pairs={{0,0},{1,193},{2,2},{3,195},{4,4},{5,197},{6,6},{7,199},{8,8},{9,2... | collective-permute-start | bytes 393224 | tf_op jit(solution)/shard_map/ppermute | solution.py:345
  32.2 0.7 %collective-permute-start.1 = (bf16[32,16,128]{2,1,0:T(8,128)(2,1)S(1)}, bf16[32,16,128]{2,1,0:T(8,128)(2,1)S(1)}, u32[]{:S(2)}, u32[]{:S(2)}) collective-permute-start(bf16[32,16,128]{2,1,0:T(8,128)(2,1)S(1)} %slice.17), channel_id=1, source_target_pairs={{0,6},{1,199},{2,4},{3,197},{4,2},{5,195},{6,0},{7,193},{8,14},{9,... | collective-permute-start | bytes 393224 | tf_op jit(solution)/shard_map/ppermute | solution.py:345
  32.9 0.0 collective-permute-done.a_ref
  32.9 0.9 %collective-permute-start.2 = (bf16[32,24,128]{2,1,0:T(8,128)(2,1)S(1)}, bf16[32,24,128]{2,1,0:T(8,128)(2,1)S(1)}, u32[]{:S(2)}, u32[]{:S(2)}) collective-permute-start(bf16[32,24,128]{2,1,0:T(8,128)(2,1)S(1)} %collective-permute-done.a_ref), channel_id=1, source_target_pairs={{0,1},{1,0},{2,3},{3,2},{4,5},{5,4},{6,7},{7,6},{8,9},{9,8},{10,11... | collective-permute-start | bytes 589832 | tf_op jit(solution)/shard_map/ppermute | solution.py:345
  33.8 0.3 collective-permute-done.4.b_ref
  34.1 4.1 %collective-permute-done.1.b_ref = bf16[32,16,128]{2,1,0:T(8,128)(2,1)S(1)} collective-permute-done((bf16[32,16,128]{2,1,0:T(8,128)(2,1)S(1)}, bf16[32,16,128]{2,1,0:T(8,128)(2,1)S(1)}, u32[]{:S(2)}, u32[]{:S(2)}) %collective-permute-start.1) | collective-permute-done | bytes 131104 | tf_op jit(solution)/shard_map/ppermute | solution.py:345
  38.2 0.0 collective-permute-start.3
  38.2 1.0 %near_grads.1 = (bf16[4,256,128]{2,1,0:T(8,128)(2,1)S(1)}, f32[256,128]{1,0:T(8,128)S(1)}, f32[256,128]{1,0:T(8,128)S(1)}, f32[256,128]{1,0:T(8,128)S(1)}, f32[256,128]{1,0:T(8,128)S(1)}) custom-call(s32[1]{0:T(128)} %bitcast.core_ref, bf16[32,24,128]{2,1,0:T(8,128)(2,1)S(1)} %slice.16.a_ref, bf16[32,16,128]{2,1,0:T(8,128)(2,1)S(1)} %collective-permute-done.4.b_ref, ...), custom_call_target="tpu_custom_call" | custom-call | flops 469762048 | bytes 1572864 | tf_op jit(solution)/shard_map/near_grads/pallas_call | solution.py:246
  39.2 0.3 collective-permute-done.3.ob_ref
  39.5 1.5 %far_grads.1 = bf16[32,24,128]{2,1,0:T(8,128)(2,1)} custom-call(s32[1]{0:T(128)} %bitcast.core_ref, bf16[32,24,128]{2,1,0:T(8,128)(2,1)S(1)} %collective-permute-done.a_ref, bf16[32,16,128]{2,1,0:T(8,128)(2,1)S(1)} %collective-permute-done.1.b_ref, bf16[32,24,128]{2,1,0:T(8,128)(2,1)S(1)} %collective-permute-done.2.oa_ref, ...), custom_call_target="tpu_custom_call" | custom-call | tf_op jit(solution)/shard_map/far_grads/pallas_call | solution.py:273
  41.0 6.9 %all-to-all-start.1 = ((bf16[32,24,128]{2,1,0:T(8,128)(2,1)}), bf16[32,24,128]{2,1,0:T(8,128)(2,1)S(1)}, u32[]{:S(2)}, u32[]{:S(2)}) async-start(bf16[32,24,128]{2,1,0:T(8,128)(2,1)} %far_grads.1), calls=%async_computation.1 | async-start | bytes 393216 | tf_op jit(solution)/shard_map/all_to_all | solution.py:349
  47.9 0.0 copy-start
  47.9 0.0 copy-start.1
  48.0 0.0 copy-start.5
  48.0 1.8 %collective-permute-start.8 = (bf16[1,64,2048]{2,1,0:T(8,128)(2,1)S(1)}, bf16[1,64,2048]{2,1,0:T(8,128)(2,1)S(1)}, u32[]{:S(2)}, u32[]{:S(2)}) collective-permute-start(bf16[1,64,2048]{2,1,0:T(8,128)(2,1)S(1)} %get-tuple-element.23), channel_id=1, source_target_pairs={{0,192},{1,193},{2,194},{3,195},{4,196},{5,197},{6,198},{7,199},{8... | collective-permute-start | bytes 786440 | tf_op jit(solution)/shard_map/ppermute | solution.py:345
  49.8 0.1 collective-permute-start.7
  49.9 1.6 %local_scores.1 = (f32[16,128,128]{2,1,0:T(8,128)S(1)}, s32[16,128]{1,0:T(8,128)S(1)}) custom-call(s32[1,16]{1,0:T(1,128)S(1)} %copy-done.5, bf16[1,128,2048]{2,1,0:T(8,128)(2,1)S(1)} %copy-done, bf16[1,128,2048]{2,1,0:T(8,128)(2,1)S(1)} %copy-done.1, bf16[1,16,128]{2,1,0:T(8,128)(2,1)S(1)} %copy-done.3), custom_call_target="tpu_custom_call" | custom-call | flops 268435456 | bytes 2097152 | tf_op jit(solution)/shard_map/local_scores/pallas_call | solution.py:140
  51.5 4.0 %collective-permute-done.8.g1_ref = bf16[1,64,2048]{2,1,0:T(8,128)(2,1)S(1)} collective-permute-done((bf16[1,64,2048]{2,1,0:T(8,128)(2,1)S(1)}, bf16[1,64,2048]{2,1,0:T(8,128)(2,1)S(1)}, u32[]{:S(2)}, u32[]{:S(2)}) %collective-permute-start.8) | collective-permute-done | bytes 262176 | tf_op jit(solution)/shard_map/ppermute | solution.py:345
  55.6 5.6 %collective-permute-done.7.g0_ref = bf16[1,64,2048]{2,1,0:T(8,128)(2,1)S(1)} collective-permute-done((bf16[1,64,2048]{2,1,0:T(8,128)(2,1)S(1)}, bf16[1,64,2048]{2,1,0:T(8,128)(2,1)S(1)}, u32[]{:S(2)}, u32[]{:S(2)}) %collective-permute-start.7) | collective-permute-done | bytes 262176 | tf_op jit(solution)/shard_map/ppermute | solution.py:345
  61.2 3.7 %local_grads.1 = (bf16[128,2048]{1,0:T(8,128)(2,1)S(1)}, bf16[128,2048]{1,0:T(8,128)(2,1)S(1)}, bf16[128,2048]{1,0:T(8,128)(2,1)S(1)}) custom-call(f32[16,128,128]{2,1,0:T(8,128)S(1)} %get-tuple-element.18.p_ref, bf16[1,128,2048]{2,1,0:T(8,128)(2,1)S(1)} %copy-done, bf16[1,128,2048]{2,1,0:T(8,128)(2,1)S(1)} %copy-done.1, ...), custom_call_target="tpu_custom_call" | custom-call | flops 1073741824 | bytes 4718592 | tf_op jit(solution)/shard_map/local_grads/pallas_call | solution.py:178
  64.8 1.5 %combine.1 = (bf16[1,128,2048]{2,1,0:T(8,128)(2,1)}, bf16[1,128,2048]{2,1,0:T(8,128)(2,1)}, bf16[1,128,2048]{2,1,0:T(8,128)(2,1)}) custom-call(bf16[32,24,128]{2,1,0:T(8,128)(2,1)S(1)} %all-to-all-done.1.w_ref, bf16[128,2048]{1,0:T(8,128)(2,1)S(1)} %get-tuple-element.19.dq_ref, bf16[128,2048]{1,0:T(8,128)(2,1)S(1)} %get-tuple-element.20.dk_ref, ...), custom_call_target="tpu_custom_call" | custom-call | tf_op jit(solution)/shard_map/combine/pallas_call | solution.py:307
  (20 shorter events, 0.1 us)
Async XLA Ops:
  25.2 7.7 %collective-permute-start = (bf16[32,24,128]{2,1,0:T(8,128)(2,1)S(1)}, bf16[32,24,128]{2,1,0:T(8,128)(2,1)S(1)}, u32[]{:S(2)}, u32[]{:S(2)}) collective-permute-start(bf16[32,24,128]{2,1,0:T(8,128)(2,1)S(1)} %slice.16.a_ref), channel_id=1, source_target_pairs={{0,6},{1,7},{2,4},{3,5},{4,2},{5,3},{6,0},{7,1},{8,14},{9,15},{10,... | collective-permute-start | bytes 589832 | tf_op jit(solution)/shard_map/ppermute | solution.py:345
  27.5 6.6 %collective-permute-start.4 = (bf16[32,16,128]{2,1,0:T(8,128)(2,1)S(1)}, bf16[32,16,128]{2,1,0:T(8,128)(2,1)S(1)}, u32[]{:S(2)}, u32[]{:S(2)}) collective-permute-start(bf16[32,16,128]{2,1,0:T(8,128)(2,1)S(1)} %slice.17), channel_id=1, source_target_pairs={{0,0},{1,193},{2,2},{3,195},{4,4},{5,197},{6,6},{7,199},{8,8},{9,2... | collective-permute-start | bytes 393224 | tf_op jit(solution)/shard_map/ppermute | solution.py:345
  32.2 6.0 %collective-permute-start.1 = (bf16[32,16,128]{2,1,0:T(8,128)(2,1)S(1)}, bf16[32,16,128]{2,1,0:T(8,128)(2,1)S(1)}, u32[]{:S(2)}, u32[]{:S(2)}) collective-permute-start(bf16[32,16,128]{2,1,0:T(8,128)(2,1)S(1)} %slice.17), channel_id=1, source_target_pairs={{0,6},{1,199},{2,4},{3,197},{4,2},{5,195},{6,0},{7,193},{8,14},{9,... | collective-permute-start | bytes 393224 | tf_op jit(solution)/shard_map/ppermute | solution.py:345
  32.9 5.3 %collective-permute-start.5 = (bf16[32,24,128]{2,1,0:T(8,128)(2,1)S(1)}, bf16[32,24,128]{2,1,0:T(8,128)(2,1)S(1)}, u32[]{:S(2)}, u32[]{:S(2)}) collective-permute-start(bf16[32,24,128]{2,1,0:T(8,128)(2,1)S(1)} %slice.16.a_ref), channel_id=1, source_target_pairs={{0,1},{1,0},{2,3},{3,2},{4,5},{5,4},{6,7},{7,6},{8,9},{9,8},{10,11... | collective-permute-start | bytes 589832 | tf_op jit(solution)/shard_map/ppermute | solution.py:345
  32.9 6.6 %collective-permute-start.2 = (bf16[32,24,128]{2,1,0:T(8,128)(2,1)S(1)}, bf16[32,24,128]{2,1,0:T(8,128)(2,1)S(1)}, u32[]{:S(2)}, u32[]{:S(2)}) collective-permute-start(bf16[32,24,128]{2,1,0:T(8,128)(2,1)S(1)} %collective-permute-done.a_ref), channel_id=1, source_target_pairs={{0,1},{1,0},{2,3},{3,2},{4,5},{5,4},{6,7},{7,6},{8,9},{9,8},{10,11... | collective-permute-start | bytes 589832 | tf_op jit(solution)/shard_map/ppermute | solution.py:345
  34.1 4.1 %collective-permute-start.6 = (bf16[32,16,128]{2,1,0:T(8,128)(2,1)S(1)}, bf16[32,16,128]{2,1,0:T(8,128)(2,1)S(1)}, u32[]{:S(2)}, u32[]{:S(2)}) collective-permute-start(bf16[32,16,128]{2,1,0:T(8,128)(2,1)S(1)} %collective-permute-done.4.b_ref), channel_id=1, source_target_pairs={{0,1},{1,0},{2,3},{3,2},{4,5},{5,4},{6,7},{7,6},{8,9},{9,8},{10,11... | collective-permute-start | bytes 393224 | tf_op jit(solution)/shard_map/ppermute | solution.py:345
  38.2 1.3 %collective-permute-start.3 = (bf16[32,16,128]{2,1,0:T(8,128)(2,1)S(1)}, bf16[32,16,128]{2,1,0:T(8,128)(2,1)S(1)}, u32[]{:S(2)}, u32[]{:S(2)}) collective-permute-start(bf16[32,16,128]{2,1,0:T(8,128)(2,1)S(1)} %collective-permute-done.1.b_ref), channel_id=1, source_target_pairs={{0,1},{1,0},{2,3},{3,2},{4,5},{5,4},{6,7},{7,6},{8,9},{9,8},{10,11... | collective-permute-start | bytes 393224 | tf_op jit(solution)/shard_map/ppermute | solution.py:345
  39.5 8.4 %copy-start.6 = (bf16[1,128,2048]{2,1,0:T(8,128)(2,1)S(1)}, bf16[1,128,2048]{2,1,0:T(8,128)(2,1)}, u32[]{:S(2)}) copy-start(bf16[1,128,2048]{2,1,0:T(8,128)(2,1)} %g_hbm.1) | copy-start | bytes 1572868
  41.0 8.8 %copy-start.3 = (bf16[1,16,128]{2,1,0:T(8,128)(2,1)S(1)}, bf16[1,16,128]{2,1,0:T(8,128)(2,1)}, u32[]{:S(2)}) copy-start(bf16[1,16,128]{2,1,0:T(8,128)(2,1)} %l_ref.1) | copy-start | bytes 12292
  41.0 23.8 %all-to-all-start.1 = ((bf16[32,24,128]{2,1,0:T(8,128)(2,1)}), bf16[32,24,128]{2,1,0:T(8,128)(2,1)S(1)}, u32[]{:S(2)}, u32[]{:S(2)}) async-start(bf16[32,24,128]{2,1,0:T(8,128)(2,1)} %far_grads.1), calls=%async_computation.1 | async-start | bytes 393216 | tf_op jit(solution)/shard_map/all_to_all | solution.py:349
  47.9 2.0 %copy-start = (bf16[1,128,2048]{2,1,0:T(8,128)(2,1)S(1)}, bf16[1,128,2048]{2,1,0:T(8,128)(2,1)}, u32[]{:S(2)}) copy-start(bf16[1,128,2048]{2,1,0:T(8,128)(2,1)} %q_ref.3) | copy-start | bytes 1572868
  47.9 1.9 %copy-start.1 = (bf16[1,128,2048]{2,1,0:T(8,128)(2,1)S(1)}, bf16[1,128,2048]{2,1,0:T(8,128)(2,1)}, u32[]{:S(2)}) copy-start(bf16[1,128,2048]{2,1,0:T(8,128)(2,1)} %k_ref.3) | copy-start | bytes 1572868
  48.0 1.9 %copy-start.5 = (s32[1,16]{1,0:T(1,128)S(1)}, s32[1,16]{1,0:T(1,128)}, u32[]{:S(2)}) copy-start(s32[1,16]{1,0:T(1,128)} %off_ref.1) | copy-start | bytes 196
  48.0 7.6 %collective-permute-start.8 = (bf16[1,64,2048]{2,1,0:T(8,128)(2,1)S(1)}, bf16[1,64,2048]{2,1,0:T(8,128)(2,1)S(1)}, u32[]{:S(2)}, u32[]{:S(2)}) collective-permute-start(bf16[1,64,2048]{2,1,0:T(8,128)(2,1)S(1)} %get-tuple-element.23), channel_id=1, source_target_pairs={{0,192},{1,193},{2,194},{3,195},{4,196},{5,197},{6,198},{7,199},{8... | collective-permute-start | bytes 786440 | tf_op jit(solution)/shard_map/ppermute | solution.py:345
  49.8 11.4 %copy-start.2 = (bf16[1,128,2048]{2,1,0:T(8,128)(2,1)S(1)}, bf16[1,128,2048]{2,1,0:T(8,128)(2,1)}, u32[]{:S(2)}) copy-start(bf16[1,128,2048]{2,1,0:T(8,128)(2,1)} %v_ref.1) | copy-start | bytes 1572868
  49.8 11.4 %copy-start.4 = (bf16[1,16,128]{2,1,0:T(8,128)(2,1)S(1)}, bf16[1,16,128]{2,1,0:T(8,128)(2,1)}, u32[]{:S(2)}) copy-start(bf16[1,16,128]{2,1,0:T(8,128)(2,1)} %d_ref.1) | copy-start | bytes 12292
  49.8 11.4 %collective-permute-start.7 = (bf16[1,64,2048]{2,1,0:T(8,128)(2,1)S(1)}, bf16[1,64,2048]{2,1,0:T(8,128)(2,1)S(1)}, u32[]{:S(2)}, u32[]{:S(2)}) collective-permute-start(bf16[1,64,2048]{2,1,0:T(8,128)(2,1)S(1)} %get-tuple-element.24), channel_id=1, source_target_pairs={{0,192},{1,193},{2,194},{3,195},{4,196},{5,197},{6,198},{7,199},{8... | collective-permute-start | bytes 786440 | tf_op jit(solution)/shard_map/ppermute | solution.py:345

commit v9 on v8

--- a/solution.py
+++ b/solution.py
@@ -119,73 +119,59 @@
     )(pos, offsets, lse, delta, query, key, value, grad).reshape(GROUP, ROWS, HD)
 
 
-def score_kernel(off_ref, q_ref, k_ref, l_ref, p_ref, offs_ref, st_ref):
+def offsets_kernel(off_ref, o_ref):
+    for h in range(HEADS):
+        o_ref[h:h + 1, :] = jnp.full((1, TOK), off_ref[0, h], jnp.int32)
+
+
+def spread_offsets(offsets):
+    return pl.pallas_call(
+        offsets_kernel,
+        in_specs=[SM],
+        out_specs=VM,
+        out_shape=jax.ShapeDtypeStruct((HEADS, TOK), jnp.int32),
+        compiler_params=small(),
+        name="spread_offsets",
+    )(offsets)
+
+
+def local_kernel(q_ref, k_ref, v_ref, g_ref, l_ref, d_ref, dq_ref, dk_ref, dv_ref, st_ref):
     step = pl.program_id(0)
 
     @pl.when(step == 0)
     def _():
-        st_ref[...] = l_ref[0].astype(F32)
-        for h in range(HEADS):
-            offs_ref[h:h + 1, :] = jnp.full((1, TOK), off_ref[0, h], jnp.int32)
-
-    lses = st_ref[pl.ds(pl.multiple_of(step * 4, 4), 4), :]
+        st_ref[0] = l_ref[0].astype(F32)
+        st_ref[1] = d_ref[0].astype(F32)
+
+    base = pl.multiple_of(step * 4, 4)
+    lses = st_ref[0, pl.ds(base, 4), :]
+    dlts = st_ref[1, pl.ds(base, 4), :]
     for i in range(4):
         cols = slice(i * HD, (i + 1) * HD)
-        p_ref[i] = jnp.exp(dot_t(k_ref[0, :, cols], q_ref[0, :, cols]) * SCALE - lses[i:i + 1])
-
-
-def local_scores(offsets, query, key, lse):
-    wide = pl.BlockSpec((1, TOK, 4 * HD), lambda i: (0, 0, i))
-    stat = pl.BlockSpec((1, HEADS, TOK), lambda i: (0, 0, 0))
-    return pl.pallas_call(
-        score_kernel,
-        grid=(4,),
-        in_specs=[SM, wide, wide, stat],
-        out_specs=[pl.BlockSpec((4, TOK, TOK), lambda i: (i, 0, 0)), pl.BlockSpec((HEADS, TOK), lambda i: (0, 0))],
-        out_shape=[jax.ShapeDtypeStruct((HEADS, TOK, TOK), F32), jax.ShapeDtypeStruct((HEADS, TOK), jnp.int32)],
-        scratch_shapes=[pltpu.VMEM((HEADS, TOK), F32)],
-        compiler_params=small(),
-        cost_estimate=pl.CostEstimate(flops=16 * 2 * 128 ** 3 * 4, bytes_accessed=2097152, transcendentals=262144),
-        name="local_scores",
-    )(offsets, query, key, lse)
-
-
-def local_kernel(p_ref, q_ref, k_ref, v_ref, g0_ref, g1_ref, d_ref, dq_ref, dk_ref, dv_ref, st_ref):
-    step = pl.program_id(0)
-
-    @pl.when(step == 0)
-    def _():
-        st_ref[...] = d_ref[0].astype(F32)
-
-    dlts = st_ref[pl.ds(pl.multiple_of(step * 4, 4), 4), :]
-    for i in range(4):
-        cols = slice(i * HD, (i + 1) * HD)
-        q, k, v = q_ref[0, :, cols], k_ref[0, :, cols], v_ref[0, :, cols]
-        g = jnp.concatenate([g0_ref[0, :, cols], g1_ref[0, :, cols]], axis=0)
-        p = p_ref[i]
+        q, k, v, g = q_ref[0, :, cols], k_ref[0, :, cols], v_ref[0, :, cols], g_ref[0, :, cols]
+        p = jnp.exp(dot_t(k, q) * SCALE - lses[i:i + 1])
         ds = (p * (dot_t(v, g) - dlts[i:i + 1])).astype(BF)
         dv_ref[:, cols] = dot(p.astype(BF), g).astype(BF)
         dk_ref[:, cols] = (dot(ds, q) * SCALE).astype(BF)
         dq_ref[:, cols] = (dot_l(ds, k) * SCALE).astype(BF)
 
 
-def local_grads(probs, query, key, value, grad0, grad1, delta):
+def local_grads(query, key, value, grad, lse, delta):
     wide = pl.BlockSpec((1, TOK, 4 * HD), lambda i: (0, 0, i))
-    half = pl.BlockSpec((1, TOK // 2, 4 * HD), lambda i: (0, 0, i))
     out = pl.BlockSpec((TOK, 4 * HD), lambda i: (0, i))
     stat = pl.BlockSpec((1, HEADS, TOK), lambda i: (0, 0, 0))
     shape = jax.ShapeDtypeStruct((TOK, HEADS * HD), BF)
     return pl.pallas_call(
         local_kernel,
         grid=(4,),
-        in_specs=[pl.BlockSpec((4, TOK, TOK), lambda i: (i, 0, 0)), wide, wide, wide, half, half, stat],
+        in_specs=[wide, wide, wide, wide, stat, stat],
         out_specs=[out, out, out],
         out_shape=[shape, shape, shape],
-        scratch_shapes=[pltpu.VMEM((HEADS, TOK), F32)],
-        compiler_params=small(),
-        cost_estimate=pl.CostEstimate(flops=16 * 4 * 2 * 128 ** 3 * 4, bytes_accessed=4718592, transcendentals=0),
+        scratch_shapes=[pltpu.VMEM((2, HEADS, TOK), F32)],
+        compiler_params=small(),
+        cost_estimate=pl.CostEstimate(flops=16 * 5 * 2 * 128 ** 3 * 4, bytes_accessed=3670016, transcendentals=262144),
         name="local_grads",
-    )(probs, query, key, value, grad0, grad1, delta)
+    )(query, key, value, grad, lse, delta)
 
 
 def query_side(q, g, k, v, lse, dlt):
@@ -225,9 +211,10 @@
     return jnp.where(core == 0, t[:, 0], t[:, 1]).reshape(HALF, width)
 
 
-def near_kernel(core_ref, a_ref, b_ref, oa_ref, ob_ref, sub_ref, col_ref, dq_ref, dk_ref, dv_ref):
+def near_kernel(core_ref, a_ref, b_ref, oa_ref, hop_ref, ob_ref, sub_ref, col_ref, dq_ref, dk_ref, dv_ref):
     core = core_ref[0]
-    q, k, v, g = whole(core, a_ref[:, 0:16], b_ref[...], oa_ref[:, 0:16], ob_ref[...])
+    mine_b = jnp.where(core == 0, b_ref[...], hop_ref[...])
+    q, k, v, g = whole(core, a_ref[:, 0:16], mine_b, oa_ref[:, 0:16], ob_ref[...])
     stats = stats_of(core, a_ref, oa_ref)
     turned = jnp.transpose(jnp.concatenate([stats, jnp.zeros((HD - 8, HD), F32)], axis=0))
     lse = share(core, jnp.concatenate([turned[:, i:i + 1] for i in range(4)], axis=0))
@@ -245,7 +232,7 @@
     part = jax.ShapeDtypeStruct((HALF, HD), F32)
     return pl.pallas_call(
         near_kernel,
-        in_specs=[SM] + [VM] * 4,
+        in_specs=[SM] + [VM] * 5,
         out_specs=[VM] * 5,
         out_shape=[jax.ShapeDtypeStruct((4, HALF, HD), BF)] + [part] * 4,
         compiler_params=small(),
@@ -358,19 +345,18 @@
     pos = (turn * 4 + jnp.where(x < 2, x, NX - 1 - x) * 2 + seat % NC).reshape(1)
     picked = pick_all(pos, offsets, log_sums, deltas, queries, key_rows, value_rows, grad_out)
     mine = swap(picked, IN_ORDER)
-    grad0 = move(grad_out[:, :TOK // 2], lambda s, x, c: (s - 1, x, c))
-    grad1 = move(grad_out[:, TOK // 2:], lambda s, x, c: (s - 1, x, c))
-    probs, offs = local_scores(offsets, queries, key_rows, log_sums)
+    offs = spread_offsets(offsets)
     a, b = mine[:, :MAIN], mine[:, MAIN:]
     far_a = move(a, lambda s, x, c: (s, 3 - x, c))
     far_b = move(b, lambda s, x, c: (s - c, 3 - x, c))
+    hop = move(b, lambda s, x, c: (s - 1, x, 1) if c == 1 else None)
+    other_b = move(b, lambda s, x, c: (s - c, x, 1 - c))
     other_a = move(a, lambda s, x, c: (s, x, 1 - c))
-    own_b = move(b, lambda s, x, c: (s - c, x, c))
-    other_b = move(own_b, lambda s, x, c: (s, x, 1 - c))
+    grad = move(grad_out, lambda s, x, c: (s - 1, x, c))
     other_far_a = move(far_a, lambda s, x, c: (s, x, 1 - c))
     other_far_b = move(far_b, lambda s, x, c: (s, x, 1 - c))
-    local = local_grads(probs, queries, key_rows, value_rows, grad0, grad1, deltas)
-    part = near_grads(core, a, own_b, other_a, other_b)
+    local = local_grads(queries, key_rows, value_rows, grad, log_sums, deltas)
+    part = near_grads(core, a, b, other_a, hop, other_b)
     back = swap(far_grads(core, far_a, far_b, other_far_a, other_far_b, *part), OUT_ORDER)
     return tuple(combine(back, (*local, offs)))
 

time: 66.7 us -> 65.3 us (0.979)
  waiting for transfers between devices: 14.4 us -> 8.9 us
  starting transfers between devices: 17.3 us -> 19.7 us
  local copies, waits for them, and re-layouts: 0.1 us -> 1.9 us
    ppermute x9 -> x8, waiting for transfers between devices: 14.4 us -> 8.5 us  [move(): return lax.ppermute(value, ('section', 'seq'), pairs)]
    ppermute x9 -> x8, starting transfers between devices: 10.4 us -> 12.7 us  [move(): return lax.ppermute(value, ('section', 'seq'), pairs)]
    unnamed x14 -> x18, local copies, waits for them, and re-layouts: 0.03 us -> 1.87 us
  transfers between devices with their start and end apart: 10 -> 9, of which waited for: 5 -> 3; matrix products, arithmetic and copies ran while one was open for 0% -> 0% of each run, Pallas kernels for 9% -> 11%
where the time goes in v9:
time: 65.3 us; the launch traced here: 65 us
  blocking collectives  21.7 us (33%)
  starting transfers between devices  19.7 us (30%)
  Pallas kernels  11.8 us (18%)
  waiting for transfers between devices  8.9 us (14%)
  local copies, waits for them, and re-layouts  1.9 us (3%)
  between operations  0.89 us (1%)
    all_to_all x1, blocking collectives, swap(): lax.all_to_all(value, 'seq', 0, 0, axis_index_groups=groups_of(order), ti...  21.7 us
    ppermute x8, starting transfers between devices, move(): return lax.ppermute(value, ('section', 'seq'), pairs)  12.7 us
    ppermute x8, waiting for transfers between devices, move(): return lax.ppermute(value, ('section', 'seq'), pairs)  8.5 us
    all_to_all x1, starting transfers between devices, swap(): lax.all_to_all(value, 'seq', 0, 0, axis_index_groups=groups_of(order), ti...  6.99 us
    pallas_call x1, Pallas kernels, local_grads(): pl.pallas_call(local_kernel, grid=(4,), in_specs=[wide, wide, wide, wide,...  4.38 us
    pallas_call x1, Pallas kernels, pick_all(): pl.pallas_call(pick_kernel, in_specs=[SM] + [raw] * 7, out_specs=raw, out...  2.84 us
    unnamed x18, local copies, waits for them, and re-layouts  1.87 us
    pallas_call x1, Pallas kernels, combine(): pl.pallas_call(combine_kernel, in_specs=[VM] * 5, out_specs=[pl.BlockSpec...  1.54 us
  transfers between devices with their start and end apart: 9, of which 3 were waited for; matrix products, arithmetic and copies ran while one was open for 0% of the time, Pallas kernels for 11%

profile of v9, /device:TPU:1, one launch (start us, length us, event | category | flops | bytes accessed | tf_op | source)
XLA Modules:
  0.0 65.0 jit_solution(4716768112527333057)
XLA Ops:
  0.7 2.8 %pick_all.1 = bf16[16,2,40,128]{3,2,1,0:T(8,128)(2,1)} custom-call(s32[1]{0:T(128)} %bitcast.1.pos_ref, s32[1,16]{1,0:T(1,128)} %off_ref.1, bf16[1,16,128]{2,1,0:T(8,128)(2,1)} %l_ref.1, bf16[1,16,128]{2,1,0:T(8,128)(2,1)} %d_ref.1, bf16[1,128,2048]{2,1,0:T(8,128)(2,1)} %q_ref.1, bf16[1,128,2048]{2,1,0:T(8,128)(2,1)} %k_ref.1, bf16[1,128,2048]{2,1,0:T(8,128)(2,1)} %v_ref.1, ...), custom_call_target="tpu_custom_call" | custom-call | tf_op jit(solution)/shard_map/pick_all/pallas_call | solution.py:104
  3.6 0.0 copy-start.8
  3.6 21.7 %all_to_all.10 = bf16[32,40,128]{2,1,0:T(8,128)(2,1)S(1)} all-to-all(bf16[32,40,128]{2,1,0:T(8,128)(2,1)} %bitcast.3), channel_id=1, replica_groups={{40,41,42,43,32,33,34,35,24,25,26,27,16,17,18,19,8,9,10,11,0,1,2,3,56,5..., dimensions={0} | all-to-all | bytes 655360 | tf_op jit(solution)/shard_map/all_to_all | solution.py:336
  25.3 2.3 %collective-permute-start = (bf16[32,24,128]{2,1,0:T(8,128)(2,1)S(1)}, bf16[32,24,128]{2,1,0:T(8,128)(2,1)S(1)}, u32[]{:S(2)}, u32[]{:S(2)}) collective-permute-start(bf16[32,24,128]{2,1,0:T(8,128)(2,1)S(1)} %slice.8.a_ref), channel_id=1, source_target_pairs={{0,6},{1,7},{2,4},{3,5},{4,2},{5,3},{6,0},{7,1},{8,14},{9,15},{10,... | collective-permute-start | bytes 589832 | tf_op jit(solution)/shard_map/ppermute | solution.py:332
  27.7 3.0 %collective-permute-start.6 = (bf16[32,16,128]{2,1,0:T(8,128)(2,1)S(1)}, bf16[32,16,128]{2,1,0:T(8,128)(2,1)S(1)}, u32[]{:S(2)}, u32[]{:S(2)}) collective-permute-start(bf16[32,16,128]{2,1,0:T(8,128)(2,1)S(1)} %slice.9.b_ref), channel_id=1, source_target_pairs={{0,1},{1,192},{2,3},{3,194},{4,5},{5,196},{6,7},{7,198},{8,9},{9,2... | collective-permute-start | bytes 393224 | tf_op jit(solution)/shard_map/ppermute | solution.py:332
  30.6 0.5 collective-permute-start.7
  31.1 0.4 collective-permute-start.1
  31.5 0.5 collective-permute-start.4
  32.0 1.1 %collective-permute-done.a_ref = bf16[32,24,128]{2,1,0:T(8,128)(2,1)S(1)} collective-permute-done((bf16[32,24,128]{2,1,0:T(8,128)(2,1)S(1)}, bf16[32,24,128]{2,1,0:T(8,128)(2,1)S(1)}, u32[]{:S(2)}, u32[]{:S(2)}) %collective-permute-start) | collective-permute-done | bytes 196640 | tf_op jit(solution)/shard_map/ppermute | solution.py:332
  33.0 0.9 %collective-permute-start.2 = (bf16[32,24,128]{2,1,0:T(8,128)(2,1)S(1)}, bf16[32,24,128]{2,1,0:T(8,128)(2,1)S(1)}, u32[]{:S(2)}, u32[]{:S(2)}) collective-permute-start(bf16[32,24,128]{2,1,0:T(8,128)(2,1)S(1)} %collective-permute-done.a_ref), channel_id=1, source_target_pairs={{0,1},{1,0},{2,3},{3,2},{4,5},{5,4},{6,7},{7,6},{8,9},{9,8},{10,11... | collective-permute-start | bytes 589832 | tf_op jit(solution)/shard_map/ppermute | solution.py:332
  33.9 5.1 %collective-permute-start.5 = (bf16[32,16,128]{2,1,0:T(8,128)(2,1)S(1)}, bf16[32,16,128]{2,1,0:T(8,128)(2,1)S(1)}, u32[]{:S(2)}, u32[]{:S(2)}) collective-permute-start(bf16[32,16,128]{2,1,0:T(8,128)(2,1)S(1)} %slice.9.b_ref), channel_id=1, source_target_pairs={{1,193},{3,195},{5,197},{7,199},{9,201},{11,203},{13,205},{15,207}... | collective-permute-start | bytes 393224 | tf_op jit(solution)/shard_map/ppermute | solution.py:332
  39.1 0.1 collective-permute-start.3
  39.2 7.4 %collective-permute-done.5.hop_ref = bf16[32,16,128]{2,1,0:T(8,128)(2,1)S(1)} collective-permute-done((bf16[32,16,128]{2,1,0:T(8,128)(2,1)S(1)}, bf16[32,16,128]{2,1,0:T(8,128)(2,1)S(1)}, u32[]{:S(2)}, u32[]{:S(2)}) %collective-permute-start.5) | collective-permute-done | bytes 131104 | tf_op jit(solution)/shard_map/ppermute | solution.py:332
  46.6 1.0 %near_grads.1 = (bf16[4,256,128]{2,1,0:T(8,128)(2,1)S(1)}, f32[256,128]{1,0:T(8,128)S(1)}, f32[256,128]{1,0:T(8,128)S(1)}, f32[256,128]{1,0:T(8,128)S(1)}, f32[256,128]{1,0:T(8,128)S(1)}) custom-call(s32[1]{0:T(128)} %bitcast.core_ref, bf16[32,24,128]{2,1,0:T(8,128)(2,1)S(1)} %slice.8.a_ref, bf16[32,16,128]{2,1,0:T(8,128)(2,1)S(1)} %slice.9.b_ref, ...), custom_call_target="tpu_custom_call" | custom-call | flops 469762048 | bytes 1572864 | tf_op jit(solution)/shard_map/near_grads/pallas_call | solution.py:233
  47.7 0.0 copy-start.2
  47.7 1.5 %far_grads.1 = bf16[32,24,128]{2,1,0:T(8,128)(2,1)} custom-call(s32[1]{0:T(128)} %bitcast.core_ref, bf16[32,24,128]{2,1,0:T(8,128)(2,1)S(1)} %collective-permute-done.a_ref, bf16[32,16,128]{2,1,0:T(8,128)(2,1)S(1)} %collective-permute-done.1.b_ref, bf16[32,24,128]{2,1,0:T(8,128)(2,1)S(1)} %collective-permute-done.2.oa_ref, ...), custom_call_target="tpu_custom_call" | custom-call | tf_op jit(solution)/shard_map/far_grads/pallas_call | solution.py:260
  49.2 7.0 %all-to-all-start.1 = ((bf16[32,24,128]{2,1,0:T(8,128)(2,1)}), bf16[32,24,128]{2,1,0:T(8,128)(2,1)S(1)}, u32[]{:S(2)}, u32[]{:S(2)}) async-start(bf16[32,24,128]{2,1,0:T(8,128)(2,1)} %far_grads.1), calls=%async_computation.1 | async-start | bytes 393216 | tf_op jit(solution)/shard_map/all_to_all | solution.py:336
  56.2 0.0 copy-start.4
  56.2 0.5 spread_offsets.1.off_ref
  56.8 0.8 %copy-done.6 = bf16[1,128,2048]{2,1,0:T(8,128)(2,1)} copy-done((bf16[1,128,2048]{2,1,0:T(8,128)(2,1)}, bf16[1,128,2048]{2,1,0:T(8,128)(2,1)S(1)}, u32[]{:S(2)}) %copy-start.6) | copy-done | bytes 524312
  57.6 1.0 %copy-done.7 = bf16[1,128,2048]{2,1,0:T(8,128)(2,1)S(1)} copy-done((bf16[1,128,2048]{2,1,0:T(8,128)(2,1)S(1)}, bf16[1,128,2048]{2,1,0:T(8,128)(2,1)}, u32[]{:S(2)}) %copy-start.7) | copy-done | bytes 524312
  58.7 4.4 %local_grads.1 = (bf16[128,2048]{1,0:T(8,128)(2,1)S(1)}, bf16[128,2048]{1,0:T(8,128)(2,1)S(1)}, bf16[128,2048]{1,0:T(8,128)(2,1)S(1)}) custom-call(bf16[1,128,2048]{2,1,0:T(8,128)(2,1)S(1)} %copy-done, bf16[1,128,2048]{2,1,0:T(8,128)(2,1)S(1)} %copy-done.1, bf16[1,128,2048]{2,1,0:T(8,128)(2,1)S(1)} %copy-done.2, bf16[1,128,2048]{2,1,0:T(8,128)(2,1)S(1)} %copy-done.7, ...), custom_call_target="tpu_custom_call" | custom-call | flops 1342177280 | bytes 3670016 | tf_op jit(solution)/shard_map/local_grads/pallas_call | solution.py:164
  63.0 0.4 all-to-all-done.1.w_ref
  63.4 1.5 %combine.1 = (bf16[1,128,2048]{2,1,0:T(8,128)(2,1)}, bf16[1,128,2048]{2,1,0:T(8,128)(2,1)}, bf16[1,128,2048]{2,1,0:T(8,128)(2,1)}) custom-call(bf16[32,24,128]{2,1,0:T(8,128)(2,1)S(1)} %all-to-all-done.1.w_ref, bf16[128,2048]{1,0:T(8,128)(2,1)S(1)} %get-tuple-element.16.dq_ref, bf16[128,2048]{1,0:T(8,128)(2,1)S(1)} %get-tuple-element.17.dk_ref, ...), custom_call_target="tpu_custom_call" | custom-call | tf_op jit(solution)/shard_map/combine/pallas_call | solution.py:294
  (21 shorter events, 0.1 us)
Async XLA Ops:
  3.6 27.1 %copy-start.8 = (bf16[1,128,2048]{2,1,0:T(8,128)(2,1)S(1)}, bf16[1,128,2048]{2,1,0:T(8,128)(2,1)}, u32[]{:S(2)}) copy-start(bf16[1,128,2048]{2,1,0:T(8,128)(2,1)} %g_hbm.1) | copy-start | bytes 1572868
  25.3 7.7 %collective-permute-start = (bf16[32,24,128]{2,1,0:T(8,128)(2,1)S(1)}, bf16[32,24,128]{2,1,0:T(8,128)(2,1)S(1)}, u32[]{:S(2)}, u32[]{:S(2)}) collective-permute-start(bf16[32,24,128]{2,1,0:T(8,128)(2,1)S(1)} %slice.8.a_ref), channel_id=1, source_target_pairs={{0,6},{1,7},{2,4},{3,5},{4,2},{5,3},{6,0},{7,1},{8,14},{9,15},{10,... | collective-permute-start | bytes 589832 | tf_op jit(solution)/shard_map/ppermute | solution.py:332
  27.7 6.3 %collective-permute-start.6 = (bf16[32,16,128]{2,1,0:T(8,128)(2,1)S(1)}, bf16[32,16,128]{2,1,0:T(8,128)(2,1)S(1)}, u32[]{:S(2)}, u32[]{:S(2)}) collective-permute-start(bf16[32,16,128]{2,1,0:T(8,128)(2,1)S(1)} %slice.9.b_ref), channel_id=1, source_target_pairs={{0,1},{1,192},{2,3},{3,194},{4,5},{5,196},{6,7},{7,198},{8,9},{9,2... | collective-permute-start | bytes 393224 | tf_op jit(solution)/shard_map/ppermute | solution.py:332
  30.6 26.1 %collective-permute-start.7 = (bf16[1,128,2048]{2,1,0:T(8,128)(2,1)S(1)}, bf16[1,128,2048]{2,1,0:T(8,128)(2,1)S(1)}, u32[]{:S(2)}, u32[]{:S(2)}) collective-permute-start(bf16[1,128,2048]{2,1,0:T(8,128)(2,1)S(1)} %copy-done.8), channel_id=1, source_target_pairs={{0,192},{1,193},{2,194},{3,195},{4,196},{5,197},{6,198},{7,199},{8... | collective-permute-start | bytes 1572872 | tf_op jit(solution)/shard_map/ppermute | solution.py:332
  31.1 8.0 %collective-permute-start.1 = (bf16[32,16,128]{2,1,0:T(8,128)(2,1)S(1)}, bf16[32,16,128]{2,1,0:T(8,128)(2,1)S(1)}, u32[]{:S(2)}, u32[]{:S(2)}) collective-permute-start(bf16[32,16,128]{2,1,0:T(8,128)(2,1)S(1)} %slice.9.b_ref), channel_id=1, source_target_pairs={{0,6},{1,199},{2,4},{3,197},{4,2},{5,195},{6,0},{7,193},{8,14},{9,... | collective-permute-start | bytes 393224 | tf_op jit(solution)/shard_map/ppermute | solution.py:332
  31.5 15.1 %collective-permute-start.4 = (bf16[32,24,128]{2,1,0:T(8,128)(2,1)S(1)}, bf16[32,24,128]{2,1,0:T(8,128)(2,1)S(1)}, u32[]{:S(2)}, u32[]{:S(2)}) collective-permute-start(bf16[32,24,128]{2,1,0:T(8,128)(2,1)S(1)} %slice.8.a_ref), channel_id=1, source_target_pairs={{0,1},{1,0},{2,3},{3,2},{4,5},{5,4},{6,7},{7,6},{8,9},{9,8},{10,11... | collective-permute-start | bytes 589832 | tf_op jit(solution)/shard_map/ppermute | solution.py:332
  33.0 14.6 %collective-permute-start.2 = (bf16[32,24,128]{2,1,0:T(8,128)(2,1)S(1)}, bf16[32,24,128]{2,1,0:T(8,128)(2,1)S(1)}, u32[]{:S(2)}, u32[]{:S(2)}) collective-permute-start(bf16[32,24,128]{2,1,0:T(8,128)(2,1)S(1)} %collective-permute-done.a_ref), channel_id=1, source_target_pairs={{0,1},{1,0},{2,3},{3,2},{4,5},{5,4},{6,7},{7,6},{8,9},{9,8},{10,11... | collective-permute-start | bytes 589832 | tf_op jit(solution)/shard_map/ppermute | solution.py:332
  33.9 12.7 %collective-permute-start.5 = (bf16[32,16,128]{2,1,0:T(8,128)(2,1)S(1)}, bf16[32,16,128]{2,1,0:T(8,128)(2,1)S(1)}, u32[]{:S(2)}, u32[]{:S(2)}) collective-permute-start(bf16[32,16,128]{2,1,0:T(8,128)(2,1)S(1)} %slice.9.b_ref), channel_id=1, source_target_pairs={{1,193},{3,195},{5,197},{7,199},{9,201},{11,203},{13,205},{15,207}... | collective-permute-start | bytes 393224 | tf_op jit(solution)/shard_map/ppermute | solution.py:332
  39.1 8.5 %collective-permute-start.3 = (bf16[32,16,128]{2,1,0:T(8,128)(2,1)S(1)}, bf16[32,16,128]{2,1,0:T(8,128)(2,1)S(1)}, u32[]{:S(2)}, u32[]{:S(2)}) collective-permute-start(bf16[32,16,128]{2,1,0:T(8,128)(2,1)S(1)} %collective-permute-done.1.b_ref), channel_id=1, source_target_pairs={{0,1},{1,0},{2,3},{3,2},{4,5},{5,4},{6,7},{7,6},{8,9},{9,8},{10,11... | collective-permute-start | bytes 393224 | tf_op jit(solution)/shard_map/ppermute | solution.py:332
  47.6 10.0 %copy-start = (bf16[1,128,2048]{2,1,0:T(8,128)(2,1)S(1)}, bf16[1,128,2048]{2,1,0:T(8,128)(2,1)}, u32[]{:S(2)}) copy-start(bf16[1,128,2048]{2,1,0:T(8,128)(2,1)} %q_ref.1) | copy-start | bytes 1572868
  47.6 9.9 %copy-start.1 = (bf16[1,128,2048]{2,1,0:T(8,128)(2,1)S(1)}, bf16[1,128,2048]{2,1,0:T(8,128)(2,1)}, u32[]{:S(2)}) copy-start(bf16[1,128,2048]{2,1,0:T(8,128)(2,1)} %k_ref.1) | copy-start | bytes 1572868
  47.7 9.9 %copy-start.2 = (bf16[1,128,2048]{2,1,0:T(8,128)(2,1)S(1)}, bf16[1,128,2048]{2,1,0:T(8,128)(2,1)}, u32[]{:S(2)}) copy-start(bf16[1,128,2048]{2,1,0:T(8,128)(2,1)} %v_ref.1) | copy-start | bytes 1572868
  49.2 7.0 %copy-start.5 = (s32[1,16]{1,0:T(1,128)S(1)}, s32[1,16]{1,0:T(1,128)}, u32[]{:S(2)}) copy-start(s32[1,16]{1,0:T(1,128)} %off_ref.1) | copy-start | bytes 196
  49.2 14.3 %all-to-all-start.1 = ((bf16[32,24,128]{2,1,0:T(8,128)(2,1)}), bf16[32,24,128]{2,1,0:T(8,128)(2,1)S(1)}, u32[]{:S(2)}, u32[]{:S(2)}) async-start(bf16[32,24,128]{2,1,0:T(8,128)(2,1)} %far_grads.1), calls=%async_computation.1 | async-start | bytes 393216 | tf_op jit(solution)/shard_map/all_to_all | solution.py:336
  56.2 1.4 %copy-start.3 = (bf16[1,16,128]{2,1,0:T(8,128)(2,1)S(1)}, bf16[1,16,128]{2,1,0:T(8,128)(2,1)}, u32[]{:S(2)}) copy-start(bf16[1,16,128]{2,1,0:T(8,128)(2,1)} %l_ref.1) | copy-start | bytes 12292
  56.2 1.4 %copy-start.4 = (bf16[1,16,128]{2,1,0:T(8,128)(2,1)S(1)}, bf16[1,16,128]{2,1,0:T(8,128)(2,1)}, u32[]{:S(2)}) copy-start(bf16[1,16,128]{2,1,0:T(8,128)(2,1)} %d_ref.1) | copy-start | bytes 12292
  56.8 0.8 %copy-start.6 = (bf16[1,128,2048]{2,1,0:T(8,128)(2,1)}, bf16[1,128,2048]{2,1,0:T(8,128)(2,1)S(1)}, u32[]{:S(2)}) copy-start(bf16[1,128,2048]{2,1,0:T(8,128)(2,1)S(1)} %collective-permute-done.7.g_ref) | copy-start | bytes 1572868
  57.6 1.0 %copy-start.7 = (bf16[1,128,2048]{2,1,0:T(8,128)(2,1)S(1)}, bf16[1,128,2048]{2,1,0:T(8,128)(2,1)}, u32[]{:S(2)}) copy-start(bf16[1,128,2048]{2,1,0:T(8,128)(2,1)} %copy-done.6) | copy-start | bytes 1572868

commit v10 on v9

--- a/solution.py
+++ b/solution.py
@@ -211,10 +211,9 @@
     return jnp.where(core == 0, t[:, 0], t[:, 1]).reshape(HALF, width)
 
 
-def near_kernel(core_ref, a_ref, b_ref, oa_ref, hop_ref, ob_ref, sub_ref, col_ref, dq_ref, dk_ref, dv_ref):
+def near_kernel(core_ref, a_ref, b_ref, oa_ref, ob_ref, sub_ref, col_ref, dq_ref, dk_ref, dv_ref):
     core = core_ref[0]
-    mine_b = jnp.where(core == 0, b_ref[...], hop_ref[...])
-    q, k, v, g = whole(core, a_ref[:, 0:16], mine_b, oa_ref[:, 0:16], ob_ref[...])
+    q, k, v, g = whole(core, a_ref[:, 0:16], b_ref[...], oa_ref[:, 0:16], ob_ref[...])
     stats = stats_of(core, a_ref, oa_ref)
     turned = jnp.transpose(jnp.concatenate([stats, jnp.zeros((HD - 8, HD), F32)], axis=0))
     lse = share(core, jnp.concatenate([turned[:, i:i + 1] for i in range(4)], axis=0))
@@ -232,7 +231,7 @@
     part = jax.ShapeDtypeStruct((HALF, HD), F32)
     return pl.pallas_call(
         near_kernel,
-        in_specs=[SM] + [VM] * 5,
+        in_specs=[SM] + [VM] * 4,
         out_specs=[VM] * 5,
         out_shape=[jax.ShapeDtypeStruct((4, HALF, HD), BF)] + [part] * 4,
         compiler_params=small(),
@@ -349,14 +348,14 @@
     a, b = mine[:, :MAIN], mine[:, MAIN:]
     far_a = move(a, lambda s, x, c: (s, 3 - x, c))
     far_b = move(b, lambda s, x, c: (s - c, 3 - x, c))
-    hop = move(b, lambda s, x, c: (s - 1, x, 1) if c == 1 else None)
-    other_b = move(b, lambda s, x, c: (s - c, x, 1 - c))
+    own_b = move(b, lambda s, x, c: (s - c, x, c))
+    other_b = move(own_b, lambda s, x, c: (s, x, 1 - c))
     other_a = move(a, lambda s, x, c: (s, x, 1 - c))
     grad = move(grad_out, lambda s, x, c: (s - 1, x, c))
     other_far_a = move(far_a, lambda s, x, c: (s, x, 1 - c))
     other_far_b = move(far_b, lambda s, x, c: (s, x, 1 - c))
     local = local_grads(queries, key_rows, value_rows, grad, log_sums, deltas)
-    part = near_grads(core, a, b, other_a, hop, other_b)
+    part = near_grads(core, a, own_b, other_a, other_b)
     back = swap(far_grads(core, far_a, far_b, other_far_a, other_far_b, *part), OUT_ORDER)
     return tuple(combine(back, (*local, offs)))
 

time: 65.3 us -> 58.5 us (0.90)
  starting transfers between devices: 19.7 us -> 16.2 us
  waiting for transfers between devices: 8.9 us -> 5.67 us
    ppermute x8, starting transfers between devices: 12.7 us -> 8.58 us  [move(): return lax.ppermute(value, ('section', 'seq'), pairs)]
    ppermute x8, waiting for transfers between devices: 8.5 us -> 5.3 us  [move(): return lax.ppermute(value, ('section', 'seq'), pairs)]
  transfers between devices with their start and end apart: 9 -> 9, of which waited for: 3 -> 4; matrix products, arithmetic and copies ran while one was open for 0% -> 0% of each run, Pallas kernels for 11% -> 13%
where the time goes in v10:
time: 58.5 us; the launch traced here: 58.2 us
  blocking collectives  21.7 us (37%)
  starting transfers between devices  16.2 us (28%)
  Pallas kernels  11.8 us (20%)
  waiting for transfers between devices  5.67 us (10%)
  local copies, waits for them, and re-layouts  1.89 us (3%)
  between operations  0.85 us (1%)
    all_to_all x1, blocking collectives, swap(): lax.all_to_all(value, 'seq', 0, 0, axis_index_groups=groups_of(order), ti...  21.7 us
    ppermute x8, starting transfers between devices, move(): return lax.ppermute(value, ('section', 'seq'), pairs)  8.58 us
    all_to_all x1, starting transfers between devices, swap(): lax.all_to_all(value, 'seq', 0, 0, axis_index_groups=groups_of(order), ti...  7.63 us
    ppermute x8, waiting for transfers between devices, move(): return lax.ppermute(value, ('section', 'seq'), pairs)  5.3 us
    pallas_call x1, Pallas kernels, local_grads(): pl.pallas_call(local_kernel, grid=(4,), in_specs=[wide, wide, wide, wide,...  4.38 us
    pallas_call x1, Pallas kernels, pick_all(): pl.pallas_call(pick_kernel, in_specs=[SM] + [raw] * 7, out_specs=raw, out...  2.84 us
    unnamed x18, local copies, waits for them, and re-layouts  1.86 us
    pallas_call x1, Pallas kernels, combine(): pl.pallas_call(combine_kernel, in_specs=[VM] * 5, out_specs=[pl.BlockSpec...  1.54 us
  transfers between devices with their start and end apart: 9, of which 4 were waited for; matrix products, arithmetic and copies ran while one was open for 0% of the time, Pallas kernels for 13%

profile of v10, /device:TPU:1, one launch (start us, length us, event | category | flops | bytes accessed | tf_op | source)
XLA Modules:
  0.0 58.2 jit_solution(12551193842675554863)
XLA Ops:
  0.7 2.8 %pick_all.1 = bf16[16,2,40,128]{3,2,1,0:T(8,128)(2,1)} custom-call(s32[1]{0:T(128)} %bitcast.1.pos_ref, s32[1,16]{1,0:T(1,128)} %off_ref.1, bf16[1,16,128]{2,1,0:T(8,128)(2,1)} %l_ref.1, bf16[1,16,128]{2,1,0:T(8,128)(2,1)} %d_ref.1, bf16[1,128,2048]{2,1,0:T(8,128)(2,1)} %q_ref.1, bf16[1,128,2048]{2,1,0:T(8,128)(2,1)} %k_ref.1, bf16[1,128,2048]{2,1,0:T(8,128)(2,1)} %v_ref.1, ...), custom_call_target="tpu_custom_call" | custom-call | tf_op jit(solution)/shard_map/pick_all/pallas_call | solution.py:104
  3.6 0.0 copy-start.8
  3.6 21.7 %all_to_all.10 = bf16[32,40,128]{2,1,0:T(8,128)(2,1)S(1)} all-to-all(bf16[32,40,128]{2,1,0:T(8,128)(2,1)} %bitcast.3), channel_id=1, replica_groups={{40,41,42,43,32,33,34,35,24,25,26,27,16,17,18,19,8,9,10,11,0,1,2,3,56,5..., dimensions={0} | all-to-all | bytes 655360 | tf_op jit(solution)/shard_map/all_to_all | solution.py:335
  25.3 2.3 %collective-permute-start = (bf16[32,24,128]{2,1,0:T(8,128)(2,1)S(1)}, bf16[32,24,128]{2,1,0:T(8,128)(2,1)S(1)}, u32[]{:S(2)}, u32[]{:S(2)}) collective-permute-start(bf16[32,24,128]{2,1,0:T(8,128)(2,1)S(1)} %slice.8.a_ref), channel_id=1, source_target_pairs={{0,6},{1,7},{2,4},{3,5},{4,2},{5,3},{6,0},{7,1},{8,14},{9,15},{10,... | collective-permute-start | bytes 589832 | tf_op jit(solution)/shard_map/ppermute | solution.py:331
  27.7 4.6 %collective-permute-start.4 = (bf16[32,16,128]{2,1,0:T(8,128)(2,1)S(1)}, bf16[32,16,128]{2,1,0:T(8,128)(2,1)S(1)}, u32[]{:S(2)}, u32[]{:S(2)}) collective-permute-start(bf16[32,16,128]{2,1,0:T(8,128)(2,1)S(1)} %slice.9), channel_id=1, source_target_pairs={{0,0},{1,193},{2,2},{3,195},{4,4},{5,197},{6,6},{7,199},{8,8},{9,2... | collective-permute-start | bytes 393224 | tf_op jit(solution)/shard_map/ppermute | solution.py:331
  32.3 0.5 collective-permute-start.7
  32.9 0.3 collective-permute-start.1
  33.2 0.7 %collective-permute-start.2 = (bf16[32,24,128]{2,1,0:T(8,128)(2,1)S(1)}, bf16[32,24,128]{2,1,0:T(8,128)(2,1)S(1)}, u32[]{:S(2)}, u32[]{:S(2)}) collective-permute-start(bf16[32,24,128]{2,1,0:T(8,128)(2,1)S(1)} %collective-permute-done.a_ref), channel_id=1, source_target_pairs={{0,1},{1,0},{2,3},{3,2},{4,5},{5,4},{6,7},{7,6},{8,9},{9,8},{10,11... | collective-permute-start | bytes 589832 | tf_op jit(solution)/shard_map/ppermute | solution.py:331
  33.9 1.7 %collective-permute-done.4.b_ref = bf16[32,16,128]{2,1,0:T(8,128)(2,1)S(1)} collective-permute-done((bf16[32,16,128]{2,1,0:T(8,128)(2,1)S(1)}, bf16[32,16,128]{2,1,0:T(8,128)(2,1)S(1)}, u32[]{:S(2)}, u32[]{:S(2)}) %collective-permute-start.4) | collective-permute-done | bytes 131104 | tf_op jit(solution)/shard_map/ppermute | solution.py:331
  35.6 3.3 %collective-permute-done.1.b_ref = bf16[32,16,128]{2,1,0:T(8,128)(2,1)S(1)} collective-permute-done((bf16[32,16,128]{2,1,0:T(8,128)(2,1)S(1)}, bf16[32,16,128]{2,1,0:T(8,128)(2,1)S(1)}, u32[]{:S(2)}, u32[]{:S(2)}) %collective-permute-start.1) | collective-permute-done | bytes 131104 | tf_op jit(solution)/shard_map/ppermute | solution.py:331
  38.9 1.0 %near_grads.1 = (bf16[4,256,128]{2,1,0:T(8,128)(2,1)S(1)}, f32[256,128]{1,0:T(8,128)S(1)}, f32[256,128]{1,0:T(8,128)S(1)}, f32[256,128]{1,0:T(8,128)S(1)}, f32[256,128]{1,0:T(8,128)S(1)}) custom-call(s32[1]{0:T(128)} %bitcast.core_ref, bf16[32,24,128]{2,1,0:T(8,128)(2,1)S(1)} %slice.8.a_ref, bf16[32,16,128]{2,1,0:T(8,128)(2,1)S(1)} %collective-permute-done.4.b_ref, ...), custom_call_target="tpu_custom_call" | custom-call | flops 469762048 | bytes 1572864 | tf_op jit(solution)/shard_map/near_grads/pallas_call | solution.py:232
  39.9 0.3 collective-permute-done.3.ob_ref
  40.3 1.5 %far_grads.1 = bf16[32,24,128]{2,1,0:T(8,128)(2,1)} custom-call(s32[1]{0:T(128)} %bitcast.core_ref, bf16[32,24,128]{2,1,0:T(8,128)(2,1)S(1)} %collective-permute-done.a_ref, bf16[32,16,128]{2,1,0:T(8,128)(2,1)S(1)} %collective-permute-done.1.b_ref, bf16[32,24,128]{2,1,0:T(8,128)(2,1)S(1)} %collective-permute-done.2.oa_ref, ...), custom_call_target="tpu_custom_call" | custom-call | tf_op jit(solution)/shard_map/far_grads/pallas_call | solution.py:259
  41.8 7.6 %all-to-all-start.1 = ((bf16[32,24,128]{2,1,0:T(8,128)(2,1)}), bf16[32,24,128]{2,1,0:T(8,128)(2,1)S(1)}, u32[]{:S(2)}, u32[]{:S(2)}) async-start(bf16[32,24,128]{2,1,0:T(8,128)(2,1)} %far_grads.1), calls=%async_computation.1 | async-start | bytes 393216 | tf_op jit(solution)/shard_map/all_to_all | solution.py:335
  49.4 0.0 copy-start.3
  49.4 0.0 copy-start.4
  49.5 0.5 spread_offsets.1.off_ref
  50.0 0.0 copy-start.6
  50.0 0.8 %copy-done.6 = bf16[1,128,2048]{2,1,0:T(8,128)(2,1)} copy-done((bf16[1,128,2048]{2,1,0:T(8,128)(2,1)}, bf16[1,128,2048]{2,1,0:T(8,128)(2,1)S(1)}, u32[]{:S(2)}) %copy-start.6) | copy-done | bytes 524312
  50.8 0.0 copy-start.7
  50.9 1.0 %copy-done.7 = bf16[1,128,2048]{2,1,0:T(8,128)(2,1)S(1)} copy-done((bf16[1,128,2048]{2,1,0:T(8,128)(2,1)S(1)}, bf16[1,128,2048]{2,1,0:T(8,128)(2,1)}, u32[]{:S(2)}) %copy-start.7) | copy-done | bytes 524312
  51.9 4.4 %local_grads.1 = (bf16[128,2048]{1,0:T(8,128)(2,1)S(1)}, bf16[128,2048]{1,0:T(8,128)(2,1)S(1)}, bf16[128,2048]{1,0:T(8,128)(2,1)S(1)}) custom-call(bf16[1,128,2048]{2,1,0:T(8,128)(2,1)S(1)} %copy-done, bf16[1,128,2048]{2,1,0:T(8,128)(2,1)S(1)} %copy-done.1, bf16[1,128,2048]{2,1,0:T(8,128)(2,1)S(1)} %copy-done.2, bf16[1,128,2048]{2,1,0:T(8,128)(2,1)S(1)} %copy-done.7, ...), custom_call_target="tpu_custom_call" | custom-call | flops 1342177280 | bytes 3670016 | tf_op jit(solution)/shard_map/local_grads/pallas_call | solution.py:164
  56.3 0.4 all-to-all-done.1.w_ref
  56.6 1.5 %combine.1 = (bf16[1,128,2048]{2,1,0:T(8,128)(2,1)}, bf16[1,128,2048]{2,1,0:T(8,128)(2,1)}, bf16[1,128,2048]{2,1,0:T(8,128)(2,1)}) custom-call(bf16[32,24,128]{2,1,0:T(8,128)(2,1)S(1)} %all-to-all-done.1.w_ref, bf16[128,2048]{1,0:T(8,128)(2,1)S(1)} %get-tuple-element.16.dq_ref, bf16[128,2048]{1,0:T(8,128)(2,1)S(1)} %get-tuple-element.17.dk_ref, ...), custom_call_target="tpu_custom_call" | custom-call | tf_op jit(solution)/shard_map/combine/pallas_call | solution.py:293
  (21 shorter events, 0.1 us)
Async XLA Ops:
  3.6 28.8 %copy-start.8 = (bf16[1,128,2048]{2,1,0:T(8,128)(2,1)S(1)}, bf16[1,128,2048]{2,1,0:T(8,128)(2,1)}, u32[]{:S(2)}) copy-start(bf16[1,128,2048]{2,1,0:T(8,128)(2,1)} %g_hbm.1) | copy-start | bytes 1572868
  25.3 7.9 %collective-permute-start = (bf16[32,24,128]{2,1,0:T(8,128)(2,1)S(1)}, bf16[32,24,128]{2,1,0:T(8,128)(2,1)S(1)}, u32[]{:S(2)}, u32[]{:S(2)}) collective-permute-start(bf16[32,24,128]{2,1,0:T(8,128)(2,1)S(1)} %slice.8.a_ref), channel_id=1, source_target_pairs={{0,6},{1,7},{2,4},{3,5},{4,2},{5,3},{6,0},{7,1},{8,14},{9,15},{10,... | collective-permute-start | bytes 589832 | tf_op jit(solution)/shard_map/ppermute | solution.py:331
  27.7 7.9 %collective-permute-start.4 = (bf16[32,16,128]{2,1,0:T(8,128)(2,1)S(1)}, bf16[32,16,128]{2,1,0:T(8,128)(2,1)S(1)}, u32[]{:S(2)}, u32[]{:S(2)}) collective-permute-start(bf16[32,16,128]{2,1,0:T(8,128)(2,1)S(1)} %slice.9), channel_id=1, source_target_pairs={{0,0},{1,193},{2,2},{3,195},{4,4},{5,197},{6,6},{7,199},{8,8},{9,2... | collective-permute-start | bytes 393224 | tf_op jit(solution)/shard_map/ppermute | solution.py:331
  32.3 17.7 %collective-permute-start.7 = (bf16[1,128,2048]{2,1,0:T(8,128)(2,1)S(1)}, bf16[1,128,2048]{2,1,0:T(8,128)(2,1)S(1)}, u32[]{:S(2)}, u32[]{:S(2)}) collective-permute-start(bf16[1,128,2048]{2,1,0:T(8,128)(2,1)S(1)} %copy-done.8), channel_id=1, source_target_pairs={{0,192},{1,193},{2,194},{3,195},{4,196},{5,197},{6,198},{7,199},{8... | collective-permute-start | bytes 1572872 | tf_op jit(solution)/shard_map/ppermute | solution.py:331
  32.9 6.0 %collective-permute-start.1 = (bf16[32,16,128]{2,1,0:T(8,128)(2,1)S(1)}, bf16[32,16,128]{2,1,0:T(8,128)(2,1)S(1)}, u32[]{:S(2)}, u32[]{:S(2)}) collective-permute-start(bf16[32,16,128]{2,1,0:T(8,128)(2,1)S(1)} %slice.9), channel_id=1, source_target_pairs={{0,6},{1,199},{2,4},{3,197},{4,2},{5,195},{6,0},{7,193},{8,14},{9,... | collective-permute-start | bytes 393224 | tf_op jit(solution)/shard_map/ppermute | solution.py:331
  33.2 5.7 %collective-permute-start.5 = (bf16[32,24,128]{2,1,0:T(8,128)(2,1)S(1)}, bf16[32,24,128]{2,1,0:T(8,128)(2,1)S(1)}, u32[]{:S(2)}, u32[]{:S(2)}) collective-permute-start(bf16[32,24,128]{2,1,0:T(8,128)(2,1)S(1)} %slice.8.a_ref), channel_id=1, source_target_pairs={{0,1},{1,0},{2,3},{3,2},{4,5},{5,4},{6,7},{7,6},{8,9},{9,8},{10,11... | collective-permute-start | bytes 589832 | tf_op jit(solution)/shard_map/ppermute | solution.py:331
  33.2 7.1 %collective-permute-start.2 = (bf16[32,24,128]{2,1,0:T(8,128)(2,1)S(1)}, bf16[32,24,128]{2,1,0:T(8,128)(2,1)S(1)}, u32[]{:S(2)}, u32[]{:S(2)}) collective-permute-start(bf16[32,24,128]{2,1,0:T(8,128)(2,1)S(1)} %collective-permute-done.a_ref), channel_id=1, source_target_pairs={{0,1},{1,0},{2,3},{3,2},{4,5},{5,4},{6,7},{7,6},{8,9},{9,8},{10,11... | collective-permute-start | bytes 589832 | tf_op jit(solution)/shard_map/ppermute | solution.py:331
  35.6 3.3 %collective-permute-start.6 = (bf16[32,16,128]{2,1,0:T(8,128)(2,1)S(1)}, bf16[32,16,128]{2,1,0:T(8,128)(2,1)S(1)}, u32[]{:S(2)}, u32[]{:S(2)}) collective-permute-start(bf16[32,16,128]{2,1,0:T(8,128)(2,1)S(1)} %collective-permute-done.4.b_ref), channel_id=1, source_target_pairs={{0,1},{1,0},{2,3},{3,2},{4,5},{5,4},{6,7},{7,6},{8,9},{9,8},{10,11... | collective-permute-start | bytes 393224 | tf_op jit(solution)/shard_map/ppermute | solution.py:331
  38.9 1.3 %collective-permute-start.3 = (bf16[32,16,128]{2,1,0:T(8,128)(2,1)S(1)}, bf16[32,16,128]{2,1,0:T(8,128)(2,1)S(1)}, u32[]{:S(2)}, u32[]{:S(2)}) collective-permute-start(bf16[32,16,128]{2,1,0:T(8,128)(2,1)S(1)} %collective-permute-done.1.b_ref), channel_id=1, source_target_pairs={{0,1},{1,0},{2,3},{3,2},{4,5},{5,4},{6,7},{7,6},{8,9},{9,8},{10,11... | collective-permute-start | bytes 393224 | tf_op jit(solution)/shard_map/ppermute | solution.py:331
  40.3 10.6 %copy-start = (bf16[1,128,2048]{2,1,0:T(8,128)(2,1)S(1)}, bf16[1,128,2048]{2,1,0:T(8,128)(2,1)}, u32[]{:S(2)}) copy-start(bf16[1,128,2048]{2,1,0:T(8,128)(2,1)} %q_ref.1) | copy-start | bytes 1572868
  40.3 10.6 %copy-start.1 = (bf16[1,128,2048]{2,1,0:T(8,128)(2,1)S(1)}, bf16[1,128,2048]{2,1,0:T(8,128)(2,1)}, u32[]{:S(2)}) copy-start(bf16[1,128,2048]{2,1,0:T(8,128)(2,1)} %k_ref.1) | copy-start | bytes 1572868
  40.3 10.6 %copy-start.2 = (bf16[1,128,2048]{2,1,0:T(8,128)(2,1)S(1)}, bf16[1,128,2048]{2,1,0:T(8,128)(2,1)}, u32[]{:S(2)}) copy-start(bf16[1,128,2048]{2,1,0:T(8,128)(2,1)} %v_ref.1) | copy-start | bytes 1572868
  41.8 7.6 %copy-start.5 = (s32[1,16]{1,0:T(1,128)S(1)}, s32[1,16]{1,0:T(1,128)}, u32[]{:S(2)}) copy-start(s32[1,16]{1,0:T(1,128)} %off_ref.1) | copy-start | bytes 196
  41.8 14.9 %all-to-all-start.1 = ((bf16[32,24,128]{2,1,0:T(8,128)(2,1)}), bf16[32,24,128]{2,1,0:T(8,128)(2,1)S(1)}, u32[]{:S(2)}, u32[]{:S(2)}) async-start(bf16[32,24,128]{2,1,0:T(8,128)(2,1)} %far_grads.1), calls=%async_computation.1 | async-start | bytes 393216 | tf_op jit(solution)/shard_map/all_to_all | solution.py:335
  49.4 1.4 %copy-start.3 = (bf16[1,16,128]{2,1,0:T(8,128)(2,1)S(1)}, bf16[1,16,128]{2,1,0:T(8,128)(2,1)}, u32[]{:S(2)}) copy-start(bf16[1,16,128]{2,1,0:T(8,128)(2,1)} %l_ref.1) | copy-start | bytes 12292
  49.4 1.4 %copy-start.4 = (bf16[1,16,128]{2,1,0:T(8,128)(2,1)S(1)}, bf16[1,16,128]{2,1,0:T(8,128)(2,1)}, u32[]{:S(2)}) copy-start(bf16[1,16,128]{2,1,0:T(8,128)(2,1)} %d_ref.1) | copy-start | bytes 12292
  50.0 0.8 %copy-start.6 = (bf16[1,128,2048]{2,1,0:T(8,128)(2,1)}, bf16[1,128,2048]{2,1,0:T(8,128)(2,1)S(1)}, u32[]{:S(2)}) copy-start(bf16[1,128,2048]{2,1,0:T(8,128)(2,1)S(1)} %collective-permute-done.7.g_ref) | copy-start | bytes 1572868
  50.8 1.0 %copy-start.7 = (bf16[1,128,2048]{2,1,0:T(8,128)(2,1)S(1)}, bf16[1,128,2048]{2,1,0:T(8,128)(2,1)}, u32[]{:S(2)}) copy-start(bf16[1,128,2048]{2,1,0:T(8,128)(2,1)} %copy-done.6) | copy-start | bytes 1572868

commit v11 on v8

--- a/solution.py
+++ b/solution.py
@@ -150,7 +150,7 @@
     )(offsets, query, key, lse)
 
 
-def local_kernel(p_ref, q_ref, k_ref, v_ref, g0_ref, g1_ref, d_ref, dq_ref, dk_ref, dv_ref, st_ref):
+def local_kernel(p_ref, q_ref, k_ref, v_ref, g_ref, d_ref, dq_ref, dk_ref, dv_ref, st_ref):
     step = pl.program_id(0)
 
     @pl.when(step == 0)
@@ -160,8 +160,7 @@
     dlts = st_ref[pl.ds(pl.multiple_of(step * 4, 4), 4), :]
     for i in range(4):
         cols = slice(i * HD, (i + 1) * HD)
-        q, k, v = q_ref[0, :, cols], k_ref[0, :, cols], v_ref[0, :, cols]
-        g = jnp.concatenate([g0_ref[0, :, cols], g1_ref[0, :, cols]], axis=0)
+        q, k, v, g = q_ref[0, :, cols], k_ref[0, :, cols], v_ref[0, :, cols], g_ref[0, :, cols]
         p = p_ref[i]
         ds = (p * (dot_t(v, g) - dlts[i:i + 1])).astype(BF)
         dv_ref[:, cols] = dot(p.astype(BF), g).astype(BF)
@@ -169,23 +168,22 @@
         dq_ref[:, cols] = (dot_l(ds, k) * SCALE).astype(BF)
 
 
-def local_grads(probs, query, key, value, grad0, grad1, delta):
+def local_grads(probs, query, key, value, grad, delta):
     wide = pl.BlockSpec((1, TOK, 4 * HD), lambda i: (0, 0, i))
-    half = pl.BlockSpec((1, TOK // 2, 4 * HD), lambda i: (0, 0, i))
     out = pl.BlockSpec((TOK, 4 * HD), lambda i: (0, i))
     stat = pl.BlockSpec((1, HEADS, TOK), lambda i: (0, 0, 0))
     shape = jax.ShapeDtypeStruct((TOK, HEADS * HD), BF)
     return pl.pallas_call(
         local_kernel,
         grid=(4,),
-        in_specs=[pl.BlockSpec((4, TOK, TOK), lambda i: (i, 0, 0)), wide, wide, wide, half, half, stat],
+        in_specs=[pl.BlockSpec((4, TOK, TOK), lambda i: (i, 0, 0)), wide, wide, wide, wide, stat],
         out_specs=[out, out, out],
         out_shape=[shape, shape, shape],
         scratch_shapes=[pltpu.VMEM((HEADS, TOK), F32)],
         compiler_params=small(),
         cost_estimate=pl.CostEstimate(flops=16 * 4 * 2 * 128 ** 3 * 4, bytes_accessed=4718592, transcendentals=0),
         name="local_grads",
-    )(probs, query, key, value, grad0, grad1, delta)
+    )(probs, query, key, value, grad, delta)
 
 
 def query_side(q, g, k, v, lse, dlt):
@@ -358,8 +356,7 @@
     pos = (turn * 4 + jnp.where(x < 2, x, NX - 1 - x) * 2 + seat % NC).reshape(1)
     picked = pick_all(pos, offsets, log_sums, deltas, queries, key_rows, value_rows, grad_out)
     mine = swap(picked, IN_ORDER)
-    grad0 = move(grad_out[:, :TOK // 2], lambda s, x, c: (s - 1, x, c))
-    grad1 = move(grad_out[:, TOK // 2:], lambda s, x, c: (s - 1, x, c))
+    grad = move(grad_out, lambda s, x, c: (s - 1, x, c))
     probs, offs = local_scores(offsets, queries, key_rows, log_sums)
     a, b = mine[:, :MAIN], mine[:, MAIN:]
     far_a = move(a, lambda s, x, c: (s, 3 - x, c))
@@ -369,7 +366,7 @@
     other_b = move(own_b, lambda s, x, c: (s, x, 1 - c))
     other_far_a = move(far_a, lambda s, x, c: (s, x, 1 - c))
     other_far_b = move(far_b, lambda s, x, c: (s, x, 1 - c))
-    local = local_grads(probs, queries, key_rows, value_rows, grad0, grad1, deltas)
+    local = local_grads(probs, queries, key_rows, value_rows, grad, deltas)
     part = near_grads(core, a, own_b, other_a, other_b)
     back = swap(far_grads(core, far_a, far_b, other_far_a, other_far_b, *part), OUT_ORDER)
     return tuple(combine(back, (*local, offs)))

time: 66.7 us -> 57.3 us (0.86)
  waiting for transfers between devices: 14.4 us -> 6.65 us
  starting transfers between devices: 17.3 us -> 15.5 us
    ppermute x9 -> x8, waiting for transfers between devices: 14.4 us -> 4.81 us  [move(): return lax.ppermute(value, ('section', 'seq'), pairs)]
    all_to_all x1, waiting for transfers between devices: 0.01 us -> 1.84 us  [swap(): lax.all_to_all(value, 'seq', 0, 0, axis_index_groups=groups_of(order), ti...]
    ppermute x9 -> x8, starting transfers between devices: 10.4 us -> 8.59 us  [move(): return lax.ppermute(value, ('section', 'seq'), pairs)]
  transfers between devices with their start and end apart: 10 -> 9, of which waited for: 5 -> 4; matrix products, arithmetic and copies ran while one was open for 0% -> 0% of each run, Pallas kernels for 9% -> 14%
where the time goes in v11:
time: 57.3 us; the launch traced here: 56.9 us
  blocking collectives  21.7 us (38%)
  starting transfers between devices  15.5 us (27%)
  Pallas kernels  12.2 us (21%)
  waiting for transfers between devices  6.65 us (12%)
  between operations  0.85 us (1%)
    all_to_all x1, blocking collectives, swap(): lax.all_to_all(value, 'seq', 0, 0, axis_index_groups=groups_of(order), ti...  21.7 us
    ppermute x8, starting transfers between devices, move(): return lax.ppermute(value, ('section', 'seq'), pairs)  8.59 us
    all_to_all x1, starting transfers between devices, swap(): lax.all_to_all(value, 'seq', 0, 0, axis_index_groups=groups_of(order), ti...  6.88 us
    ppermute x8, waiting for transfers between devices, move(): return lax.ppermute(value, ('section', 'seq'), pairs)  4.81 us
    pallas_call x1, Pallas kernels, local_grads(): pl.pallas_call(local_kernel, grid=(4,), in_specs=[pl.BlockSpec((4, TOK, T...  3.64 us
    pallas_call x1, Pallas kernels, pick_all(): pl.pallas_call(pick_kernel, in_specs=[SM] + [raw] * 7, out_specs=raw, out...  2.84 us
    all_to_all x1, waiting for transfers between devices, swap(): lax.all_to_all(value, 'seq', 0, 0, axis_index_groups=groups_of(order), ti...  1.84 us
    pallas_call x1, Pallas kernels, local_scores(): pl.pallas_call(score_kernel, grid=(4,), in_specs=[SM, wide, wide, stat],...  1.63 us
  transfers between devices with their start and end apart: 9, of which 4 were waited for; matrix products, arithmetic and copies ran while one was open for 0% of the time, Pallas kernels for 14%

profile of v11, /device:TPU:1, one launch (start us, length us, event | category | flops | bytes accessed | tf_op | source)
XLA Modules:
  0.0 56.9 jit_solution(13523520461924101929)
XLA Ops:
  0.7 2.8 %pick_all.1 = bf16[16,2,40,128]{3,2,1,0:T(8,128)(2,1)} custom-call(s32[1]{0:T(128)} %bitcast.1.pos_ref, s32[1,16]{1,0:T(1,128)} %off_ref.1, bf16[1,16,128]{2,1,0:T(8,128)(2,1)} %l_ref.1, bf16[1,16,128]{2,1,0:T(8,128)(2,1)} %d_ref.1, bf16[1,128,2048]{2,1,0:T(8,128)(2,1)} %q_ref.3, bf16[1,128,2048]{2,1,0:T(8,128)(2,1)} %k_ref.3, bf16[1,128,2048]{2,1,0:T(8,128)(2,1)} %v_ref.1, ...), custom_call_target="tpu_custom_call" | custom-call | tf_op jit(solution)/shard_map/pick_all/pallas_call | solution.py:104
  3.6 0.0 copy-start.6
  3.6 21.7 %all_to_all.10 = bf16[32,40,128]{2,1,0:T(8,128)(2,1)S(1)} all-to-all(bf16[32,40,128]{2,1,0:T(8,128)(2,1)} %bitcast.3), channel_id=1, replica_groups={{40,41,42,43,32,33,34,35,24,25,26,27,16,17,18,19,8,9,10,11,0,1,2,3,56,5..., dimensions={0} | all-to-all | bytes 655360 | tf_op jit(solution)/shard_map/all_to_all | solution.py:347
  25.3 2.3 %collective-permute-start = (bf16[32,24,128]{2,1,0:T(8,128)(2,1)S(1)}, bf16[32,24,128]{2,1,0:T(8,128)(2,1)S(1)}, u32[]{:S(2)}, u32[]{:S(2)}) collective-permute-start(bf16[32,24,128]{2,1,0:T(8,128)(2,1)S(1)} %slice.8.a_ref), channel_id=1, source_target_pairs={{0,6},{1,7},{2,4},{3,5},{4,2},{5,3},{6,0},{7,1},{8,14},{9,15},{10,... | collective-permute-start | bytes 589832 | tf_op jit(solution)/shard_map/ppermute | solution.py:343
  27.7 4.6 %collective-permute-start.4 = (bf16[32,16,128]{2,1,0:T(8,128)(2,1)S(1)}, bf16[32,16,128]{2,1,0:T(8,128)(2,1)S(1)}, u32[]{:S(2)}, u32[]{:S(2)}) collective-permute-start(bf16[32,16,128]{2,1,0:T(8,128)(2,1)S(1)} %slice.9), channel_id=1, source_target_pairs={{0,0},{1,193},{2,2},{3,195},{4,4},{5,197},{6,6},{7,199},{8,8},{9,2... | collective-permute-start | bytes 393224 | tf_op jit(solution)/shard_map/ppermute | solution.py:343
  32.3 0.7 %collective-permute-start.1 = (bf16[32,16,128]{2,1,0:T(8,128)(2,1)S(1)}, bf16[32,16,128]{2,1,0:T(8,128)(2,1)S(1)}, u32[]{:S(2)}, u32[]{:S(2)}) collective-permute-start(bf16[32,16,128]{2,1,0:T(8,128)(2,1)S(1)} %slice.9), channel_id=1, source_target_pairs={{0,6},{1,199},{2,4},{3,197},{4,2},{5,195},{6,0},{7,193},{8,14},{9,... | collective-permute-start | bytes 393224 | tf_op jit(solution)/shard_map/ppermute | solution.py:343
  33.0 0.2 collective-permute-start.7
  33.2 0.0 collective-permute-start.5
  33.2 0.0 collective-permute-done.a_ref
  33.2 0.8 %collective-permute-start.2 = (bf16[32,24,128]{2,1,0:T(8,128)(2,1)S(1)}, bf16[32,24,128]{2,1,0:T(8,128)(2,1)S(1)}, u32[]{:S(2)}, u32[]{:S(2)}) collective-permute-start(bf16[32,24,128]{2,1,0:T(8,128)(2,1)S(1)} %collective-permute-done.a_ref), channel_id=1, source_target_pairs={{0,1},{1,0},{2,3},{3,2},{4,5},{5,4},{6,7},{7,6},{8,9},{9,8},{10,11... | collective-permute-start | bytes 589832 | tf_op jit(solution)/shard_map/ppermute | solution.py:343
  33.9 1.3 %collective-permute-done.4.b_ref = bf16[32,16,128]{2,1,0:T(8,128)(2,1)S(1)} collective-permute-done((bf16[32,16,128]{2,1,0:T(8,128)(2,1)S(1)}, bf16[32,16,128]{2,1,0:T(8,128)(2,1)S(1)}, u32[]{:S(2)}, u32[]{:S(2)}) %collective-permute-start.4) | collective-permute-done | bytes 131104 | tf_op jit(solution)/shard_map/ppermute | solution.py:343
  35.3 0.0 collective-permute-start.6
  35.3 3.1 %collective-permute-done.1.b_ref = bf16[32,16,128]{2,1,0:T(8,128)(2,1)S(1)} collective-permute-done((bf16[32,16,128]{2,1,0:T(8,128)(2,1)S(1)}, bf16[32,16,128]{2,1,0:T(8,128)(2,1)S(1)}, u32[]{:S(2)}, u32[]{:S(2)}) %collective-permute-start.1) | collective-permute-done | bytes 131104 | tf_op jit(solution)/shard_map/ppermute | solution.py:343
  38.4 0.0 collective-permute-done.5.oa_ref
  38.4 1.0 %near_grads.1 = (bf16[4,256,128]{2,1,0:T(8,128)(2,1)S(1)}, f32[256,128]{1,0:T(8,128)S(1)}, f32[256,128]{1,0:T(8,128)S(1)}, f32[256,128]{1,0:T(8,128)S(1)}, f32[256,128]{1,0:T(8,128)S(1)}) custom-call(s32[1]{0:T(128)} %bitcast.core_ref, bf16[32,24,128]{2,1,0:T(8,128)(2,1)S(1)} %slice.8.a_ref, bf16[32,16,128]{2,1,0:T(8,128)(2,1)S(1)} %collective-permute-done.4.b_ref, ...), custom_call_target="tpu_custom_call" | custom-call | flops 469762048 | bytes 1572864 | tf_op jit(solution)/shard_map/near_grads/pallas_call | solution.py:244
  39.5 0.3 collective-permute-done.3.ob_ref
  39.8 1.5 %far_grads.1 = bf16[32,24,128]{2,1,0:T(8,128)(2,1)} custom-call(s32[1]{0:T(128)} %bitcast.core_ref, bf16[32,24,128]{2,1,0:T(8,128)(2,1)S(1)} %collective-permute-done.a_ref, bf16[32,16,128]{2,1,0:T(8,128)(2,1)S(1)} %collective-permute-done.1.b_ref, bf16[32,24,128]{2,1,0:T(8,128)(2,1)S(1)} %collective-permute-done.2.oa_ref, ...), custom_call_target="tpu_custom_call" | custom-call | tf_op jit(solution)/shard_map/far_grads/pallas_call | solution.py:271
  41.3 6.9 %all-to-all-start.1 = ((bf16[32,24,128]{2,1,0:T(8,128)(2,1)}), bf16[32,24,128]{2,1,0:T(8,128)(2,1)S(1)}, u32[]{:S(2)}, u32[]{:S(2)}) async-start(bf16[32,24,128]{2,1,0:T(8,128)(2,1)} %far_grads.1), calls=%async_computation.1 | async-start | bytes 393216 | tf_op jit(solution)/shard_map/all_to_all | solution.py:347
  48.2 0.0 copy-start.2
  48.2 0.0 copy-start.4
  48.2 1.6 %local_scores.1 = (f32[16,128,128]{2,1,0:T(8,128)S(1)}, s32[16,128]{1,0:T(8,128)S(1)}) custom-call(s32[1,16]{1,0:T(1,128)S(1)} %copy-done.5, bf16[1,128,2048]{2,1,0:T(8,128)(2,1)S(1)} %copy-done, bf16[1,128,2048]{2,1,0:T(8,128)(2,1)S(1)} %copy-done.1, bf16[1,16,128]{2,1,0:T(8,128)(2,1)S(1)} %copy-done.3), custom_call_target="tpu_custom_call" | custom-call | flops 268435456 | bytes 2097152 | tf_op jit(solution)/shard_map/local_scores/pallas_call | solution.py:140
  49.9 3.6 %local_grads.1 = (bf16[128,2048]{1,0:T(8,128)(2,1)S(1)}, bf16[128,2048]{1,0:T(8,128)(2,1)S(1)}, bf16[128,2048]{1,0:T(8,128)(2,1)S(1)}) custom-call(f32[16,128,128]{2,1,0:T(8,128)S(1)} %get-tuple-element.18.p_ref, bf16[1,128,2048]{2,1,0:T(8,128)(2,1)S(1)} %copy-done, bf16[1,128,2048]{2,1,0:T(8,128)(2,1)S(1)} %copy-done.1, ...), custom_call_target="tpu_custom_call" | custom-call | flops 1073741824 | bytes 4718592 | tf_op jit(solution)/shard_map/local_grads/pallas_call | solution.py:176
  53.6 1.8 %all-to-all-done.1.w_ref = bf16[32,24,128]{2,1,0:T(8,128)(2,1)S(1)} async-done(((bf16[32,24,128]{2,1,0:T(8,128)(2,1)}), bf16[32,24,128]{2,1,0:T(8,128)(2,1)S(1)}, u32[]{:S(2)}, u32[]{:S(2)}) %all-to-all-start.1) | async-done | bytes 196640 | tf_op jit(solution)/shard_map/all_to_all | solution.py:347
  55.4 1.5 %combine.1 = (bf16[1,128,2048]{2,1,0:T(8,128)(2,1)}, bf16[1,128,2048]{2,1,0:T(8,128)(2,1)}, bf16[1,128,2048]{2,1,0:T(8,128)(2,1)}) custom-call(bf16[32,24,128]{2,1,0:T(8,128)(2,1)S(1)} %all-to-all-done.1.w_ref, bf16[128,2048]{1,0:T(8,128)(2,1)S(1)} %get-tuple-element.19.dq_ref, bf16[128,2048]{1,0:T(8,128)(2,1)S(1)} %get-tuple-element.20.dk_ref, ...), custom_call_target="tpu_custom_call" | custom-call | tf_op jit(solution)/shard_map/combine/pallas_call | solution.py:305
  (17 shorter events, 0.1 us)
Async XLA Ops:
  3.6 29.4 %copy-start.6 = (bf16[1,128,2048]{2,1,0:T(8,128)(2,1)S(1)}, bf16[1,128,2048]{2,1,0:T(8,128)(2,1)}, u32[]{:S(2)}) copy-start(bf16[1,128,2048]{2,1,0:T(8,128)(2,1)} %g_hbm.1) | copy-start | bytes 1572868
  25.3 7.9 %collective-permute-start = (bf16[32,24,128]{2,1,0:T(8,128)(2,1)S(1)}, bf16[32,24,128]{2,1,0:T(8,128)(2,1)S(1)}, u32[]{:S(2)}, u32[]{:S(2)}) collective-permute-start(bf16[32,24,128]{2,1,0:T(8,128)(2,1)S(1)} %slice.8.a_ref), channel_id=1, source_target_pairs={{0,6},{1,7},{2,4},{3,5},{4,2},{5,3},{6,0},{7,1},{8,14},{9,15},{10,... | collective-permute-start | bytes 589832 | tf_op jit(solution)/shard_map/ppermute | solution.py:343
  27.7 7.6 %collective-permute-start.4 = (bf16[32,16,128]{2,1,0:T(8,128)(2,1)S(1)}, bf16[32,16,128]{2,1,0:T(8,128)(2,1)S(1)}, u32[]{:S(2)}, u32[]{:S(2)}) collective-permute-start(bf16[32,16,128]{2,1,0:T(8,128)(2,1)S(1)} %slice.9), channel_id=1, source_target_pairs={{0,0},{1,193},{2,2},{3,195},{4,4},{5,197},{6,6},{7,199},{8,8},{9,2... | collective-permute-start | bytes 393224 | tf_op jit(solution)/shard_map/ppermute | solution.py:343
  32.3 6.1 %collective-permute-start.1 = (bf16[32,16,128]{2,1,0:T(8,128)(2,1)S(1)}, bf16[32,16,128]{2,1,0:T(8,128)(2,1)S(1)}, u32[]{:S(2)}, u32[]{:S(2)}) collective-permute-start(bf16[32,16,128]{2,1,0:T(8,128)(2,1)S(1)} %slice.9), channel_id=1, source_target_pairs={{0,6},{1,199},{2,4},{3,197},{4,2},{5,195},{6,0},{7,193},{8,14},{9,... | collective-permute-start | bytes 393224 | tf_op jit(solution)/shard_map/ppermute | solution.py:343
  33.0 16.9 %collective-permute-start.7 = (bf16[1,128,2048]{2,1,0:T(8,128)(2,1)S(1)}, bf16[1,128,2048]{2,1,0:T(8,128)(2,1)S(1)}, u32[]{:S(2)}, u32[]{:S(2)}) collective-permute-start(bf16[1,128,2048]{2,1,0:T(8,128)(2,1)S(1)} %copy-done.6), channel_id=1, source_target_pairs={{0,192},{1,193},{2,194},{3,195},{4,196},{5,197},{6,198},{7,199},{8... | collective-permute-start | bytes 1572872 | tf_op jit(solution)/shard_map/ppermute | solution.py:343
  33.2 5.3 %collective-permute-start.5 = (bf16[32,24,128]{2,1,0:T(8,128)(2,1)S(1)}, bf16[32,24,128]{2,1,0:T(8,128)(2,1)S(1)}, u32[]{:S(2)}, u32[]{:S(2)}) collective-permute-start(bf16[32,24,128]{2,1,0:T(8,128)(2,1)S(1)} %slice.8.a_ref), channel_id=1, source_target_pairs={{0,1},{1,0},{2,3},{3,2},{4,5},{5,4},{6,7},{7,6},{8,9},{9,8},{10,11... | collective-permute-start | bytes 589832 | tf_op jit(solution)/shard_map/ppermute | solution.py:343
  33.2 6.6 %collective-permute-start.2 = (bf16[32,24,128]{2,1,0:T(8,128)(2,1)S(1)}, bf16[32,24,128]{2,1,0:T(8,128)(2,1)S(1)}, u32[]{:S(2)}, u32[]{:S(2)}) collective-permute-start(bf16[32,24,128]{2,1,0:T(8,128)(2,1)S(1)} %collective-permute-done.a_ref), channel_id=1, source_target_pairs={{0,1},{1,0},{2,3},{3,2},{4,5},{5,4},{6,7},{7,6},{8,9},{9,8},{10,11... | collective-permute-start | bytes 589832 | tf_op jit(solution)/shard_map/ppermute | solution.py:343
  35.3 3.2 %collective-permute-start.6 = (bf16[32,16,128]{2,1,0:T(8,128)(2,1)S(1)}, bf16[32,16,128]{2,1,0:T(8,128)(2,1)S(1)}, u32[]{:S(2)}, u32[]{:S(2)}) collective-permute-start(bf16[32,16,128]{2,1,0:T(8,128)(2,1)S(1)} %collective-permute-done.4.b_ref), channel_id=1, source_target_pairs={{0,1},{1,0},{2,3},{3,2},{4,5},{5,4},{6,7},{7,6},{8,9},{9,8},{10,11... | collective-permute-start | bytes 393224 | tf_op jit(solution)/shard_map/ppermute | solution.py:343
  38.4 1.3 %collective-permute-start.3 = (bf16[32,16,128]{2,1,0:T(8,128)(2,1)S(1)}, bf16[32,16,128]{2,1,0:T(8,128)(2,1)S(1)}, u32[]{:S(2)}, u32[]{:S(2)}) collective-permute-start(bf16[32,16,128]{2,1,0:T(8,128)(2,1)S(1)} %collective-permute-done.1.b_ref), channel_id=1, source_target_pairs={{0,1},{1,0},{2,3},{3,2},{4,5},{5,4},{6,7},{7,6},{8,9},{9,8},{10,11... | collective-permute-start | bytes 393224 | tf_op jit(solution)/shard_map/ppermute | solution.py:343
  39.8 8.4 %copy-start = (bf16[1,128,2048]{2,1,0:T(8,128)(2,1)S(1)}, bf16[1,128,2048]{2,1,0:T(8,128)(2,1)}, u32[]{:S(2)}) copy-start(bf16[1,128,2048]{2,1,0:T(8,128)(2,1)} %q_ref.3) | copy-start | bytes 1572868
  39.8 8.4 %copy-start.1 = (bf16[1,128,2048]{2,1,0:T(8,128)(2,1)S(1)}, bf16[1,128,2048]{2,1,0:T(8,128)(2,1)}, u32[]{:S(2)}) copy-start(bf16[1,128,2048]{2,1,0:T(8,128)(2,1)} %k_ref.3) | copy-start | bytes 1572868
  41.3 6.9 %copy-start.3 = (bf16[1,16,128]{2,1,0:T(8,128)(2,1)S(1)}, bf16[1,16,128]{2,1,0:T(8,128)(2,1)}, u32[]{:S(2)}) copy-start(bf16[1,16,128]{2,1,0:T(8,128)(2,1)} %l_ref.1) | copy-start | bytes 12292
  41.3 6.9 %copy-start.5 = (s32[1,16]{1,0:T(1,128)S(1)}, s32[1,16]{1,0:T(1,128)}, u32[]{:S(2)}) copy-start(s32[1,16]{1,0:T(1,128)} %off_ref.1) | copy-start | bytes 196
  41.3 14.1 %all-to-all-start.1 = ((bf16[32,24,128]{2,1,0:T(8,128)(2,1)}), bf16[32,24,128]{2,1,0:T(8,128)(2,1)S(1)}, u32[]{:S(2)}, u32[]{:S(2)}) async-start(bf16[32,24,128]{2,1,0:T(8,128)(2,1)} %far_grads.1), calls=%async_computation.1 | async-start | bytes 393216 | tf_op jit(solution)/shard_map/all_to_all | solution.py:347
  48.2 1.7 %copy-start.2 = (bf16[1,128,2048]{2,1,0:T(8,128)(2,1)S(1)}, bf16[1,128,2048]{2,1,0:T(8,128)(2,1)}, u32[]{:S(2)}) copy-start(bf16[1,128,2048]{2,1,0:T(8,128)(2,1)} %v_ref.1) | copy-start | bytes 1572868
  48.2 1.7 %copy-start.4 = (bf16[1,16,128]{2,1,0:T(8,128)(2,1)S(1)}, bf16[1,16,128]{2,1,0:T(8,128)(2,1)}, u32[]{:S(2)}) copy-start(bf16[1,16,128]{2,1,0:T(8,128)(2,1)} %d_ref.1) | copy-start | bytes 12292
